TPU v7x, 128 devices: a whole 4x4x4 slice. The times are simulated.
128 devices in a mesh: seq: 16 (over y, z), head: 8 (over x, core).
Axes of the slice: x: 4, y: 4, z: 4, core: 2. Of those that a mesh axis runs over, the one named last changes fastest.
Arguments:
- queries: bfloat16 [4096, 128, 576], P('seq', 'head'), may hold values from -6 to 6
- lse: float32 [4096, 128], P('seq', 'head'), may hold values from 8 to 11
- latent: bfloat16 [1024, 128, 576], P('seq'), may hold values from -6 to 6
- index_keys: bfloat16 [1024, 128, 128], P('seq'), may hold values from -6 to 6
- index_queries: bfloat16 [4096, 64, 128], P('seq', 'head'), may hold values from -6 to 6
- index_weights: float32 [4096, 64], P('seq', 'head'), may hold values from 0.03 to 0.3
- block_lists: int32 [32, 16], P('seq'), may hold values from 0 to 1023, as said below
- block_place: int32 [1024], replicated, may hold values from 0 to 1023, as said below
Outputs:
- grad_index_queries: float32 [4096, 64, 128], P('seq', 'head')
- grad_index_weights: float32 [4096, 64], P('seq', 'head')
- grad_index_keys: float32 [1024, 128, 128], P('seq', 'head')
Inputs may be any that keep to these rules, and one draw needn't show every extreme that they name: block_place is a permutation of the 1024 pages; page p lies on index p // 64 of seq, and each aligned run of 16 logical blocks (blocks r * 16 to r * 16 + 15) has its pages on 16 different indices of seq. `block_lists`: row g lists 16 different logical blocks, each below 32 * (g + 1). The row is made of 16 runs of 1 entries; the entries of run k are blocks whose pages lie on index k of seq.
All inputs are finite; a program needn't handle non-finite values.
Results may differ from a plain program's by a relative error of at most 0.0029.
Values may be sent and summed in bfloat16 or wider, within the bound.
No kernel may reach another device: no remote copies, remote signals or barrier semaphores. Data moves between devices by JAX's collectives and lax.ppermute only.
A program may use at most 128 MiB of HBM per device.

v0:
```python
import jax
import jax.numpy as jnp
from jax import lax
from jax.sharding import PartitionSpec as P

BLOCK = 128
SEL = 16
QBLK = 128


softmax_scale = 192.0 ** (-0.5)
loss_scale = 2048.0


def loss_gradient(teacher_sum, score_sum):
    target = teacher_sum / jnp.sum(teacher_sum, axis=1, keepdims=True)
    probs = jax.nn.softmax(score_sum, axis=-1)
    return loss_scale * (probs - target)


def shards(
    queries, lse, latent, index_keys, index_queries, index_weights, block_lists, block_place
):
    seq_count = lax.axis_size("seq")
    page_count = latent.shape[0]
    qblocks = block_lists.shape[0]
    per_owner = SEL // seq_count
    key_span = SEL * BLOCK
    pages = jnp.take(block_place, block_lists, axis=0)
    wanted_slots = (pages % page_count).reshape(qblocks, seq_count, per_owner)
    wanted_slots = wanted_slots.transpose(1, 0, 2).reshape(seq_count, qblocks * per_owner)
    wanted = lax.all_to_all(wanted_slots, "seq", split_axis=0, concat_axis=0, tiled=True)
    fetched_latent = lax.all_to_all(
        jnp.take(latent, wanted, axis=0), "seq", split_axis=0, concat_axis=0, tiled=True
    )
    fetched_keys = lax.all_to_all(
        jnp.take(index_keys, wanted, axis=0), "seq", split_axis=0, concat_axis=0, tiled=True
    )

    def forward_block(block_index):
        key_rows = lax.dynamic_slice_in_dim(
            fetched_latent, block_index * per_owner, per_owner, 1
        ).reshape(key_span, -1)
        index_rows = lax.dynamic_slice_in_dim(
            fetched_keys, block_index * per_owner, per_owner, 1
        ).reshape(key_span, -1)
        first = block_index * QBLK
        query_rows = lax.dynamic_slice_in_dim(queries, first, QBLK, 0)
        lse_rows = lax.dynamic_slice_in_dim(lse, first, QBLK, 0)
        probe_rows = lax.dynamic_slice_in_dim(index_queries, first, QBLK, 0)
        head_weights = lax.dynamic_slice_in_dim(index_weights, first, QBLK, 0)
        scores = (
            jnp.einsum("qhd,kd->qhk", query_rows, key_rows, preferred_element_type=jnp.float32)
            * softmax_scale
        )
        teacher = jnp.sum(jnp.exp(scores - lse_rows[:, :, None]), axis=1)
        raw_scores = jnp.einsum(
            "qhd,kd->qhk", probe_rows, index_rows, preferred_element_type=jnp.float32
        )
        indexed = jnp.sum(head_weights[:, :, None] * jnp.maximum(raw_scores, 0.0), axis=1)
        return (teacher, indexed, raw_scores)

    teacher, indexed, raw_all = lax.map(forward_block, jnp.arange(qblocks, dtype=jnp.int32))
    teacher_flat = teacher.reshape(qblocks * QBLK, key_span)
    indexed_flat = indexed.reshape(qblocks * QBLK, key_span)
    teacher_sum, score_sum = lax.psum((teacher_flat, indexed_flat), "head")
    grad_score = loss_gradient(teacher_sum, score_sum)
    grad_score = grad_score.reshape(qblocks, QBLK, key_span)

    def backward_block(inputs):
        block_index, grad_rows, raw_scores = inputs
        index_rows = lax.dynamic_slice_in_dim(
            fetched_keys, block_index * per_owner, per_owner, 1
        ).reshape(key_span, -1)
        first = block_index * QBLK
        probe_rows = lax.dynamic_slice_in_dim(index_queries, first, QBLK, 0)
        head_weights = lax.dynamic_slice_in_dim(index_weights, first, QBLK, 0)
        active = jnp.maximum(raw_scores, 0.0)
        grad_weight = jnp.sum(grad_rows[:, None, :] * active, axis=2)
        grad_raw = (
            grad_rows[:, None, :] * head_weights[:, :, None] * (raw_scores > 0).astype(jnp.float32)
        ).astype(jnp.bfloat16)
        grad_query = jnp.einsum(
            "qhk,kd->qhd", grad_raw, index_rows, preferred_element_type=jnp.float32
        )
        key_grad = jnp.einsum(
            "qhk,qhd->kd", grad_raw, probe_rows, preferred_element_type=jnp.float32
        )
        return (grad_query, grad_weight, key_grad.reshape(seq_count, per_owner, BLOCK, -1))

    grad_queries, grad_weights, key_grads = lax.map(
        backward_block, (jnp.arange(qblocks, dtype=jnp.int32), grad_score, raw_all)
    )
    key_grads = key_grads.transpose(1, 0, 2, 3, 4).reshape(
        seq_count, qblocks * per_owner, BLOCK, -1
    )
    onehot = (
        wanted.reshape(-1)[:, None] == jnp.arange(page_count, dtype=jnp.int32)[None, :]
    ).astype(jnp.float32)
    returned_grads = lax.all_to_all(key_grads, "seq", split_axis=0, concat_axis=0, tiled=True)
    flattened = returned_grads.reshape(onehot.shape[0], -1)
    summed_rows = jnp.dot(
        onehot.T, flattened, precision=lax.Precision.HIGHEST, preferred_element_type=jnp.float32
    )
    grad_keys = lax.psum_scatter(
        summed_rows.reshape(page_count, returned_grads.shape[2], returned_grads.shape[3]),
        "head",
        scatter_dimension=1,
        tiled=True,
    )
    grad_queries = grad_queries.reshape(
        qblocks * QBLK, grad_queries.shape[2], grad_queries.shape[3]
    )
    grad_weights = grad_weights.reshape(qblocks * QBLK, grad_weights.shape[2])
    return (grad_queries, grad_weights, grad_keys)


def solution(mesh):
    return jax.shard_map(
        shards,
        mesh=mesh,
        in_specs=(
            P("seq", "head", None),
            P("seq", "head"),
            P("seq", None, None),
            P("seq", None, None),
            P("seq", "head", None),
            P("seq", "head"),
            P("seq", None),
            P(),
        ),
        out_specs=(P("seq", "head", None), P("seq", "head"), P("seq", "head", None)),
        check_vma=False,
    )
```

profile of v0, /device:TPU:1, one launch (start us, length us, event | category | flops | bytes accessed | tf_op | source)
XLA Modules:
  0.0 365.2 jit_solution(15279410345109099436)
XLA Ops:
  8.1 1.4 gather_fusion
  10.4 14.8 %all_to_all.30 = s32[16,1,2]{2,1,0:T(1,128)S(1)} all-to-all(s32[16,1,2]{2,1,0:T(1,128)S(1)} %copy.33), channel_id=1, replica_groups=mesh['seq'=16,'head'=8] {'seq'}, dimensions={0} | all-to-all | bytes 256 | tf_op jit(solution)/shard_map/all_to_all | solution.py:32
  26.6 1.1 broadcast_select_fusion.1
  27.8 3.7 %all-to-all-start.2 = ((bf16[16,2,128,128]{3,2,1,0:T(8,128)(2,1)}), bf16[16,2,128,128]{3,2,1,0:T(8,128)(2,1)S(1)}, u32[]{:S(2)}, u32[]{:S(2)}) async-start(bf16[16,2,128,128]{3,2,1,0:T(8,128)(2,1)} %broadcast_select_fusion.1), calls=%async_computation.2 | async-start | bytes 2097152 | tf_op jit(solution)/shard_map/all_to_all | solution.py:36
  31.4 7.0 %gather_fusion.1 = bf16[32,128,576]{1,2,0:T(8,128)(2,1)} fusion(bf16[64,128,576]{1,2,0:T(8,128)(2,1)} %param.14, s32[1024]{0:T(1024)S(1)} %pad_clamp_fusion), kind=kCustom, calls=%fused_computation.1 | custom fusion | bytes 9437312 | tf_op jit(solution)/shard_map/jit(_take)/gather | solution.py:34
  38.4 5.0 %broadcast_select_fusion = bf16[16,2,128,576]{2,3,1,0:T(8,128)(2,1)} fusion(bf16[16,2,128,576]{2,3,1,0:T(8,128)(2,1)} %bitcast.138, pred[16,2]{1,0:T(8,128)(4,1)S(1)} %copy.35), kind=kLoop, calls=%fused_computation.43 | loop fusion | flops 2359296 | bytes 9437216 | tf_op jit(solution)/shard_map/jit(_take)/select_n | solution.py:34
  43.4 2.9 all-to-all-done.2
  46.3 4.6 %all-to-all-start.1 = ((bf16[16,2,128,576]{2,3,1,0:T(8,128)(2,1)}), bf16[16,2,128,576]{2,3,1,0:T(8,128)(2,1)}, u32[]{:S(2)}, u32[]{:S(2)}) async-start(bf16[16,2,128,576]{2,3,1,0:T(8,128)(2,1)} %broadcast_select_fusion), calls=%async_computation.1 | async-start | bytes 9437184 | tf_op jit(solution)/shard_map/all_to_all | solution.py:33
  52.3 54.8 %all-to-all-done.1 = bf16[16,2,128,576]{2,3,1,0:T(8,128)(2,1)} async-done(((bf16[16,2,128,576]{2,3,1,0:T(8,128)(2,1)}), bf16[16,2,128,576]{2,3,1,0:T(8,128)(2,1)}, u32[]{:S(2)}, u32[]{:S(2)}) %all-to-all-start.1) | async-done | bytes 4718624 | tf_op jit(solution)/shard_map/all_to_all | solution.py:33
  107.1 58.2 %while.28 = (s32[]{:T(128)}, f32[2,128,2048]{2,1,0:T(8,128)}, f32[2,128,2048]{2,1,0:T(8,128)}, f32[2,128,8,2048]{3,1,2,0:T(8,128)}, s32[2]{0:T(128)S(1)}, /*inde...) while((s32[]{:T(128)}, f32[2,128,2048]{2,1,0:T(8,128)}, ...), condition=%wide.region_3.4_spmd, body=%wide.region_0.3_spmd.sunk | while | flops 5387059200 | bytes 89953200 | solution.py:63
  110.4 1.1 constant_dynamic-slice_fusion.13
  111.5 1.3 multiply_reduce_fusion.2
  112.8 3.8 %bitcast_dynamic-update-slice_fusion.8 = f32[2,128,8,2048]{3,1,2,0:T(8,128)} fusion(f32[2,128,8,2048]{3,1,2,0:T(8,128)} %get-tuple-element.406, s32[]{:T(128)} %get-tuple-element.403, f32[128,8,2048]{2,0,1:T(8,128)S(1)} %get-tuple-element.373), kind=kLoop, calls=%fused_computation.4.clone.1 | loop fusion | bytes 16777728 | tf_op jit(solution)/shard_map/while/body/jit(dynamic_update_index_in_dim)/dynamic_update_slice | solution.py:63
  116.6 1.8 constant_dynamic-slice_fusion.15
  118.4 1.5 copy.78
  120.0 2.5 reshape.172
  122.5 10.7 %exponential_reduce_fusion.2 = f32[128,2048]{1,0:T(8,128)S(1)} fusion(f32[128,16]{0,1:T(8,128)S(1)} %constant_dynamic-slice_fusion.14, bf16[2048,576,1]{0,1,2:T(8,128)(2,1)} %reshape.172, bf16[256,16,576]{0,2,1:T(8,128)(2,1)} %get-tuple-element.424, s32[]{:T(128)S(6)} %select_n.94), kind=kOutput, calls=%fused_computation.3.clone.1 | convolution fusion | flops 4844158976 | bytes 5775364 | tf_op jit(solution)/shard_map/while/body/eval_jaxpr/qhd,kd->qhk/dot_general | solution.py:53
  133.4 1.3 copy-done.10
  134.8 1.4 copy-done.12
  139.5 1.1 constant_dynamic-slice_fusion.13
  140.6 1.3 multiply_reduce_fusion.2
  141.9 3.8 %bitcast_dynamic-update-slice_fusion.8 = f32[2,128,8,2048]{3,1,2,0:T(8,128)} fusion(f32[2,128,8,2048]{3,1,2,0:T(8,128)} %get-tuple-element.406, s32[]{:T(128)} %get-tuple-element.403, f32[128,8,2048]{2,0,1:T(8,128)S(1)} %get-tuple-element.373), kind=kLoop, calls=%fused_computation.4.clone.1 | loop fusion | bytes 16777728 | tf_op jit(solution)/shard_map/while/body/jit(dynamic_update_index_in_dim)/dynamic_update_slice | solution.py:63
  145.7 1.8 constant_dynamic-slice_fusion.15
  147.5 1.5 copy.78
  149.0 2.5 reshape.172
  151.5 10.7 %exponential_reduce_fusion.2 = f32[128,2048]{1,0:T(8,128)S(1)} fusion(f32[128,16]{0,1:T(8,128)S(1)} %constant_dynamic-slice_fusion.14, bf16[2048,576,1]{0,1,2:T(8,128)(2,1)} %reshape.172, bf16[256,16,576]{0,2,1:T(8,128)(2,1)} %get-tuple-element.424, s32[]{:T(128)S(6)} %select_n.94), kind=kOutput, calls=%fused_computation.3.clone.1 | convolution fusion | flops 4844158976 | bytes 5775364 | tf_op jit(solution)/shard_map/while/body/eval_jaxpr/qhd,kd->qhk/dot_general | solution.py:53
  162.5 1.3 copy-done.10
  163.8 1.4 copy-done.12
  166.1 74.0 %all-reduce.3.cloned.1.call-done = (f32[256,2048]{1,0:T(8,128)}, f32[256,2048]{1,0:T(8,128)}) async-done(((f32[256,2048]{1,0:T(8,128)}, f32[256,2048]{1,0:T(8,128)}), (f32[256,2048]{1,0:T(8,128)}, f32[256,2048]{1,0:T(8,128)})) %all-reduce.3.cloned.1.call-update) | async-done | bytes 4194320 | tf_op jit(solution)/shard_map/psum | solution.py:66
  240.1 1.9 reduce_max.9
  242.8 1.8 reduce_sum.46
  244.5 3.5 subtract_multiply_fusion
  248.1 31.6 %while.29 = (s32[]{:T(128)}, f32[2,128,8,128]{3,2,1,0:T(8,128)}, f32[2,128,8]{1,2,0:T(8,128)S(1)}, f32[2,16,1,128,128]{4,3,0,1,2:T(8,128)}, f32[2,128,8,2048]{3,...) while((s32[]{:T(128)}, f32[2,128,8,128]{3,2,1,0:T(8,128)}, ...), condition=%wide.region_11.12_spmd, body=%wide.region_9.11_spmd.sunk | while | flops 1094712320 | bytes 56914324 | solution.py:91
  249.2 1.3 dynamic-slice_bitcast_fusion.2
  250.5 5.3 %fusion.58 = (bf16[8,16,16,8,128]{4,3,2,1,0:T(8,128)(2,1)S(1)}, pred[1,128,8,2048]{3,1,2,0:T(32,128)(4,1)S(1)}, f32[128,8]{0,1:T(8,128)S(1)}) fusion(f32[128,8]{0,1:T(8,128)S(1)} %constant_dynamic-slice_fusion.17, f32[128,2048]{1,0:T(8,128)S(1)} %dynamic-slice_bitcast_fusion.2, f32[2,128,8,2048]{3,1,2,0:T(8,128)} %get-tuple-element.469, ...), kind=kLoop, calls=%fused_computation.24.clone.1 | loop fusion | flops 14679040 | bytes 15736836 | tf_op jit(solution)/shard_map/while
  255.8 1.3 fusion.60
  257.2 1.3 copy-done.8
  261.2 1.3 fusion.59
  265.0 1.3 dynamic-slice_bitcast_fusion.2
  266.3 5.3 %fusion.58 = (bf16[8,16,16,8,128]{4,3,2,1,0:T(8,128)(2,1)S(1)}, pred[1,128,8,2048]{3,1,2,0:T(32,128)(4,1)S(1)}, f32[128,8]{0,1:T(8,128)S(1)}) fusion(f32[128,8]{0,1:T(8,128)S(1)} %constant_dynamic-slice_fusion.17, f32[128,2048]{1,0:T(8,128)S(1)} %dynamic-slice_bitcast_fusion.2, f32[2,128,8,2048]{3,1,2,0:T(8,128)} %get-tuple-element.469, ...), kind=kLoop, calls=%fused_computation.24.clone.1 | loop fusion | flops 14679040 | bytes 15736836 | tf_op jit(solution)/shard_map/while
  271.6 1.3 fusion.60
  273.0 1.3 copy-done.8
  277.0 1.3 fusion.59
  279.6 6.8 %all-to-all-start.3 = ((f32[16,2,128,128]{3,2,1,0:T(8,128)}), f32[16,2,128,128]{3,2,1,0:T(8,128)S(1)}, u32[]{:S(2)}, u32[]{:S(2)}) async-start(f32[16,2,128,128]{3,2,1,0:T(8,128)} %bitcast.142), calls=%async_computation.3 | async-start | bytes 4194304 | tf_op jit(solution)/shard_map/all_to_all | solution.py:100
  287.8 24.2 %all-to-all-done.3 = f32[16,2,128,128]{3,2,1,0:T(8,128)S(1)} async-done(((f32[16,2,128,128]{3,2,1,0:T(8,128)}), f32[16,2,128,128]{3,2,1,0:T(8,128)S(1)}, u32[]{:S(2)}, u32[]{:S(2)}) %all-to-all-start.3) | async-done | bytes 2097184 | tf_op jit(solution)/shard_map/all_to_all | solution.py:100
  312.0 5.2 %fusion.29 = f32[64,128,128]{2,0,1:T(8,128)} fusion(s32[32]{0:T(128)S(1)} %eq.17, f32[4,8,128,128]{3,2,1,0:T(8,128)S(1)} %bitcast.140), kind=kOutput, calls=%fused_computation.45 | convolution fusion | flops 402655232 | bytes 6291584 | tf_op jit(solution)/shard_map/dot_general | solution.py:102
  317.2 39.1 %reduce-scatter.2.cloned.1.call-done = f32[64,16,128]{2,0,1:T(8,128)} async-done(((f32[64,128,128]{2,0,1:T(8,128)}), f32[64,16,128]{2,0,1:T(8,128)}) %reduce-scatter.2.cloned.1.call-update) | async-done | bytes 524304 | tf_op jit(solution)/shard_map/reduce_scatter | solution.py:105
  356.2 2.1 copy.47
  (108 shorter events, 15.3 us)
Async XLA Ops:
  7.2 18.7 %copy-start = (bf16[64,128,128]{2,1,0:T(8,128)(2,1)S(1)}, bf16[64,128,128]{2,1,0:T(8,128)(2,1)}, u32[]{:S(2)}) copy-start(bf16[64,128,128]{2,1,0:T(8,128)(2,1)} %param.15) | copy-start | bytes 6291460
  25.2 0.6 copy-start.16
  27.8 18.6 %all-to-all-start.2 = ((bf16[16,2,128,128]{3,2,1,0:T(8,128)(2,1)}), bf16[16,2,128,128]{3,2,1,0:T(8,128)(2,1)S(1)}, u32[]{:S(2)}, u32[]{:S(2)}) async-start(bf16[16,2,128,128]{3,2,1,0:T(8,128)(2,1)} %broadcast_select_fusion.1), calls=%async_computation.2 | async-start | bytes 2097152 | tf_op jit(solution)/shard_map/all_to_all | solution.py:36
  43.4 7.7 %copy-start.13 = (bf16[256,8,128]{2,1,0:T(8,128)(2,1)S(1)}, bf16[256,8,128]{2,1,0:T(8,128)(2,1)}, u32[]{:S(2)}) copy-start(bf16[256,8,128]{2,1,0:T(8,128)(2,1)} %param.16) | copy-start | bytes 1572868
  46.3 60.8 %all-to-all-start.1 = ((bf16[16,2,128,576]{2,3,1,0:T(8,128)(2,1)}), bf16[16,2,128,576]{2,3,1,0:T(8,128)(2,1)}, u32[]{:S(2)}, u32[]{:S(2)}) async-start(bf16[16,2,128,576]{2,3,1,0:T(8,128)(2,1)} %broadcast_select_fusion), calls=%async_computation.1 | async-start | bytes 9437184 | tf_op jit(solution)/shard_map/all_to_all | solution.py:33
  50.9 56.2 %copy-start.14 = (f32[256,8]{0,1:T(8,128)S(1)}, f32[256,8]{0,1:T(8,128)}, u32[]{:S(2)}) copy-start(f32[256,8]{0,1:T(8,128)} %param.17) | copy-start | bytes 24580
  50.9 56.2 %copy-start.15 = (f32[256,16]{0,1:T(8,128)S(1)}, f32[256,16]{0,1:T(8,128)}, u32[]{:S(2)}) copy-start(f32[256,16]{0,1:T(8,128)} %param.13) | copy-start | bytes 49156
  50.9 189.2 %all-reduce.3.cloned.1.call-start = ((), (), s32[]{:S(2)}) async-start(), calls=%async_computation.6 | async-start | bytes 8388608 | tf_op jit(solution)/shard_map/psum | solution.py:66
  107.1 5.7 %copy-start.3 = (bf16[256,8,128]{2,0,1:T(8,128)(2,1)}, bf16[256,8,128]{2,0,1:T(8,128)(2,1)S(1)}, u32[]{:S(2)}) copy-start(bf16[256,8,128]{2,0,1:T(8,128)(2,1)S(1)} %get-tuple-element.428) | copy-start | bytes 1572868 | tf_op jit(solution)/shard_map/while
  122.4 10.7 %copy-start.9 = (f32[2,128,2048]{2,1,0:T(8,128)S(1)}, f32[2,128,2048]{2,1,0:T(8,128)}, u32[]{:S(2)}) copy-start(f32[2,128,2048]{2,1,0:T(8,128)} %get-tuple-element.404) | copy-start | bytes 6291460 | tf_op jit(solution)/shard_map/while
  122.5 10.7 %copy-start.11 = (f32[2,128,2048]{2,1,0:T(8,128)S(1)}, f32[2,128,2048]{2,1,0:T(8,128)}, u32[]{:S(2)}) copy-start(f32[2,128,2048]{2,1,0:T(8,128)} %get-tuple-element.405) | copy-start | bytes 6291460 | tf_op jit(solution)/shard_map/while
  133.2 3.0 copy-start.4
  133.4 1.3 copy-start.10
  134.7 1.4 copy-start.12
  136.2 5.7 %copy-start.3 = (bf16[256,8,128]{2,0,1:T(8,128)(2,1)}, bf16[256,8,128]{2,0,1:T(8,128)(2,1)S(1)}, u32[]{:S(2)}) copy-start(bf16[256,8,128]{2,0,1:T(8,128)(2,1)S(1)} %get-tuple-element.428) | copy-start | bytes 1572868 | tf_op jit(solution)/shard_map/while
  151.5 10.7 %copy-start.9 = (f32[2,128,2048]{2,1,0:T(8,128)S(1)}, f32[2,128,2048]{2,1,0:T(8,128)}, u32[]{:S(2)}) copy-start(f32[2,128,2048]{2,1,0:T(8,128)} %get-tuple-element.404) | copy-start | bytes 6291460 | tf_op jit(solution)/shard_map/while
  151.5 10.7 %copy-start.11 = (f32[2,128,2048]{2,1,0:T(8,128)S(1)}, f32[2,128,2048]{2,1,0:T(8,128)}, u32[]{:S(2)}) copy-start(f32[2,128,2048]{2,1,0:T(8,128)} %get-tuple-element.405) | copy-start | bytes 6291460 | tf_op jit(solution)/shard_map/while
  162.2 3.0 copy-start.4
  162.5 1.3 copy-start.10
  163.8 1.4 copy-start.12
  165.3 0.8 copy-start.5
  240.1 2.2 copy-start.2
  250.5 5.3 %copy-start.6 = (bf16[256,8,128]{2,0,1:T(8,128)(2,1)S(1)}, bf16[256,8,128]{2,0,1:T(8,128)(2,1)}, u32[]{:S(2)}) copy-start(bf16[256,8,128]{2,0,1:T(8,128)(2,1)} %get-tuple-element.474) | copy-start | bytes 1572868 | tf_op jit(solution)/shard_map/while
  250.5 5.3 %copy-start.7 = (f32[2,16,1,128,128]{4,3,0,1,2:T(8,128)S(1)}, f32[2,16,1,128,128]{4,3,0,1,2:T(8,128)}, u32[]{:S(2)}) copy-start(f32[2,16,1,128,128]{4,3,0,1,2:T(8,128)} %get-tuple-element.453) | copy-start | bytes 6291460 | tf_op jit(solution)/shard_map/while
  257.2 1.3 copy-start.8
  261.2 1.3 copy-start.18
  262.9 1.0 copy-start.19
  266.3 5.3 %copy-start.6 = (bf16[256,8,128]{2,0,1:T(8,128)(2,1)S(1)}, bf16[256,8,128]{2,0,1:T(8,128)(2,1)}, u32[]{:S(2)}) copy-start(bf16[256,8,128]{2,0,1:T(8,128)(2,1)} %get-tuple-element.474) | copy-start | bytes 1572868 | tf_op jit(solution)/shard_map/while
  266.3 5.3 %copy-start.7 = (f32[2,16,1,128,128]{4,3,0,1,2:T(8,128)S(1)}, f32[2,16,1,128,128]{4,3,0,1,2:T(8,128)}, u32[]{:S(2)}) copy-start(f32[2,16,1,128,128]{4,3,0,1,2:T(8,128)} %get-tuple-element.453) | copy-start | bytes 6291460 | tf_op jit(solution)/shard_map/while
  272.9 1.3 copy-start.8
  277.0 1.3 copy-start.18
  278.7 1.0 copy-start.19
  279.6 37.5 %copy-start.20 = (f32[2,128,8]{1,2,0:T(8,128)}, f32[2,128,8]{1,2,0:T(8,128)S(1)}, u32[]{:S(2)}) copy-start(f32[2,128,8]{1,2,0:T(8,128)S(1)} %get-tuple-element.120) | copy-start | bytes 24580
  279.6 7.4 %copy-start.17 = (s32[16,1,2]{2,1,0:T(1,128)S(1)}, s32[16,1,2]{2,1,0:T(1,128)}, u32[]{:S(2)}) copy-start(s32[16,1,2]{2,1,0:T(1,128)} %copy-done.16) | copy-start | bytes 388
  279.6 32.3 %all-to-all-start.3 = ((f32[16,2,128,128]{3,2,1,0:T(8,128)}), f32[16,2,128,128]{3,2,1,0:T(8,128)S(1)}, u32[]{:S(2)}, u32[]{:S(2)}) async-start(f32[16,2,128,128]{3,2,1,0:T(8,128)} %bitcast.142), calls=%async_computation.3 | async-start | bytes 4194304 | tf_op jit(solution)/shard_map/all_to_all | solution.py:100
  286.5 69.8 %reduce-scatter.2.cloned.1.call-start = ((), (), s32[]{:S(2)}) async-start(), calls=%async_computation.5 | async-start | bytes 4718592 | tf_op jit(solution)/shard_map/reduce_scatter | solution.py:105
  317.2 41.2 %copy-start.1 = (bf16[64,128,128]{2,1,0:T(8,128)(2,1)S(1)}, bf16[64,128,128]{2,1,0:T(8,128)(2,1)}, u32[]{:S(2)}) copy-start(bf16[64,128,128]{2,1,0:T(8,128)(2,1)} %param.15) | copy-start | bytes 6291460
Sparse Core Ops, SparseCore 0:
  165.4 74.6 all-reduce.2
  317.3 38.8 reduce-scatter.1
where the time goes:
time: 369 us; the launch traced here: 365 us
  waiting for transfers between devices  195 us (53%)
  local copies, waits for them, and re-layouts  54.9 us (15%)
  matrix products  34.3 us (9%)
  other arithmetic  26.6 us (7%)
  starting transfers between devices  15.3 us (4%)
  blocking collectives  14.8 us (4%)
  between operations  14.2 us (4%)
  loops' own time  10 us (3%)
    psum x1, waiting for transfers between devices, shards(): teacher_sum, score_sum = lax.psum((teacher_flat, indexed_flat), 'head')  74 us
    all_to_all x1, waiting for transfers between devices, shards(): lax.all_to_all(jnp.take(latent, wanted, axis=0), 'seq', split_axis=0, con...  54.8 us
    reduce_scatter x1, waiting for transfers between devices, shards(): lax.psum_scatter(summed_rows.reshape(page_count, returned_grads.shape[2],...  39.1 us
    all_to_all x1, waiting for transfers between devices, shards(): lax.all_to_all(key_grads, 'seq', split_axis=0, concat_axis=0, tiled=True)  24.2 us
    dot_general x2, matrix products, forward_block(): jnp.einsum('qhd,kd->qhk', query_rows, key_rows, preferred_element_type=jn...  21.4 us
    all_to_all x1, blocking collectives, shards(): lax.all_to_all(wanted_slots, 'seq', split_axis=0, concat_axis=0, tiled=True)  14.8 us
    while x2, other arithmetic  10.6 us
    while x44, local copies, waits for them, and re-layouts  10.1 us
  transfers between devices with their start and end apart: 5, of which 5 were waited for; matrix products, arithmetic and copies ran while one was open for 4% of the time, Pallas kernels for 0%

commit v1 on v0

v1 whole, which is shorter than its diff:
```python
import functools
import math

import jax
import jax.numpy as jnp
from jax import lax
from jax.experimental import pallas as pl
from jax.experimental.pallas import tpu as pltpu
from jax.sharding import PartitionSpec as P

BLOCK = 128
SEL = 16
QBLK = 128
LAT = 576
IDXD = 128
IDXH = 64
QPART = 32
WIDE = LAT + IDXD

f32 = jnp.float32
bf16 = jnp.bfloat16

LOG2E = math.log2(math.e)
softmax_scale = 192.0 ** (-0.5)
loss_scale = 2048.0

NT = (((1,), (1,)), ((), ()))
NN = (((1,), (0,)), ((), ()))


def dot_nt(a, b):
    return lax.dot_general(a, b, NT, preferred_element_type=f32)


def dot_nn(a, b):
    return lax.dot_general(a, b, NN, preferred_element_type=f32)


def pack_body(slots_ref, keys_ref, lat_ref, out_ref):
    out_ref[0, :, :IDXD] = keys_ref[0]
    out_ref[0, :, IDXD:] = lat_ref[0]


def pack_pages(slots, index_keys, latent):
    n = slots.shape[0]
    return pl.pallas_call(
        pack_body,
        out_shape=jax.ShapeDtypeStruct((n, BLOCK, WIDE), bf16),
        grid_spec=pltpu.PrefetchScalarGridSpec(
            num_scalar_prefetch=1,
            grid=(n,),
            in_specs=[
                pl.BlockSpec((1, BLOCK, IDXD), lambda i, s: (s[i], 0, 0)),
                pl.BlockSpec((1, BLOCK, LAT), lambda i, s: (s[i], 0, 0)),
            ],
            out_specs=pl.BlockSpec((1, BLOCK, WIDE), lambda i, s: (i, 0, 0)),
        ),
        cost_estimate=pl.CostEstimate(flops=0, bytes_accessed=n * BLOCK * WIDE * 4, transcendentals=0),
        name="pack_pages",
    )(slots, index_keys, latent)


HG = 8


def teacher_body(qa_ref, qb_ref, la_ref, lb_ref, kj_ref, out_ref):
    keys = kj_ref[:, :, IDXD:].reshape(-1, LAT)
    acc = None
    for q_ref, l_ref in ((qa_ref, la_ref), (qb_ref, lb_ref)):
        heads = q_ref.shape[0]
        for g in range(heads // HG):
            rows = q_ref[g * HG : (g + 1) * HG].reshape(HG * QBLK, LAT)
            s = dot_nt(rows, keys)
            for k in range(HG):
                h = g * HG + k
                col = l_ref[:, h : h + 1] * LOG2E
                part = jnp.exp2(s[k * QBLK : (k + 1) * QBLK] * (softmax_scale * LOG2E) - col)
                acc = part if acc is None else acc + part
    out_ref[...] = acc


def teacher_terms(qa, qb, la, lb, kj):
    tile = 2
    n = kj.shape[0]
    whole = lambda a: pl.BlockSpec(a.shape, lambda i: (0,) * a.ndim)
    return pl.pallas_call(
        teacher_body,
        out_shape=jax.ShapeDtypeStruct((QBLK, n * BLOCK), f32),
        grid=(n // tile,),
        in_specs=[whole(qa), whole(qb), whole(la), whole(lb), pl.BlockSpec((tile, BLOCK, WIDE), lambda i: (i, 0, 0))],
        out_specs=pl.BlockSpec((QBLK, tile * BLOCK), lambda i: (0, i)),
        cost_estimate=pl.CostEstimate(flops=2 * 32 * QBLK * n * BLOCK * LAT, bytes_accessed=12 << 20, transcendentals=32 * QBLK * n * BLOCK),
        name="teacher_terms",
    )(qa, qb, la, lb, kj)


def weights_of(pack_ref, e):
    src, i = divmod(e, 8)
    rows = pack_ref[src, 8 * QPART :, :].astype(f32)
    return rows[:, i : i + 1] + rows[:, 8 + i : 9 + i] + rows[:, 16 + i : 17 + i]


def score_body(iq_ref, kj_ref, out_ref):
    keys = kj_ref[:, :, :IDXD].reshape(-1, IDXD)
    acc = None
    for src in range(8):
        raw = dot_nt(iq_ref[src, : 8 * QPART, :], keys)
        for i in range(8):
            part = jnp.maximum(raw[i * QPART : (i + 1) * QPART], 0.0) * weights_of(iq_ref, src * 8 + i)
            acc = part if acc is None else acc + part
    out_ref[...] = acc


def scores(iq, kj):
    tile = 4
    n = kj.shape[0]
    return pl.pallas_call(
        score_body,
        out_shape=jax.ShapeDtypeStruct((QPART, n * BLOCK), f32),
        grid=(n // tile,),
        in_specs=[pl.BlockSpec(iq.shape, lambda i: (0, 0, 0)), pl.BlockSpec((tile, BLOCK, IDXD), lambda i: (i, 0, 0))],
        out_specs=pl.BlockSpec((QPART, tile * BLOCK), lambda i: (0, i)),
        cost_estimate=pl.CostEstimate(flops=2 * IDXH * QPART * n * BLOCK * IDXD, bytes_accessed=2 << 20, transcendentals=0),
        name="scores",
    )(iq, kj)


def backward_body(own_ref, t1_ref, t2_ref, t3_ref, score_ref, iq_ref, iqt_ref, kj_ref, gk_ref, gq_ref, grad_ref, gw_ref):
    step = pl.program_id(0)
    span = gk_ref.shape[0]

    @pl.when(step == 0)
    def _():
        teacher = own_ref[...] + t1_ref[...].astype(f32) + t2_ref[...].astype(f32) + t3_ref[...].astype(f32)
        target = teacher / jnp.sum(teacher, axis=1, keepdims=True)
        score = score_ref[...]
        e = jnp.exp(score - jnp.max(score, axis=1, keepdims=True))
        probs = e / jnp.sum(e, axis=1, keepdims=True)
        grad_ref[...] = loss_scale * (probs - target)
        gq_ref[...] = jnp.zeros_like(gq_ref)
        gw_ref[...] = jnp.zeros_like(gw_ref)

    keys = kj_ref[:, :, :IDXD].reshape(-1, IDXD)
    grad = grad_ref[:, pl.ds(pl.multiple_of(step * span, span), span)]
    gkt = None
    lane = lax.broadcasted_iota(jnp.int32, (QPART, IDXD), 1)
    for src in range(8):
        raw = dot_nt(iq_ref[src, : 8 * QPART, :], keys)
        parts = []
        gws = jnp.zeros((QPART, IDXD), f32)
        for i in range(8):
            r = raw[i * QPART : (i + 1) * QPART]
            gw = grad * jnp.maximum(r, 0.0)
            gws = gws + jnp.where(lane == i, jnp.sum(gw, axis=1, keepdims=True), 0.0)
            w = weights_of(iq_ref, src * 8 + i)
            parts.append(jnp.where(r > 0.0, grad * w, 0.0).astype(bf16))
        gr = jnp.concatenate(parts, axis=0)
        gq_ref[src, : 8 * QPART, :] += dot_nn(gr, keys)
        gq_ref[src, 8 * QPART :, :] += gws
        piece = dot_nn(iqt_ref[:, src * 8 * QPART : (src + 1) * 8 * QPART], gr)
        gkt = piece if gkt is None else gkt + piece
    gk_ref[...] = gkt.T.astype(gk_ref.dtype)


def backward(own, t1, t2, t3, score, iq, iqt, kj):
    tile = 4
    n = kj.shape[0]
    whole = lambda a: pl.BlockSpec(a.shape, lambda i: (0,) * a.ndim)
    return pl.pallas_call(
        backward_body,
        out_shape=(
            jax.ShapeDtypeStruct((n * BLOCK, IDXD), bf16),
            jax.ShapeDtypeStruct((8, 9 * QPART, IDXD), f32),
        ),
        grid=(n // tile,),
        in_specs=[whole(a) for a in (own, t1, t2, t3, score, iq, iqt)] + [pl.BlockSpec((tile, BLOCK, IDXD), lambda i: (i, 0, 0))],
        out_specs=(
            pl.BlockSpec((tile * BLOCK, IDXD), lambda i: (i, 0)),
            pl.BlockSpec((8, 9 * QPART, IDXD), lambda i: (0, 0, 0)),
        ),
        scratch_shapes=[pltpu.VMEM((QPART, n * BLOCK), f32), pltpu.VMEM((8, 128), f32)],
        cost_estimate=pl.CostEstimate(flops=6 * IDXH * QPART * n * BLOCK * IDXD, bytes_accessed=4 << 20, transcendentals=0),
        name="backward",
    )(own, t1, t2, t3, score, iq, iqt, kj)


def split3(a):
    hi = lax.reduce_precision(a, 8, 7)
    mid = lax.reduce_precision(a - hi, 8, 7)
    lo = a - hi - mid
    return [hi.astype(bf16), mid.astype(bf16), lo.astype(bf16)]


def shards(queries, lse, latent, index_keys, index_queries, index_weights, block_lists, block_place):
    page_count = latent.shape[0]
    head = lax.axis_index("head")
    core = head % 2
    quarter = head // 2
    partner = [(h, h ^ 1) for h in range(8)]

    pages = jnp.take(block_place, block_lists, axis=0) % page_count
    wanted = lax.all_to_all(pages.T.reshape(SEL, 1, 2), "seq", split_axis=0, concat_axis=0, tiled=True)
    wanted = wanted.reshape(SEL, 2)

    heads = queries.shape[1]
    by_head = queries.reshape(2, QBLK, heads, LAT).transpose(0, 2, 1, 3)
    qa = lax.dynamic_index_in_dim(by_head, core, 0, keepdims=False)
    qb = lax.ppermute(lax.dynamic_index_in_dim(by_head, 1 - core, 0, keepdims=False), "head", partner)
    lses = lse.reshape(2, QBLK, heads)
    la = lax.dynamic_index_in_dim(lses, core, 0, keepdims=False)
    lb = lax.ppermute(lax.dynamic_index_in_dim(lses, 1 - core, 0, keepdims=False), "head", partner)

    ih = index_queries.shape[1]
    iq = index_queries.reshape(2, 4, QPART, ih, IDXD).transpose(1, 0, 3, 2, 4).reshape(8, ih * QPART, IDXD)
    iw = index_weights.reshape(2, 4, QPART, ih).transpose(1, 0, 2, 3).reshape(8, QPART, ih)
    iw = jnp.concatenate(split3(iw) + [jnp.zeros((8, QPART, IDXD - 3 * ih), bf16)], axis=2)
    iq = lax.all_to_all(jnp.concatenate([iq, iw], axis=1), "head", split_axis=0, concat_axis=0, tiled=True)
    iqt = iq[:, : ih * QPART].reshape(8 * ih * QPART, IDXD).T

    mine = lax.dynamic_index_in_dim(wanted, core, 1, keepdims=False)
    kj = lax.all_to_all(pack_pages(mine, index_keys, latent), "seq", split_axis=0, concat_axis=0, tiled=True)

    score = scores(iq, kj)
    teacher = teacher_terms(qa, qb, la, lb, kj)

    quarters = teacher.reshape(4, QPART, SEL * BLOCK)
    moved = []
    for d in (2, 1, 3):
        ring = [(2 * x + c, 2 * ((x + d) % 4) + c) for x in range(4) for c in range(2)]
        part = lax.dynamic_index_in_dim(quarters, (quarter + d) % 4, 0, keepdims=False)
        moved.append(lax.ppermute(part.astype(bf16), "head", ring))
    own = lax.dynamic_index_in_dim(quarters, quarter, 0, keepdims=False)

    gk, gq = backward(own, *moved, score, iq, iqt, kj)

    gk = lax.all_to_all(gk.reshape(128, 16, IDXD), ("seq", "head"), split_axis=0, concat_axis=0, tiled=True)
    gq = lax.all_to_all(gq, "head", split_axis=0, concat_axis=0, tiled=True)

    slots = jnp.broadcast_to(wanted[:, None, :], (SEL, 4, 2)).reshape(128)
    onehot = (jnp.arange(page_count, dtype=jnp.int32)[:, None] == slots[None, :]).astype(bf16)
    grad_keys = jnp.dot(onehot, gk.reshape(128, 16 * IDXD), preferred_element_type=f32).reshape(page_count, 16, IDXD)

    gw = gq[:, 8 * QPART :, :ih].reshape(4, 2, QPART, ih).transpose(1, 0, 2, 3).reshape(2 * QBLK, ih)
    gq = gq[:, : 8 * QPART].reshape(4, 2, ih, QPART, IDXD).transpose(1, 0, 3, 2, 4).reshape(2 * QBLK, ih, IDXD)
    return gq, gw, grad_keys


def solution(mesh):
    return jax.shard_map(
        shards,
        mesh=mesh,
        in_specs=(
            P("seq", "head", None),
            P("seq", "head"),
            P("seq", None, None),
            P("seq", None, None),
            P("seq", "head", None),
            P("seq", "head"),
            P("seq", None),
            P(),
        ),
        out_specs=(P("seq", "head", None), P("seq", "head"), P("seq", "head", None)),
        check_vma=False,
    )
```

time: 369 us -> 215 us (0.58)
  waiting for transfers between devices: 195 us -> 17.6 us
  Pallas kernels: 0 us -> 58.1 us
  matrix products: 34.3 us -> 0.29 us
  local copies, waits for them, and re-layouts: 54.9 us -> 80.5 us
  other arithmetic: 26.6 us -> 2.42 us
  starting transfers between devices: 15.3 us -> 29.3 us
  between operations: 14.2 us -> 0.78 us
  loops' own time: 10 us -> 0 us
  blocking collectives: 14.8 us -> 23.8 us
    psum x1 -> x0, waiting for transfers between devices: 74 us -> none  [shards(): teacher_sum, score_sum = lax.psum((teacher_flat, indexed_flat), 'head')]
    all_to_all x3 -> x4, waiting for transfers between devices: 81.8 us -> 17.6 us  [the longest x1 14.4 us: shards(): gq = lax.all_to_all(gq, 'head', split_axis=0, concat_axis=0, tiled=True)]
    pallas_call x0 -> x4, Pallas kernels: none -> 58.1 us  [the longest x1 22.1 us: backward(): pl.pallas_call(backward_body, out_shape=(jax.ShapeDtypeStruct((n * BLOCK,...]
    reduce_scatter x1 -> x0, waiting for transfers between devices: 39.1 us -> none  [shards(): lax.psum_scatter(summed_rows.reshape(page_count, returned_grads.shape[2],...]
    dot_general x9 -> x1, matrix products: 34.3 us -> 0.29 us  [shards(): jnp.dot(onehot, gk.reshape(128, 16 * IDXD), preferred_element_type=f32)]
    unnamed x21 -> x18, local copies, waits for them, and re-layouts: 3.53 us -> 28.7 us
    while x46 -> x0, local copies, waits for them, and re-layouts: 11.2 us -> none
    while x2 -> x0, other arithmetic: 10.6 us -> none
  transfers between devices with their start and end apart: 5 -> 9, of which waited for: 5 -> 2; matrix products, arithmetic and copies ran while one was open for 4% -> 36% of each run, Pallas kernels for 0% -> 8%
where the time goes in v1:
time: 215 us; the launch traced here: 213 us
  local copies, waits for them, and re-layouts  80.5 us (37%)
  Pallas kernels  58.1 us (27%)
  starting transfers between devices  29.3 us (14%)
  blocking collectives  23.8 us (11%)
  waiting for transfers between devices  17.6 us (8%)
  other arithmetic  2.42 us (1%)
    unnamed x18, local copies, waits for them, and re-layouts  28.7 us
    all_to_all x1, blocking collectives, shards(): lax.all_to_all(gk.reshape(128, 16, IDXD), ('seq', 'head'), split_axis=0,...  23.8 us
    pallas_call x1, Pallas kernels, backward(): pl.pallas_call(backward_body, out_shape=(jax.ShapeDtypeStruct((n * BLOCK,...  22.1 us
    pallas_call x1, Pallas kernels, teacher_terms(): pl.pallas_call(teacher_body, out_shape=jax.ShapeDtypeStruct((QBLK, n * BL...  18.8 us
    dynamic_slice x1, local copies, waits for them, and re-layouts, shards(): lax.dynamic_index_in_dim(by_head, 1 - core, 0, keepdims=False)  16.7 us
    all_to_all x1, waiting for transfers between devices, shards(): gq = lax.all_to_all(gq, 'head', split_axis=0, concat_axis=0, tiled=True)  14.4 us
    pallas_call x1, Pallas kernels, pack_pages(): pl.pallas_call(pack_body, out_shape=jax.ShapeDtypeStruct((n, BLOCK, WIDE)...  10.6 us
    all_to_all x1, starting transfers between devices, shards(): lax.all_to_all(pages.T.reshape(SEL, 1, 2), 'seq', split_axis=0, concat_ax...  8.59 us
  transfers between devices with their start and end apart: 9, of which 2 were waited for; matrix products, arithmetic and copies ran while one was open for 36% of the time, Pallas kernels for 8%

profile of v1, /device:TPU:1, one launch (start us, length us, event | category | flops | bytes accessed | tf_op | source)
XLA Modules:
  0.0 212.8 jit_solution(3484610278380796089)
XLA Ops:
  0.6 0.7 compare_select_fusion
  1.3 0.1 reshape.82
  1.4 0.7 gather_fusion
  2.1 0.1 reshape.81
  2.2 0.7 fusion.9
  2.9 0.7 copy.76
  3.6 8.6 %all-to-all-start = ((s32[16,1,2]{2,1,0:T(1,128)}), s32[16,1,2]{2,1,0:T(1,128)S(1)}, u32[]{:S(2)}, u32[]{:S(2)}) async-start(s32[16,1,2]{2,1,0:T(1,128)} %copy.76), calls=%async_computation | async-start | bytes 16384 | tf_op jit(solution)/shard_map/all_to_all | solution.py:202
  12.2 0.8 reshape.71
  12.9 0.1 copy.82
  13.1 1.1 copy.81
  14.3 1.0 maximum_maximum_fusion
  15.3 3.2 %all-to-all-done = s32[16,1,2]{2,1,0:T(1,128)S(1)} async-done(((s32[16,1,2]{2,1,0:T(1,128)}), s32[16,1,2]{2,1,0:T(1,128)S(1)}, u32[]{:S(2)}, u32[]{:S(2)}) %all-to-all-start) | async-done | bytes 160 | tf_op jit(solution)/shard_map/all_to_all | solution.py:202
  18.5 6.4 %all-to-all-start.2 = ((bf16[8,288,128]{2,1,0:T(8,128)(2,1)}), bf16[8,288,128]{2,1,0:T(8,128)(2,1)S(1)}, u32[]{:S(2)}, u32[]{:S(2)}) async-start(bf16[8,288,128]{2,1,0:T(8,128)(2,1)} %maximum_maximum_fusion), calls=%async_computation.2 | async-start | bytes 1179648 | tf_op jit(solution)/shard_map/all_to_all | solution.py:217
  24.9 7.7 %reshape.65 = bf16[2,128,16,576]{1,0,3,2:T(2,128)(2,1)} reshape(bf16[256,16,576]{0,2,1:T(8,128)(2,1)} %param.8) | data formatting | bytes 9437184 | tf_op jit(solution)/shard_map/reshape | solution.py:206
  32.6 14.1 %copy.77.lat_ref = bf16[64,128,576]{2,1,0:T(8,128)(2,1)} copy(bf16[64,128,576]{1,2,0:T(8,128)(2,1)} %param.10) | data formatting | bytes 18874368 | tf_op args[2]
  46.7 1.0 dynamic-slice_reduce_fusion.slots_ref
  47.6 10.6 %pack_pages.1 = bf16[16,128,704]{2,1,0:T(8,128)(2,1)} custom-call(s32[16]{0:T(128)} %dynamic-slice_reduce_fusion.slots_ref, bf16[64,128,128]{2,1,0:T(8,128)(2,1)} %keys_ref.1, bf16[64,128,576]{2,1,0:T(8,128)(2,1)} %copy.77.lat_ref), custom_call_target="tpu_custom_call" | custom-call | bytes 5767168 | tf_op jit(solution)/shard_map/pack_pages/pallas_call | solution.py:46
  58.2 4.6 %copy.78 = bf16[16,128,704]{1,2,0:T(8,128)(2,1)} copy(bf16[16,128,704]{2,1,0:T(8,128)(2,1)} %pack_pages.1) | data formatting | bytes 5767168 | tf_op jit(solution)/shard_map/pack_pages/pallas_call | solution.py:46
  62.8 3.7 %all-to-all-start.1 = ((bf16[16,128,704]{1,2,0:T(8,128)(2,1)}), bf16[16,128,704]{1,2,0:T(8,128)(2,1)S(1)}, u32[]{:S(2)}, u32[]{:S(2)}) async-start(bf16[16,128,704]{1,2,0:T(8,128)(2,1)} %copy.78), calls=%async_computation.1 | async-start | bytes 5767168 | tf_op jit(solution)/shard_map/all_to_all | solution.py:221
  66.6 16.7 %dynamic-slice_bitcast_fusion = (bf16[1,16,128,576]{2,0,3,1:T(2,128)(2,1)S(1)}, bf16[1,128,16,576]{1,0,3,2:T(2,128)(2,1)}) fusion(bf16[2,128,16,576]{1,0,3,2:T(2,128)(2,1)} %reshape.65, s32[]{:T(128)S(6)} %select_n.65, s32[]{:T(128)S(6)} %select_n.64), kind=kLoop, calls=%fused_computation.1 | loop fusion | bytes 9437192 | tf_op jit(solution)/shard_map/jit(dynamic_index_in_dim)/dynamic_slice | solution.py:208
  83.3 1.8 copy.99
  85.1 0.8 copy.95
  85.9 1.5 dynamic-slice_bitcast_fusion.2
  87.4 0.5 collective-permute-start.1
  87.9 11.0 %copy.97 = bf16[1,128,16,576]{3,1,2,0:T(8,128)(2,1)} copy(bf16[1,128,16,576]{1,0,3,2:T(2,128)(2,1)} %get-tuple-element.23) | data formatting | bytes 4718592
  98.9 0.8 slice.14
  99.7 2.1 copy.92
  101.8 4.4 %copy.79.qb_ref = bf16[16,128,576]{2,1,0:T(8,128)(2,1)} copy(bf16[16,128,576]{1,2,0:T(8,128)(2,1)} %collective-permute-done) | data formatting | bytes 4718592 | tf_op jit(solution)/shard_map/ppermute | solution.py:208
  106.1 2.8 %copy.80.kj_ref = bf16[16,128,704]{2,1,0:T(8,128)(2,1)} copy(bf16[16,128,704]{1,2,0:T(8,128)(2,1)S(1)} %all-to-all-done.1) | data formatting | bytes 5767168 | tf_op jit(solution)/shard_map/all_to_all | solution.py:221
  108.9 18.8 %teacher_terms.1 = f32[128,2048]{1,0:T(8,128)} custom-call(bf16[16,128,576]{2,1,0:T(8,128)(2,1)} %bitcast.67, bf16[16,128,576]{2,1,0:T(8,128)(2,1)} %copy.79.qb_ref, f32[128,16]{1,0:T(8,128)} %get-tuple-element.31.la_ref, f32[128,16]{1,0:T(8,128)} %collective-permute-done.1.lb_ref, bf16[16,128,704]{2,1,0:T(8,128)(2,1)} %copy.80.kj_ref), custom_call_target="tpu_custom_call" | custom-call | flops 9663676416 | bytes 12582912 | tf_op jit(solution)/shard_map/teacher_terms/pallas_call | solution.py:86
  127.8 1.1 fusion.5
  128.9 2.9 %collective-permute-start.2 = (bf16[32,2048]{1,0:T(8,128)(2,1)S(1)}, bf16[32,2048]{1,0:T(8,128)(2,1)S(1)}, u32[]{:S(2)}, u32[]{:S(2)}) collective-permute-start(bf16[32,2048]{1,0:T(8,128)(2,1)S(1)} %get-tuple-element.26), channel_id=1, source_target_pairs={{0,4},{1,5},{2,6},{3,7},{4,0},{5,1},{6,2},{7,3},{8,12},{9,13},{10,... | collective-permute-start | bytes 393224 | tf_op jit(solution)/shard_map/ppermute | solution.py:231
  131.9 0.3 collective-permute-start.3
  132.2 2.4 %collective-permute-start.4 = (bf16[32,2048]{1,0:T(8,128)(2,1)S(1)}, bf16[32,2048]{1,0:T(8,128)(2,1)S(1)}, u32[]{:S(2)}, u32[]{:S(2)}) collective-permute-start(bf16[32,2048]{1,0:T(8,128)(2,1)S(1)} %get-tuple-element.24), channel_id=1, source_target_pairs={{0,6},{1,7},{2,0},{3,1},{4,2},{5,3},{6,4},{7,5},{8,14},{9,15},{10,... | collective-permute-start | bytes 393224 | tf_op jit(solution)/shard_map/ppermute | solution.py:231
  134.5 1.7 dynamic-slice_bitcast_fusion.1.own_ref
  136.2 6.6 %scores.1.score_ref = f32[32,2048]{1,0:T(8,128)} custom-call(bf16[8,288,128]{2,1,0:T(8,128)(2,1)} %copy-done.2, bf16[16,128,704]{2,1,0:T(8,128)(2,1)} %copy.80.kj_ref), custom_call_target="tpu_custom_call" | custom-call | flops 1073741824 | bytes 2097152 | tf_op jit(solution)/shard_map/scores/pallas_call | solution.py:117
  142.9 0.6 copy-done.4
  143.6 22.1 %backward.1 = (bf16[2048,128]{1,0:T(8,128)(2,1)}, f32[8,288,128]{2,1,0:T(8,128)}) custom-call(f32[32,2048]{1,0:T(8,128)} %dynamic-slice_bitcast_fusion.1.own_ref, bf16[32,2048]{1,0:T(8,128)(2,1)} %copy-done.4, bf16[32,2048]{1,0:T(8,128)(2,1)} %copy-done.5, bf16[32,2048]{1,0:T(8,128)(2,1)} %copy-done.6, f32[32,2048]{1,0:T(8,128)} %scores.1.score_ref, ...), custom_call_target="tpu_custom_call" | custom-call | flops 3221225472 | bytes 4194304 | tf_op jit(solution)/shard_map/backward/pallas_call | solution.py:169
  165.7 23.8 %all_to_all.25 = bf16[128,16,128]{2,1,0:T(8,128)(2,1)S(1)} all-to-all(bf16[128,16,128]{2,1,0:T(8,128)(2,1)} %bitcast.74), channel_id=1, replica_groups=mesh['seq'=16,'head'=8] {'seq','head'}, dimensions={0} | all-to-all | bytes 1048576 | tf_op jit(solution)/shard_map/all_to_all | solution.py:236
  189.5 4.4 %all-to-all-start.3 = ((f32[8,288,128]{2,1,0:T(8,128)}), f32[8,288,128]{2,1,0:T(8,128)S(1)}, u32[]{:S(2)}, u32[]{:S(2)}) async-start(f32[8,288,128]{2,1,0:T(8,128)} %get-tuple-element.5), calls=%async_computation.3 | async-start | bytes 2359296 | tf_op jit(solution)/shard_map/all_to_all | solution.py:237
  193.9 0.1 eq.23
  194.1 0.5 copy.94
  194.6 0.3 fusion
  194.9 1.1 copy.91
  196.0 14.4 %all-to-all-done.3 = f32[8,288,128]{2,1,0:T(8,128)S(1)} async-done(((f32[8,288,128]{2,1,0:T(8,128)}), f32[8,288,128]{2,1,0:T(8,128)S(1)}, u32[]{:S(2)}, u32[]{:S(2)}) %all-to-all-start.3) | async-done | bytes 1179680 | tf_op jit(solution)/shard_map/all_to_all | solution.py:237
  210.4 1.6 copy.86
  212.0 0.1 copy.87
  212.1 0.7 reshape.77
  (28 shorter events, 0.4 us)
Async XLA Ops:
  0.6 0.8 copy-start
  3.6 15.0 %all-to-all-start = ((s32[16,1,2]{2,1,0:T(1,128)}), s32[16,1,2]{2,1,0:T(1,128)S(1)}, u32[]{:S(2)}, u32[]{:S(2)}) async-start(s32[16,1,2]{2,1,0:T(1,128)} %copy.76), calls=%async_computation | async-start | bytes 16384 | tf_op jit(solution)/shard_map/all_to_all | solution.py:202
  18.5 44.3 %all-to-all-start.2 = ((bf16[8,288,128]{2,1,0:T(8,128)(2,1)}), bf16[8,288,128]{2,1,0:T(8,128)(2,1)S(1)}, u32[]{:S(2)}, u32[]{:S(2)}) async-start(bf16[8,288,128]{2,1,0:T(8,128)(2,1)} %maximum_maximum_fusion), calls=%async_computation.2 | async-start | bytes 1179648 | tf_op jit(solution)/shard_map/all_to_all | solution.py:217
  62.8 36.0 %copy-start.2 = (bf16[8,288,128]{2,1,0:T(8,128)(2,1)}, bf16[8,288,128]{2,1,0:T(8,128)(2,1)S(1)}, u32[]{:S(2)}) copy-start(bf16[8,288,128]{2,1,0:T(8,128)(2,1)S(1)} %all-to-all-done.2.iq_ref) | copy-start | bytes 1769476
  62.8 43.3 %all-to-all-start.1 = ((bf16[16,128,704]{1,2,0:T(8,128)(2,1)}), bf16[16,128,704]{1,2,0:T(8,128)(2,1)S(1)}, u32[]{:S(2)}, u32[]{:S(2)}) async-start(bf16[16,128,704]{1,2,0:T(8,128)(2,1)} %copy.78), calls=%async_computation.1 | async-start | bytes 5767168 | tf_op jit(solution)/shard_map/all_to_all | solution.py:221
  83.3 1.8 copy-start.3
  85.1 16.7 %collective-permute-start = (bf16[16,128,576]{1,2,0:T(8,128)(2,1)}, bf16[16,128,576]{1,2,0:T(8,128)(2,1)}, u32[]{:S(2)}, u32[]{:S(2)}) collective-permute-start(bf16[16,128,576]{1,2,0:T(8,128)(2,1)} %bitcast.65), channel_id=1, source_target_pairs={{0,1},{1,0},{2,3},{3,2},{4,5},{5,4},{6,7},{7,6},{8,9},{9,8},{10,11... | collective-permute-start | bytes 7077896 | tf_op jit(solution)/shard_map/ppermute | solution.py:208
  87.4 21.5 %collective-permute-start.1 = (f32[128,16]{1,0:T(8,128)S(1)}, f32[128,16]{1,0:T(8,128)}, u32[]{:S(2)}, u32[]{:S(2)}) collective-permute-start(f32[128,16]{1,0:T(8,128)S(1)} %get-tuple-element.30), channel_id=1, source_target_pairs={{0,1},{1,0},{2,3},{3,2},{4,5},{5,4},{6,7},{7,6},{8,9},{9,8},{10,11... | collective-permute-start | bytes 24584 | tf_op jit(solution)/shard_map/ppermute | solution.py:211
  128.9 13.9 %collective-permute-start.2 = (bf16[32,2048]{1,0:T(8,128)(2,1)S(1)}, bf16[32,2048]{1,0:T(8,128)(2,1)S(1)}, u32[]{:S(2)}, u32[]{:S(2)}) collective-permute-start(bf16[32,2048]{1,0:T(8,128)(2,1)S(1)} %get-tuple-element.26), channel_id=1, source_target_pairs={{0,4},{1,5},{2,6},{3,7},{4,0},{5,1},{6,2},{7,3},{8,12},{9,13},{10,... | collective-permute-start | bytes 393224 | tf_op jit(solution)/shard_map/ppermute | solution.py:231
  131.9 11.0 %collective-permute-start.3 = (bf16[32,2048]{1,0:T(8,128)(2,1)S(1)}, bf16[32,2048]{1,0:T(8,128)(2,1)S(1)}, u32[]{:S(2)}, u32[]{:S(2)}) collective-permute-start(bf16[32,2048]{1,0:T(8,128)(2,1)S(1)} %get-tuple-element.25), channel_id=1, source_target_pairs={{0,2},{1,3},{2,4},{3,5},{4,6},{5,7},{6,0},{7,1},{8,10},{9,11},{10,... | collective-permute-start | bytes 393224 | tf_op jit(solution)/shard_map/ppermute | solution.py:231
  132.2 10.7 %collective-permute-start.4 = (bf16[32,2048]{1,0:T(8,128)(2,1)S(1)}, bf16[32,2048]{1,0:T(8,128)(2,1)S(1)}, u32[]{:S(2)}, u32[]{:S(2)}) collective-permute-start(bf16[32,2048]{1,0:T(8,128)(2,1)S(1)} %get-tuple-element.24), channel_id=1, source_target_pairs={{0,6},{1,7},{2,0},{3,1},{4,2},{5,3},{6,4},{7,5},{8,14},{9,15},{10,... | collective-permute-start | bytes 393224 | tf_op jit(solution)/shard_map/ppermute | solution.py:231
  142.8 0.7 copy-start.4
  142.8 0.7 copy-start.5
  142.9 0.7 copy-start.6
  189.5 20.8 %all-to-all-start.3 = ((f32[8,288,128]{2,1,0:T(8,128)}), f32[8,288,128]{2,1,0:T(8,128)S(1)}, u32[]{:S(2)}, u32[]{:S(2)}) async-start(f32[8,288,128]{2,1,0:T(8,128)} %get-tuple-element.5), calls=%async_computation.3 | async-start | bytes 2359296 | tf_op jit(solution)/shard_map/all_to_all | solution.py:237
  194.5 18.2 %copy-start.1 = (s32[1024]{0:T(1024)S(1)}, s32[1024]{0:T(1024)}, u32[]{:S(2)}) copy-start(s32[1024]{0:T(1024)} %param.15) | copy-start | bytes 12292

commit v2 on v1

v2 whole, which is shorter than its diff:
```python
import math

import jax
import jax.numpy as jnp
from jax import lax
from jax.experimental import pallas as pl
from jax.experimental.pallas import tpu as pltpu
from jax.sharding import PartitionSpec as P

BLOCK = 128
SEL = 16
QBLK = 128
LAT = 576
LATP = 640
IDXD = 128
IDXH = 64
QPART = 32
ROWS = LAT + IDXD

f32 = jnp.float32
bf16 = jnp.bfloat16

LOG2E = math.log2(math.e)
softmax_scale = 192.0 ** (-0.5)
loss_scale = 2048.0


def dot(a, b):
    return lax.dot_general(a, b, (((1,), (0,)), ((), ())), preferred_element_type=f32)


def dot_nt(a, b):
    return lax.dot_general(a, b, (((1,), (1,)), ((), ())), preferred_element_type=f32)


def whole(a):
    return pl.BlockSpec(a.shape, lambda *i: (0,) * a.ndim)


def pack_body(slots_ref, lat_ref, key_ref, out_ref, sems):
    copies = []
    for i in range(SEL):
        copies.append(pltpu.make_async_copy(lat_ref.at[slots_ref[i]], out_ref.at[i, :LAT, :], sems.at[2 * i]))
        copies.append(pltpu.make_async_copy(key_ref.at[slots_ref[i]], out_ref.at[i, LAT:, :], sems.at[2 * i + 1]))
    for c in copies:
        c.start()
    for c in copies:
        c.wait()


def pack_pages(slots, lat, keys):
    return pl.pallas_call(
        pack_body,
        out_shape=jax.ShapeDtypeStruct((SEL, ROWS, BLOCK), bf16),
        in_specs=[
            pl.BlockSpec(memory_space=pltpu.SMEM),
            pl.BlockSpec(memory_space=pl.ANY),
            pl.BlockSpec(memory_space=pl.ANY),
        ],
        out_specs=pl.BlockSpec(memory_space=pltpu.VMEM),
        scratch_shapes=[pltpu.SemaphoreType.DMA((2 * SEL,))],
        cost_estimate=pl.CostEstimate(flops=0, bytes_accessed=6 << 20, transcendentals=0),
        name="pack_pages",
    )(slots, lat, keys)


def flip_body(core_ref, qo_ref, qs_ref, lo_ref, ls_ref, own_ref, send_ref, lown_ref, lsend_ref):
    for q_ref, o_ref in ((qo_ref, own_ref), (qs_ref, send_ref)):
        for h in range(q_ref.shape[0]):
            o_ref[h, :, :LAT] = q_ref[h].T
            o_ref[h, :, LAT:] = jnp.zeros((QBLK, LATP - LAT), bf16)

    @pl.when(pl.program_id(0) == 0)
    def _():
        for l_ref, o_ref in ((lo_ref, lown_ref), (ls_ref, lsend_ref)):
            o_ref[...] = jnp.zeros_like(o_ref)
            o_ref[:, : l_ref.shape[0]] = l_ref[...].T * LOG2E


def flip_queries(core, qt, lt):
    heads = qt.shape[0]
    hb = 4
    qspec = lambda own: pl.BlockSpec((hb, LAT, QBLK), lambda i, c: (i, 0, c[0] if own else 1 - c[0]))
    lspec = lambda own: pl.BlockSpec((heads, QBLK), lambda i, c: (0, c[0] if own else 1 - c[0]))
    oq = jax.ShapeDtypeStruct((heads, QBLK, LATP), bf16)
    ol = jax.ShapeDtypeStruct((QBLK, 128), f32)
    oqs = pl.BlockSpec((hb, QBLK, LATP), lambda i, c: (i, 0, 0))
    ols = pl.BlockSpec((QBLK, 128), lambda i, c: (0, 0))
    return pl.pallas_call(
        flip_body,
        out_shape=(oq, oq, ol, ol),
        grid_spec=pltpu.PrefetchScalarGridSpec(
            num_scalar_prefetch=1,
            grid=(heads // hb,),
            in_specs=[qspec(True), qspec(False), lspec(True), lspec(False)],
            out_specs=(oqs, oqs, ols, ols),
        ),
        cost_estimate=pl.CostEstimate(flops=0, bytes_accessed=24 << 20, transcendentals=0),
        name="flip_queries",
    )(core, qt, qt, lt, lt)


HG = 16
PT = 4


def teacher_body(quarter_ref, qa_ref, qb_ref, la_ref, lb_ref, kj_ref, out_ref):
    keys = jnp.concatenate([kj_ref[p, :LATP, :] for p in range(PT)], axis=1)
    acc = None
    for q_ref, l_ref in ((qa_ref, la_ref), (qb_ref, lb_ref)):
        s = dot(q_ref[...].reshape(HG * QPART, LATP), keys)
        for h in range(HG):
            part = jnp.exp2(s[h * QPART : (h + 1) * QPART] * (softmax_scale * LOG2E) - l_ref[:, h : h + 1])
            acc = part if acc is None else acc + part
    out_ref[...] = acc.astype(out_ref.dtype)


def teacher_terms(quarter, qa, qb, la, lb, kj, dtype):
    n = kj.shape[0]
    qspec = pl.BlockSpec((HG, QPART, LATP), lambda i, q: (0, q[0], 0))
    lspec = pl.BlockSpec((QPART, 128), lambda i, q: (q[0], 0))
    return pl.pallas_call(
        teacher_body,
        out_shape=jax.ShapeDtypeStruct((QPART, n * BLOCK), dtype),
        grid_spec=pltpu.PrefetchScalarGridSpec(
            num_scalar_prefetch=1,
            grid=(n // PT,),
            in_specs=[qspec, qspec, lspec, lspec, pl.BlockSpec((PT, ROWS, BLOCK), lambda i, q: (i, 0, 0))],
            out_specs=pl.BlockSpec((QPART, PT * BLOCK), lambda i, q: (0, i)),
        ),
        cost_estimate=pl.CostEstimate(
            flops=2 * 32 * QPART * n * BLOCK * LAT, bytes_accessed=6 << 20, transcendentals=32 * QPART * n * BLOCK
        ),
        name="teacher_terms",
    )(quarter, qa, qb, la, lb, kj)


PS = 4


def score_body(iq_ref, kj_ref, out_ref, wb_ref):
    @pl.when(pl.program_id(0) == 0)
    def _():
        for src in range(8):
            rows = iq_ref[src, 8 * QPART :, :].astype(f32)
            for i in range(8):
                col = rows[:, i : i + 1] + rows[:, 8 + i : 9 + i] + rows[:, 16 + i : 17 + i]
                wb_ref[src * 8 + i] = jnp.broadcast_to(col, (QPART, 128))

    keys = kj_ref[:, LAT:, :].reshape(-1, IDXD)
    raw = dot_nt(iq_ref[:, : 8 * QPART, :].reshape(IDXH * QPART, IDXD), keys)
    for t in range(PS):
        acc = None
        for e in range(IDXH):
            r = raw[e * QPART : (e + 1) * QPART, t * 128 : (t + 1) * 128]
            part = jnp.maximum(r, 0.0) * wb_ref[e]
            acc = part if acc is None else acc + part
        out_ref[:, t * 128 : (t + 1) * 128] = acc


def scores(iq, kj):
    n = kj.shape[0]
    return pl.pallas_call(
        score_body,
        out_shape=(
            jax.ShapeDtypeStruct((QPART, n * BLOCK), f32),
            jax.ShapeDtypeStruct((IDXH, QPART, 128), f32),
        ),
        grid=(n // PS,),
        in_specs=[whole(iq), pl.BlockSpec((PS, ROWS, BLOCK), lambda i: (i, 0, 0))],
        out_specs=(
            pl.BlockSpec((QPART, PS * BLOCK), lambda i: (0, i)),
            pl.BlockSpec((IDXH, QPART, 128), lambda i: (0, 0, 0)),
        ),
        cost_estimate=pl.CostEstimate(flops=2 * IDXH * QPART * n * BLOCK * IDXD, bytes_accessed=6 << 20, transcendentals=0),
        name="scores",
    )(iq, kj)


PB = 4


def backward_body(own_ref, t1_ref, t2_ref, t3_ref, score_ref, iq_ref, iqt_ref, wb_ref, kj_ref, gk_ref, gq_ref, grad_ref, gr_ref, gw_ref, acc_ref):
    step = pl.program_id(0)
    span = PB * BLOCK

    @pl.when(step == 0)
    def _():
        teacher = own_ref[...] + t1_ref[...].astype(f32) + t2_ref[...].astype(f32) + t3_ref[...].astype(f32)
        target = teacher / jnp.sum(teacher, axis=1, keepdims=True)
        score = score_ref[...]
        e = jnp.exp(score - jnp.max(score, axis=1, keepdims=True))
        probs = e / jnp.sum(e, axis=1, keepdims=True)
        grad_ref[...] = loss_scale * (probs - target)
        acc_ref[...] = jnp.zeros_like(acc_ref)
        gw_ref[...] = jnp.zeros_like(gw_ref)

    keys = kj_ref[:, LAT:, :].reshape(-1, IDXD)
    raw = dot_nt(iq_ref[:, : 8 * QPART, :].reshape(IDXH * QPART, IDXD), keys)
    for e in range(IDXH):
        gsum = gw_ref[e]
        w = wb_ref[e]
        for t in range(PB):
            g = grad_ref[:, pl.ds(pl.multiple_of(step * span + t * 128, 128), 128)]
            r = raw[e * QPART : (e + 1) * QPART, t * 128 : (t + 1) * 128]
            gsum = gsum + g * jnp.maximum(r, 0.0)
            gr_ref[e * QPART : (e + 1) * QPART, t * 128 : (t + 1) * 128] = jnp.where(r > 0.0, g * w, 0.0).astype(bf16)
        gw_ref[e] = gsum
    gr = gr_ref[...]
    gk_ref[...] = dot(iqt_ref[...], gr).T.astype(gk_ref.dtype)
    acc_ref[...] += dot(gr, keys)

    @pl.when(step == pl.num_programs(0) - 1)
    def _():
        lane = lax.broadcasted_iota(jnp.int32, (QPART, 128), 1)
        for src in range(8):
            gq_ref[src, : 8 * QPART, :] = acc_ref[src * 8 * QPART : (src + 1) * 8 * QPART, :].astype(bf16)
            out = jnp.zeros((QPART, 128), f32)
            for i in range(8):
                rest = jnp.sum(gw_ref[src * 8 + i], axis=1, keepdims=True)
                for k in range(3):
                    piece = rest.astype(bf16).astype(f32)
                    out = jnp.where(lane == 8 * k + i, piece, out)
                    rest = rest - piece
            gq_ref[src, 8 * QPART :, :] = out.astype(bf16)


def backward(own, moved, score, iq, iqt, wb, kj):
    n = kj.shape[0]
    fixed = (own, *moved, score, iq, iqt, wb)
    return pl.pallas_call(
        backward_body,
        out_shape=(
            jax.ShapeDtypeStruct((n * BLOCK, IDXD), bf16),
            jax.ShapeDtypeStruct((8, 9 * QPART, IDXD), bf16),
        ),
        grid=(n // PB,),
        in_specs=[whole(a) for a in fixed] + [pl.BlockSpec((PB, ROWS, BLOCK), lambda i: (i, 0, 0))],
        out_specs=(
            pl.BlockSpec((PB * BLOCK, IDXD), lambda i: (i, 0)),
            pl.BlockSpec((8, 9 * QPART, IDXD), lambda i: (0, 0, 0)),
        ),
        scratch_shapes=[
            pltpu.VMEM((QPART, n * BLOCK), f32),
            pltpu.VMEM((IDXH * QPART, PB * BLOCK), bf16),
            pltpu.VMEM((IDXH, QPART, 128), f32),
            pltpu.VMEM((IDXH * QPART, IDXD), f32),
        ],
        cost_estimate=pl.CostEstimate(flops=6 * IDXH * QPART * n * BLOCK * IDXD, bytes_accessed=8 << 20, transcendentals=0),
        name="backward",
    )(*fixed, kj)


def split3(a):
    hi = lax.reduce_precision(a, 8, 7)
    mid = lax.reduce_precision(a - hi, 8, 7)
    lo = a - hi - mid
    return [hi.astype(bf16), mid.astype(bf16), lo.astype(bf16)]


def shards(queries, lse, latent, index_keys, index_queries, index_weights, block_lists, block_place):
    page_count = latent.shape[0]
    head = lax.axis_index("head")
    core = head & 1
    quarter = head >> 1
    partner = [(h, h ^ 1) for h in range(8)]

    pages = block_place.at[block_lists].get(mode="promise_in_bounds") & (page_count - 1)
    wanted = lax.all_to_all(pages.T.reshape(SEL, 1, 2), "seq", split_axis=0, concat_axis=0, tiled=True)
    wanted = wanted.reshape(SEL, 2)

    ih = index_queries.shape[1]
    iq = index_queries.reshape(2, 4, QPART, ih, IDXD).transpose(1, 0, 3, 2, 4).reshape(8, ih * QPART, IDXD)
    iw = index_weights.reshape(2, 4, QPART, ih).transpose(1, 0, 2, 3).reshape(8, QPART, ih)
    iw = jnp.concatenate(split3(iw) + [jnp.zeros((8, QPART, IDXD - 3 * ih), bf16)], axis=2)
    iq = jnp.concatenate([iq, iw], axis=1)

    mine = lax.dynamic_index_in_dim(wanted, core, 1, keepdims=False)
    packed = pack_pages(mine, latent.transpose(0, 2, 1), index_keys)
    packed, iq = lax.optimization_barrier((packed, iq))
    kj = lax.all_to_all(packed, "seq", split_axis=0, concat_axis=0, tiled=True)
    iq = lax.all_to_all(iq, "head", split_axis=0, concat_axis=0, tiled=True)
    iqt = iq[:, : ih * QPART].reshape(8 * ih * QPART, IDXD).T

    qa, qs, la, ls = flip_queries(core.reshape(1), queries.transpose(1, 2, 0), lse.T)
    qb = lax.ppermute(qs, "head", partner)
    lb = lax.ppermute(ls, "head", partner)

    score, wb = scores(iq, kj)

    moved = []
    for d in (2, 1, 3):
        ring = [(2 * x + c, 2 * ((x + d) % 4) + c) for x in range(4) for c in range(2)]
        part = teacher_terms(((quarter + d) & 3).reshape(1), qa, qb, la, lb, kj, bf16)
        moved.append(lax.ppermute(part, "head", ring))
    own = teacher_terms(quarter.reshape(1), qa, qb, la, lb, kj, f32)

    gk, gq = backward(own, moved, score, iq, iqt, wb, kj)

    gk = lax.all_to_all(gk.reshape(128, 16, IDXD), ("seq", "head"), split_axis=0, concat_axis=0, tiled=True)
    gq = lax.all_to_all(gq, "head", split_axis=0, concat_axis=0, tiled=True)

    slots = jnp.broadcast_to(wanted[:, None, :], (SEL, 4, 2)).reshape(128)
    onehot = (jnp.arange(page_count, dtype=jnp.int32)[:, None] == slots[None, :]).astype(bf16)
    grad_keys = jnp.dot(onehot, gk.reshape(128, 16 * IDXD), preferred_element_type=f32).reshape(page_count, 16, IDXD)

    gw = gq[:, 8 * QPART :, : 3 * ih].astype(f32).reshape(4, 2, QPART, 3, ih).sum(axis=3)
    gw = gw.transpose(1, 0, 2, 3).reshape(2 * QBLK, ih)
    gq = gq[:, : 8 * QPART].astype(f32).reshape(4, 2, ih, QPART, IDXD).transpose(1, 0, 3, 2, 4).reshape(2 * QBLK, ih, IDXD)
    return gq, gw, grad_keys


def solution(mesh):
    return jax.shard_map(
        shards,
        mesh=mesh,
        in_specs=(
            P("seq", "head", None),
            P("seq", "head"),
            P("seq", None, None),
            P("seq", None, None),
            P("seq", "head", None),
            P("seq", "head"),
            P("seq", None),
            P(),
        ),
        out_specs=(P("seq", "head", None), P("seq", "head"), P("seq", "head", None)),
        check_vma=False,
    )
```

time: 215 us -> 172 us (0.80)
  local copies, waits for them, and re-layouts: 80.5 us -> 12.9 us
  waiting for transfers between devices: 17.6 us -> 43.8 us
  blocking collectives: 23.8 us -> 34.3 us
  starting transfers between devices: 29.3 us -> 23.6 us
  Pallas kernels: 58.1 us -> 53.8 us
    unnamed x18 -> x17, local copies, waits for them, and re-layouts: 28.7 us -> 3.46 us
    all_to_all x3 -> x2, waiting for transfers between devices: 14.4 us -> 36.8 us  [the longest x1 26 us: shards(): kj = lax.all_to_all(packed, 'seq', split_axis=0, concat_axis=0, tiled=True)]
    dynamic_slice x1 -> x0, local copies, waits for them, and re-layouts: 16.7 us -> none  [shards(): lax.dynamic_index_in_dim(by_head, 1 - core, 0, keepdims=False)]
    pallas_call x1, Pallas kernels: 22.1 us -> 11.6 us  [backward(): pl.pallas_call(backward_body, out_shape=(jax.ShapeDtypeStruct((n * BLOCK,...]
    all_to_all x1 -> x2, blocking collectives: 23.8 us -> 34.3 us  [the longest x1 17.8 us: shards(): gq = lax.all_to_all(gq, 'head', split_axis=0, concat_axis=0, tiled=True)]
    reshape x3, local copies, waits for them, and re-layouts: 9.14 us -> 2.35 us  [the longest x1 1.58 us: shards(): gq[:, :8 * QPART].astype(f32).reshape(4, 2, ih, QPART, IDXD)]
    pallas_call x3 -> x7, Pallas kernels: 36 us -> 42.2 us  [the longest x4 25.6 us: teacher_terms(): pl.pallas_call(teacher_body, out_shape=jax.ShapeDtypeStruct((QPART, n * B...]
    pallas_call x1 -> x0, local copies, waits for them, and re-layouts: 4.62 us -> none  [pack_pages(): pl.pallas_call(pack_body, out_shape=jax.ShapeDtypeStruct((n, BLOCK, WIDE)...]
  transfers between devices with their start and end apart: 9 -> 8, of which waited for: 2 -> 4; matrix products, arithmetic and copies ran while one was open for 36% -> 4% of each run, Pallas kernels for 8% -> 18%
where the time goes in v2:
time: 172 us; the launch traced here: 171 us
  Pallas kernels  53.8 us (31%)
  waiting for transfers between devices  43.8 us (25%)
  blocking collectives  34.3 us (20%)
  starting transfers between devices  23.6 us (14%)
  local copies, waits for them, and re-layouts  12.9 us (8%)
    all_to_all x1, waiting for transfers between devices, shards(): kj = lax.all_to_all(packed, 'seq', split_axis=0, concat_axis=0, tiled=True)  26 us
    pallas_call x4, Pallas kernels, teacher_terms(): pl.pallas_call(teacher_body, out_shape=jax.ShapeDtypeStruct((QPART, n * B...  25.6 us
    all_to_all x1, blocking collectives, shards(): gq = lax.all_to_all(gq, 'head', split_axis=0, concat_axis=0, tiled=True)  17.8 us
    all_to_all x1, blocking collectives, shards(): iq = lax.all_to_all(iq, 'head', split_axis=0, concat_axis=0, tiled=True)  16.5 us
    pallas_call x1, Pallas kernels, backward(): pl.pallas_call(backward_body, out_shape=(jax.ShapeDtypeStruct((n * BLOCK,...  11.6 us
    all_to_all x1, waiting for transfers between devices, shards(): lax.all_to_all(gk.reshape(128, 16, IDXD), ('seq', 'head'), split_axis=0,...  10.9 us
    all_to_all x1, starting transfers between devices, shards(): lax.all_to_all(pages.T.reshape(SEL, 1, 2), 'seq', split_axis=0, concat_ax...  8.59 us
    all_to_all x1, starting transfers between devices, shards(): lax.all_to_all(gk.reshape(128, 16, IDXD), ('seq', 'head'), split_axis=0,...  8.31 us
  transfers between devices with their start and end apart: 8, of which 4 were waited for; matrix products, arithmetic and copies ran while one was open for 4% of the time, Pallas kernels for 18%

profile of v2, /device:TPU:1, one launch (start us, length us, event | category | flops | bytes accessed | tf_op | source)
XLA Modules:
  0.0 170.6 jit_solution(3937336641136853794)
XLA Ops:
  0.6 0.0 copy-start
  0.7 0.7 compare_select_fusion
  1.4 0.1 reshape.98
  1.5 0.7 gather_fusion
  2.2 0.1 reshape.107
  2.3 0.7 copy.47
  2.9 8.6 %all-to-all-start = ((s32[16,1,2]{2,1,0:T(1,128)}), s32[16,1,2]{2,1,0:T(1,128)S(1)}, u32[]{:S(2)}, u32[]{:S(2)}) async-start(s32[16,1,2]{2,1,0:T(1,128)} %copy.47), calls=%async_computation | async-start | bytes 16384 | tf_op jit(solution)/shard_map/all_to_all | solution.py:269
  11.5 0.8 reshape.75
  12.3 0.1 copy.49
  12.5 0.1 copy.48
  12.6 0.1 pad.4.clone
  12.7 0.2 maximum_maximum_fusion
  12.9 5.0 %all-to-all-done = s32[16,1,2]{2,1,0:T(1,128)S(1)} async-done(((s32[16,1,2]{2,1,0:T(1,128)}), s32[16,1,2]{2,1,0:T(1,128)S(1)}, u32[]{:S(2)}, u32[]{:S(2)}) %all-to-all-start) | async-done | bytes 160 | tf_op jit(solution)/shard_map/all_to_all | solution.py:269
  17.9 1.0 dynamic-slice_reduce_fusion.slots_ref
  18.9 4.4 %pack_pages.1 = bf16[16,704,128]{2,1,0:T(8,128)(2,1)} custom-call(s32[16]{0:T(128)} %dynamic-slice_reduce_fusion.slots_ref, bf16[64,576,128]{2,1,0:T(8,128)(2,1)} %bitcast.51, bf16[64,128,128]{2,1,0:T(8,128)(2,1)} %key_ref.1), custom_call_target="tpu_custom_call" | custom-call | bytes 6291456 | tf_op jit(solution)/shard_map/pack_pages/pallas_call | solution.py:52
  23.2 16.5 %all_to_all.25.iq_ref = bf16[8,288,128]{2,1,0:T(8,128)(2,1)S(1)} all-to-all(bf16[8,288,128]{2,1,0:T(8,128)(2,1)S(1)} %maximum_maximum_fusion), channel_id=1, replica_groups=mesh['seq'=16,'head'=8] {'head'}, dimensions={0} | all-to-all | bytes 1179648 | tf_op jit(solution)/shard_map/all_to_all | solution.py:282
  39.8 3.7 %all-to-all-start.1 = ((bf16[16,704,128]{2,1,0:T(8,128)(2,1)}), bf16[16,704,128]{2,1,0:T(8,128)(2,1)S(1)}, u32[]{:S(2)}, u32[]{:S(2)}) async-start(bf16[16,704,128]{2,1,0:T(8,128)(2,1)} %pack_pages.1), calls=%async_computation.1 | async-start | bytes 5767168 | tf_op jit(solution)/shard_map/all_to_all | solution.py:281
  43.5 5.9 %flip_queries.1 = (bf16[16,128,640]{2,1,0:T(8,128)(2,1)}, bf16[16,128,640]{2,1,0:T(8,128)(2,1)}, f32[128,128]{1,0:T(8,128)}, f32[128,128]{1,0:T(8,128)}) custom-call(s32[1]{0:T(128)} %bitcast.1.core_ref, bf16[16,576,256]{2,1,0:T(8,128)(2,1)} %bitcast.49, bf16[16,576,256]{2,1,0:T(8,128)(2,1)} %bitcast.50, f32[16,256]{1,0:T(8,128)} %bitcast.61, f32[16,256]{1,0:T(8,128)} %bitcast.62), custom_call_target="tpu_custom_call" | custom-call | bytes 25165824 | tf_op jit(solution)/shard_map/flip_queries/pallas_call | solution.py:89
  49.4 0.8 collective-permute-start
  50.2 0.1 collective-permute-start.1
  50.3 0.8 slice.14
  51.1 2.0 %copy.58 = bf16[2048,128]{0,1:T(8,128)(2,1)} copy(bf16[2048,128]{1,0:T(8,128)(2,1)} %bitcast.54) | data formatting | bytes 1048576 | tf_op jit(solution)/shard_map/reshape | solution.py:283
  53.2 1.9 %collective-permute-done.1.lb_ref = f32[128,128]{1,0:T(8,128)S(1)} collective-permute-done((f32[128,128]{1,0:T(8,128)}, f32[128,128]{1,0:T(8,128)S(1)}, u32[]{:S(2)}, u32[]{:S(2)}) %collective-permute-start.1) | collective-permute-done | bytes 65568 | tf_op jit(solution)/shard_map/ppermute | solution.py:287
  55.1 26.0 %all-to-all-done.1.kj_ref = bf16[16,704,128]{2,1,0:T(8,128)(2,1)S(1)} async-done(((bf16[16,704,128]{2,1,0:T(8,128)(2,1)}), bf16[16,704,128]{2,1,0:T(8,128)(2,1)S(1)}, u32[]{:S(2)}, u32[]{:S(2)}) %all-to-all-start.1) | async-done | bytes 2883616 | tf_op jit(solution)/shard_map/all_to_all | solution.py:281
  81.1 1.6 copy-done.1
  82.7 6.4 %teacher_terms.7 = bf16[32,2048]{1,0:T(8,128)(2,1)} custom-call(s32[1]{0:T(128)} %bitcast.15.quarter_ref, bf16[16,128,640]{2,1,0:T(8,128)(2,1)} %get-tuple-element.13.qa_ref, bf16[16,128,640]{2,1,0:T(8,128)(2,1)} %collective-permute-done.qb_ref, f32[128,128]{1,0:T(8,128)} %get-tuple-element.15.la_ref, f32[128,128]{1,0:T(8,128)} %copy-done.7, ...), custom_call_target="tpu_custom_call" | custom-call | flops 2415919104 | bytes 6291456 | tf_op jit(solution)/shard_map/teacher_terms/pallas_call | solution.py:122
  89.1 0.9 collective-permute-start.4
  90.0 6.4 %teacher_terms.6 = bf16[32,2048]{1,0:T(8,128)(2,1)} custom-call(s32[1]{0:T(128)} %bitcast.14.quarter_ref, bf16[16,128,640]{2,1,0:T(8,128)(2,1)} %get-tuple-element.13.qa_ref, bf16[16,128,640]{2,1,0:T(8,128)(2,1)} %collective-permute-done.qb_ref, f32[128,128]{1,0:T(8,128)} %get-tuple-element.15.la_ref, f32[128,128]{1,0:T(8,128)} %copy-done.7, ...), custom_call_target="tpu_custom_call" | custom-call | flops 2415919104 | bytes 6291456 | tf_op jit(solution)/shard_map/teacher_terms/pallas_call | solution.py:122
  96.3 0.6 collective-permute-start.3
  96.9 6.4 %teacher_terms.5 = bf16[32,2048]{1,0:T(8,128)(2,1)} custom-call(s32[1]{0:T(128)} %bitcast.13.quarter_ref, bf16[16,128,640]{2,1,0:T(8,128)(2,1)} %get-tuple-element.13.qa_ref, bf16[16,128,640]{2,1,0:T(8,128)(2,1)} %collective-permute-done.qb_ref, f32[128,128]{1,0:T(8,128)} %get-tuple-element.15.la_ref, f32[128,128]{1,0:T(8,128)} %copy-done.7, ...), custom_call_target="tpu_custom_call" | custom-call | flops 2415919104 | bytes 6291456 | tf_op jit(solution)/shard_map/teacher_terms/pallas_call | solution.py:122
  103.3 0.6 collective-permute-start.2
  104.0 6.4 %teacher_terms.4.own_ref = f32[32,2048]{1,0:T(8,128)} custom-call(s32[1]{0:T(128)} %bitcast.quarter_ref, bf16[16,128,640]{2,1,0:T(8,128)(2,1)} %get-tuple-element.13.qa_ref, bf16[16,128,640]{2,1,0:T(8,128)(2,1)} %collective-permute-done.qb_ref, f32[128,128]{1,0:T(8,128)} %get-tuple-element.15.la_ref, f32[128,128]{1,0:T(8,128)} %copy-done.7, ...), custom_call_target="tpu_custom_call" | custom-call | flops 2415919104 | bytes 6291456 | tf_op jit(solution)/shard_map/teacher_terms/pallas_call | solution.py:122
  110.3 6.3 %scores.1 = (f32[32,2048]{1,0:T(8,128)}, f32[64,32,128]{2,1,0:T(8,128)}) custom-call(bf16[8,288,128]{2,1,0:T(8,128)(2,1)} %copy-done.2, bf16[16,704,128]{2,1,0:T(8,128)(2,1)} %copy-done.1), custom_call_target="tpu_custom_call" | custom-call | flops 1073741824 | bytes 6291456 | tf_op jit(solution)/shard_map/scores/pallas_call | solution.py:163
  116.7 0.6 copy-done.4
  117.3 0.1 copy-done.5
  117.4 0.1 copy-done.6
  117.5 11.6 %backward.1 = (bf16[2048,128]{1,0:T(8,128)(2,1)}, bf16[8,288,128]{2,1,0:T(8,128)(2,1)}) custom-call(f32[32,2048]{1,0:T(8,128)} %teacher_terms.4.own_ref, bf16[32,2048]{1,0:T(8,128)(2,1)} %copy-done.6, bf16[32,2048]{1,0:T(8,128)(2,1)} %copy-done.5, bf16[32,2048]{1,0:T(8,128)(2,1)} %copy-done.4, f32[32,2048]{1,0:T(8,128)} %get-tuple-element.19.score_ref, ...), custom_call_target="tpu_custom_call" | custom-call | flops 3221225472 | bytes 8388608 | tf_op jit(solution)/shard_map/backward/pallas_call | solution.py:231
  129.0 17.8 %all_to_all.26 = bf16[8,288,128]{2,1,0:T(8,128)(2,1)S(1)} all-to-all(bf16[8,288,128]{2,1,0:T(8,128)(2,1)} %get-tuple-element.21), channel_id=1, replica_groups=mesh['seq'=16,'head'=8] {'head'}, dimensions={0} | all-to-all | bytes 1179648 | tf_op jit(solution)/shard_map/all_to_all | solution.py:301
  146.8 8.3 %all-to-all-start.4 = ((bf16[128,16,128]{2,1,0:T(8,128)(2,1)}), bf16[128,16,128]{2,1,0:T(8,128)(2,1)S(1)}, u32[]{:S(2)}, u32[]{:S(2)}) async-start(bf16[128,16,128]{2,1,0:T(8,128)(2,1)} %bitcast.25), calls=%async_computation.4 | async-start | bytes 1048576 | tf_op jit(solution)/shard_map/all_to_all | solution.py:300
  155.1 0.1 eq.16
  155.3 0.1 convert_bitcast_fusion
  155.4 1.6 copy.51
  157.0 0.1 copy.52
  157.2 0.7 reshape.86
  157.9 10.9 %all-to-all-done.4 = bf16[128,16,128]{2,1,0:T(8,128)(2,1)S(1)} async-done(((bf16[128,16,128]{2,1,0:T(8,128)(2,1)}), bf16[128,16,128]{2,1,0:T(8,128)(2,1)S(1)}, u32[]{:S(2)}, u32[]{:S(2)}) %all-to-all-start.4) | async-done | bytes 524320 | tf_op jit(solution)/shard_map/all_to_all | solution.py:300
  168.7 0.5 copy.60
  169.2 0.3 fusion
  169.5 1.1 copy.57
  (24 shorter events, 0.2 us)
Async XLA Ops:
  0.6 0.9 copy-start
  0.6 11.8 %copy-start.3 = (bf16[256,8,128]{2,1,0:T(8,128)(2,1)S(1)}, bf16[256,8,128]{2,1,0:T(8,128)(2,1)}, u32[]{:S(2)}) copy-start(bf16[256,8,128]{2,1,0:T(8,128)(2,1)} %param.12) | copy-start | bytes 1572868
  2.9 15.0 %all-to-all-start = ((s32[16,1,2]{2,1,0:T(1,128)}), s32[16,1,2]{2,1,0:T(1,128)S(1)}, u32[]{:S(2)}, u32[]{:S(2)}) async-start(s32[16,1,2]{2,1,0:T(1,128)} %copy.47), calls=%async_computation | async-start | bytes 16384 | tf_op jit(solution)/shard_map/all_to_all | solution.py:269
  39.8 10.5 %copy-start.2 = (bf16[8,288,128]{2,1,0:T(8,128)(2,1)}, bf16[8,288,128]{2,1,0:T(8,128)(2,1)S(1)}, u32[]{:S(2)}) copy-start(bf16[8,288,128]{2,1,0:T(8,128)(2,1)S(1)} %all_to_all.25.iq_ref) | copy-start | bytes 1769476
  39.8 41.3 %all-to-all-start.1 = ((bf16[16,704,128]{2,1,0:T(8,128)(2,1)}), bf16[16,704,128]{2,1,0:T(8,128)(2,1)S(1)}, u32[]{:S(2)}, u32[]{:S(2)}) async-start(bf16[16,704,128]{2,1,0:T(8,128)(2,1)} %pack_pages.1), calls=%async_computation.1 | async-start | bytes 5767168 | tf_op jit(solution)/shard_map/all_to_all | solution.py:281
  49.4 5.7 %collective-permute-start = (bf16[16,128,640]{2,1,0:T(8,128)(2,1)}, bf16[16,128,640]{2,1,0:T(8,128)(2,1)}, u32[]{:S(2)}, u32[]{:S(2)}) collective-permute-start(bf16[16,128,640]{2,1,0:T(8,128)(2,1)} %get-tuple-element.14), channel_id=1, source_target_pairs={{0,1},{1,0},{2,3},{3,2},{4,5},{5,4},{6,7},{7,6},{8,9},{9,8},{10,11... | collective-permute-start | bytes 7864328 | tf_op jit(solution)/shard_map/ppermute | solution.py:286
  50.2 4.9 %collective-permute-start.1 = (f32[128,128]{1,0:T(8,128)}, f32[128,128]{1,0:T(8,128)S(1)}, u32[]{:S(2)}, u32[]{:S(2)}) collective-permute-start(f32[128,128]{1,0:T(8,128)} %get-tuple-element.16), channel_id=1, source_target_pairs={{0,1},{1,0},{2,3},{3,2},{4,5},{5,4},{6,7},{7,6},{8,9},{9,8},{10,11... | collective-permute-start | bytes 196616 | tf_op jit(solution)/shard_map/ppermute | solution.py:287
  55.1 26.0 %copy-start.7 = (f32[128,128]{1,0:T(8,128)}, f32[128,128]{1,0:T(8,128)S(1)}, u32[]{:S(2)}) copy-start(f32[128,128]{1,0:T(8,128)S(1)} %collective-permute-done.1.lb_ref) | copy-start | bytes 196612
  81.1 1.6 copy-start.1
  89.1 27.6 %collective-permute-start.4 = (bf16[32,2048]{1,0:T(8,128)(2,1)}, bf16[32,2048]{1,0:T(8,128)(2,1)S(1)}, u32[]{:S(2)}, u32[]{:S(2)}) collective-permute-start(bf16[32,2048]{1,0:T(8,128)(2,1)} %teacher_terms.7), channel_id=1, source_target_pairs={{0,6},{1,7},{2,0},{3,1},{4,2},{5,3},{6,4},{7,5},{8,14},{9,15},{10,... | collective-permute-start | bytes 393224 | tf_op jit(solution)/shard_map/ppermute | solution.py:295
  96.3 20.3 %collective-permute-start.3 = (bf16[32,2048]{1,0:T(8,128)(2,1)}, bf16[32,2048]{1,0:T(8,128)(2,1)S(1)}, u32[]{:S(2)}, u32[]{:S(2)}) collective-permute-start(bf16[32,2048]{1,0:T(8,128)(2,1)} %teacher_terms.6), channel_id=1, source_target_pairs={{0,2},{1,3},{2,4},{3,5},{4,6},{5,7},{6,0},{7,1},{8,10},{9,11},{10,... | collective-permute-start | bytes 393224 | tf_op jit(solution)/shard_map/ppermute | solution.py:295
  103.3 13.4 %collective-permute-start.2 = (bf16[32,2048]{1,0:T(8,128)(2,1)}, bf16[32,2048]{1,0:T(8,128)(2,1)S(1)}, u32[]{:S(2)}, u32[]{:S(2)}) collective-permute-start(bf16[32,2048]{1,0:T(8,128)(2,1)} %teacher_terms.5), channel_id=1, source_target_pairs={{0,4},{1,5},{2,6},{3,7},{4,0},{5,1},{6,2},{7,3},{8,12},{9,13},{10,... | collective-permute-start | bytes 393224 | tf_op jit(solution)/shard_map/ppermute | solution.py:295
  116.7 0.7 copy-start.4
  116.7 0.7 copy-start.5
  116.7 0.8 copy-start.6
  146.8 21.9 %all-to-all-start.4 = ((bf16[128,16,128]{2,1,0:T(8,128)(2,1)}), bf16[128,16,128]{2,1,0:T(8,128)(2,1)S(1)}, u32[]{:S(2)}, u32[]{:S(2)}) async-start(bf16[128,16,128]{2,1,0:T(8,128)(2,1)} %bitcast.25), calls=%async_computation.4 | async-start | bytes 1048576 | tf_op jit(solution)/shard_map/all_to_all | solution.py:300

commit v3 on v2

v3 whole, which is shorter than its diff:
```python
import math

import jax
import jax.numpy as jnp
from jax import lax
from jax.experimental import pallas as pl
from jax.experimental.pallas import tpu as pltpu
from jax.sharding import PartitionSpec as P


BLOCK = 128
SEL = 16
QBLK = 128
LAT = 576
LATP = 640
IDXD = 128
IDXH = 64
QPART = 32
ROWS = LAT + IDXD
PAGES = 64

f32 = jnp.float32
bf16 = jnp.bfloat16

LOG2E = math.log2(math.e)
softmax_scale = 192.0 ** (-0.5)
loss_scale = 2048.0


def dot(a, b):
    return lax.dot_general(a, b, (((1,), (0,)), ((), ())), preferred_element_type=f32)


def dot_nt(a, b):
    return lax.dot_general(a, b, (((1,), (1,)), ((), ())), preferred_element_type=f32)


def whole(a):
    return pl.BlockSpec(a.shape, lambda *i: (0,) * a.ndim)


def lookup_body(lists_ref, place_ref, out_ref):
    for k in range(SEL):
        for b in range(2):
            out_ref[k, b] = place_ref[lists_ref[b, k]] & (PAGES - 1)


def lookup(lists, place):
    smem = pl.BlockSpec(memory_space=pltpu.SMEM)
    return pl.pallas_call(
        lookup_body,
        out_shape=jax.ShapeDtypeStruct((SEL, 2), jnp.int32),
        in_specs=[smem, smem],
        out_specs=smem,
        name="lookup",
    )(lists, place)


def pack_body(core_ref, wanted_ref, lat_ref, key_ref, out_ref, sems):
    copies = []
    slots_ref = [wanted_ref[i, core_ref[0]] for i in range(SEL)]
    for i in range(SEL):
        copies.append(pltpu.make_async_copy(lat_ref.at[slots_ref[i]], out_ref.at[i, :LAT, :], sems.at[2 * i]))
        copies.append(pltpu.make_async_copy(key_ref.at[slots_ref[i]], out_ref.at[i, LAT:, :], sems.at[2 * i + 1]))
    for c in copies:
        c.start()
    for c in copies:
        c.wait()


def pack_pages(core, wanted, lat, keys):
    return pl.pallas_call(
        pack_body,
        out_shape=jax.ShapeDtypeStruct((SEL, ROWS, BLOCK), bf16),
        in_specs=[
            pl.BlockSpec(memory_space=pltpu.SMEM),
            pl.BlockSpec(memory_space=pltpu.SMEM),
            pl.BlockSpec(memory_space=pl.ANY),
            pl.BlockSpec(memory_space=pl.ANY),
        ],
        out_specs=pl.BlockSpec(memory_space=pltpu.VMEM),
        scratch_shapes=[pltpu.SemaphoreType.DMA((2 * SEL,))],
        cost_estimate=pl.CostEstimate(flops=0, bytes_accessed=6 << 20, transcendentals=0),
        name="pack_pages",
    )(core, wanted, lat, keys)


def flip_body(place_ref, qo_ref, qs_ref, lo_ref, ls_ref, own_ref, send_ref, lown_ref, lsend_ref):
    to = [pl.ds(pl.multiple_of(((k + 3 - place_ref[1]) & 3) * QPART, QPART), QPART) for k in range(4)]
    for q_ref, o_ref in ((qo_ref, own_ref), (qs_ref, send_ref)):
        for h in range(q_ref.shape[0]):
            rows = q_ref[h].T
            for k in range(4):
                o_ref[h, to[k], :LAT] = rows[k * QPART : (k + 1) * QPART]
            o_ref[h, :, LAT:] = jnp.zeros((QBLK, LATP - LAT), bf16)

    @pl.when(pl.program_id(0) == 0)
    def _():
        for l_ref, o_ref in ((lo_ref, lown_ref), (ls_ref, lsend_ref)):
            o_ref[...] = jnp.zeros_like(o_ref)
            rows = l_ref[...].T * LOG2E
            for k in range(4):
                o_ref[to[k], : l_ref.shape[0]] = rows[k * QPART : (k + 1) * QPART]


def flip_queries(place, qt, lt):
    heads = qt.shape[0]
    hb = 4
    qspec = lambda own: pl.BlockSpec((hb, LAT, QBLK), lambda i, c: (i, 0, c[0] if own else 1 - c[0]))
    lspec = lambda own: pl.BlockSpec((heads, QBLK), lambda i, c: (0, c[0] if own else 1 - c[0]))
    oq = jax.ShapeDtypeStruct((heads, QBLK, LATP), bf16)
    ol = jax.ShapeDtypeStruct((QBLK, 128), f32)
    oqs = pl.BlockSpec((hb, QBLK, LATP), lambda i, c: (i, 0, 0))
    ols = pl.BlockSpec((QBLK, 128), lambda i, c: (0, 0))
    return pl.pallas_call(
        flip_body,
        out_shape=(oq, oq, ol, ol),
        grid_spec=pltpu.PrefetchScalarGridSpec(
            num_scalar_prefetch=1,
            grid=(heads // hb,),
            in_specs=[qspec(True), qspec(False), lspec(True), lspec(False)],
            out_specs=(oqs, oqs, ols, ols),
        ),
        cost_estimate=pl.CostEstimate(flops=0, bytes_accessed=24 << 20, transcendentals=0),
        name="flip_queries",
    )(place, qt, qt, lt, lt)


def first_query(h):
    return pl.multiple_of((h & 1) * QBLK + (h >> 1) * QPART, QPART)


def deal_body(head_ref, iq_ref, w_ref, *refs):
    *out_refs, wt_ref = refs
    wt_ref[...] = w_ref[...].T
    for k in range(8):
        q0 = first_query((head_ref[0] + k) & 7)
        rows = pltpu.einshape("qed->eqd", iq_ref[pl.ds(q0, QPART)].astype(f32))
        out_refs[k][: 8 * QPART, :] = rows.reshape(8 * QPART, IDXD).astype(bf16)
        rest = wt_ref[pl.ds(q0, QPART), :]
        pieces = []
        for _ in range(3):
            piece = rest.astype(bf16).astype(f32)
            pieces.append(piece)
            rest = rest - piece
        pieces.append(jnp.zeros((QPART, IDXD - 24), f32))
        out_refs[k][8 * QPART :, :] = jnp.concatenate(pieces, axis=1).astype(bf16)


def deal(head, iq, wt):
    vmem = pl.BlockSpec(memory_space=pltpu.VMEM)
    return pl.pallas_call(
        deal_body,
        out_shape=[jax.ShapeDtypeStruct((9 * QPART, IDXD), bf16)] * 8,
        in_specs=[pl.BlockSpec(memory_space=pltpu.SMEM), vmem, vmem],
        out_specs=[vmem] * 8,
        scratch_shapes=[pltpu.VMEM((2 * QBLK, 8), f32)],
        cost_estimate=pl.CostEstimate(flops=0, bytes_accessed=2 << 20, transcendentals=0),
        name="deal",
    )(head, iq, wt)


def place_body(head_ref, *refs):
    *in_refs, gq_ref, gw_ref, wt_ref = refs
    for k in range(8):
        q0 = first_query((head_ref[0] + k) & 7)
        rows = in_refs[k][: 8 * QPART, :].astype(f32).reshape(8, QPART, IDXD)
        gq_ref[pl.ds(q0, QPART)] = pltpu.einshape("eqd->qed", rows)
        w = in_refs[k][8 * QPART :, :].astype(f32)
        wt_ref[pl.ds(q0, QPART), :] = w[:, :8] + w[:, 8:16] + w[:, 16:24]
    gw_ref[...] = wt_ref[...].T


def place(head, blocks):
    vmem = pl.BlockSpec(memory_space=pltpu.VMEM)
    return pl.pallas_call(
        place_body,
        out_shape=(jax.ShapeDtypeStruct((2 * QBLK, 8, IDXD), f32), jax.ShapeDtypeStruct((8, 2 * QBLK), f32)),
        in_specs=[pl.BlockSpec(memory_space=pltpu.SMEM)] + [vmem] * 8,
        out_specs=(vmem, vmem),
        scratch_shapes=[pltpu.VMEM((2 * QBLK, 8), f32)],
        cost_estimate=pl.CostEstimate(flops=0, bytes_accessed=2 << 20, transcendentals=0),
        name="place",
    )(head, *blocks)


def add_pages_body(wanted_ref, gk_ref, out_ref):
    out_ref[...] = jnp.zeros_like(out_ref)
    for i in range(SEL):
        for b in range(2):
            rows = [gk_ref[i * 8 + 2 * x + b].astype(f32) for x in range(4)]
            out_ref[wanted_ref[i, b]] += (rows[0] + rows[1]) + (rows[2] + rows[3])


def add_pages(wanted, gk):
    vmem = pl.BlockSpec(memory_space=pltpu.VMEM)
    return pl.pallas_call(
        add_pages_body,
        out_shape=jax.ShapeDtypeStruct((PAGES, 16, IDXD), f32),
        in_specs=[pl.BlockSpec(memory_space=pltpu.SMEM), vmem],
        out_specs=vmem,
        cost_estimate=pl.CostEstimate(flops=0, bytes_accessed=1 << 20, transcendentals=0),
        name="add_pages",
    )(wanted, gk)


HG = 8
PT = 4


def teacher_body(qa_ref, qb_ref, la_ref, lb_ref, kj_ref, t1_ref, t2_ref, t3_ref, own_ref):
    keys = jnp.concatenate([kj_ref[p, :LATP, :] for p in range(PT)], axis=1)
    acc = None
    for q_ref, l_ref in ((qa_ref, la_ref), (qb_ref, lb_ref)):
        for g in range(q_ref.shape[0] // HG):
            s = dot(q_ref[g * HG : (g + 1) * HG].reshape(HG * QBLK, LATP), keys)
            for k in range(HG):
                h = g * HG + k
                part = jnp.exp2(s[k * QBLK : (k + 1) * QBLK] * (softmax_scale * LOG2E) - l_ref[:, h : h + 1])
                acc = part if acc is None else acc + part
    for k, ref in enumerate((t1_ref, t2_ref, t3_ref, own_ref)):
        ref[...] = acc[k * QPART : (k + 1) * QPART].astype(ref.dtype)


def teacher_terms(qa, qb, la, lb, kj):
    n = kj.shape[0]
    spec = pl.BlockSpec((QPART, PT * BLOCK), lambda i: (0, i))
    return pl.pallas_call(
        teacher_body,
        out_shape=[jax.ShapeDtypeStruct((QPART, n * BLOCK), t) for t in (bf16, bf16, bf16, f32)],
        grid=(n // PT,),
        in_specs=[whole(qa), whole(qb), whole(la), whole(lb), pl.BlockSpec((PT, ROWS, BLOCK), lambda i: (i, 0, 0))],
        out_specs=[spec] * 4,
        cost_estimate=pl.CostEstimate(
            flops=2 * 32 * QBLK * n * BLOCK * LAT, bytes_accessed=12 << 20, transcendentals=32 * QBLK * n * BLOCK
        ),
        name="teacher_terms",
    )(qa, qb, la, lb, kj)


PS = 4


def score_body(iq_ref, kj_ref, out_ref, wb_ref):
    @pl.when(pl.program_id(0) == 0)
    def _():
        for src in range(8):
            rows = iq_ref[src, 8 * QPART :, :].astype(f32)
            for i in range(8):
                col = rows[:, i : i + 1] + rows[:, 8 + i : 9 + i] + rows[:, 16 + i : 17 + i]
                wb_ref[src * 8 + i] = jnp.broadcast_to(col, (QPART, 128))

    keys = kj_ref[:, LAT:, :].reshape(-1, IDXD)
    raw = dot_nt(iq_ref[:, : 8 * QPART, :].reshape(IDXH * QPART, IDXD), keys)
    for t in range(PS):
        acc = None
        for e in range(IDXH):
            r = raw[e * QPART : (e + 1) * QPART, t * 128 : (t + 1) * 128]
            part = jnp.maximum(r, 0.0) * wb_ref[e]
            acc = part if acc is None else acc + part
        out_ref[:, t * 128 : (t + 1) * 128] = acc


def scores(iq, kj):
    n = kj.shape[0]
    return pl.pallas_call(
        score_body,
        out_shape=(
            jax.ShapeDtypeStruct((QPART, n * BLOCK), f32),
            jax.ShapeDtypeStruct((IDXH, QPART, 128), f32),
        ),
        grid=(n // PS,),
        in_specs=[whole(iq), pl.BlockSpec((PS, ROWS, BLOCK), lambda i: (i, 0, 0))],
        out_specs=(
            pl.BlockSpec((QPART, PS * BLOCK), lambda i: (0, i)),
            pl.BlockSpec((IDXH, QPART, 128), lambda i: (0, 0, 0)),
        ),
        cost_estimate=pl.CostEstimate(flops=2 * IDXH * QPART * n * BLOCK * IDXD, bytes_accessed=6 << 20, transcendentals=0),
        name="scores",
    )(iq, kj)


PB = 4


def backward_body(own_ref, t1_ref, t2_ref, t3_ref, score_ref, iq_ref, iqt_ref, wb_ref, kj_ref, gk_ref, *refs):
    *gq_refs, grad_ref, gr_ref, gw_ref, acc_ref = refs
    step = pl.program_id(0)
    span = PB * BLOCK

    @pl.when(step == 0)
    def _():
        teacher = own_ref[...] + t1_ref[...].astype(f32) + t2_ref[...].astype(f32) + t3_ref[...].astype(f32)
        target = teacher / jnp.sum(teacher, axis=1, keepdims=True)
        score = score_ref[...]
        e = jnp.exp(score - jnp.max(score, axis=1, keepdims=True))
        probs = e / jnp.sum(e, axis=1, keepdims=True)
        grad_ref[...] = loss_scale * (probs - target)
        acc_ref[...] = jnp.zeros_like(acc_ref)
        gw_ref[...] = jnp.zeros_like(gw_ref)

    keys = kj_ref[:, LAT:, :].reshape(-1, IDXD)
    raw = dot_nt(iq_ref[:, : 8 * QPART, :].reshape(IDXH * QPART, IDXD), keys)
    for e in range(IDXH):
        gsum = gw_ref[e]
        w = wb_ref[e]
        for t in range(PB):
            g = grad_ref[:, pl.ds(pl.multiple_of(step * span + t * 128, 128), 128)]
            r = raw[e * QPART : (e + 1) * QPART, t * 128 : (t + 1) * 128]
            gsum = gsum + g * jnp.maximum(r, 0.0)
            gr_ref[e * QPART : (e + 1) * QPART, t * 128 : (t + 1) * 128] = jnp.where(r > 0.0, g * w, 0.0).astype(bf16)
        gw_ref[e] = gsum
    gr = gr_ref[...]
    gk_ref[...] = dot(iqt_ref[...], gr).T.astype(gk_ref.dtype)
    acc_ref[...] += dot(gr, keys)

    @pl.when(step == pl.num_programs(0) - 1)
    def _():
        lane = lax.broadcasted_iota(jnp.int32, (QPART, 128), 1)
        for src in range(8):
            gq_refs[src][: 8 * QPART, :] = acc_ref[src * 8 * QPART : (src + 1) * 8 * QPART, :].astype(bf16)
            out = jnp.zeros((QPART, 128), f32)
            for i in range(8):
                rest = jnp.sum(gw_ref[src * 8 + i], axis=1, keepdims=True)
                for k in range(3):
                    piece = rest.astype(bf16).astype(f32)
                    out = jnp.where(lane == 8 * k + i, piece, out)
                    rest = rest - piece
            gq_refs[src][8 * QPART :, :] = out.astype(bf16)


def backward(own, moved, score, iq, iqt, wb, kj):
    n = kj.shape[0]
    fixed = (own, *moved, score, iq, iqt, wb)
    return pl.pallas_call(
        backward_body,
        out_shape=(
            jax.ShapeDtypeStruct((n * BLOCK, IDXD), bf16),
        )
        + (jax.ShapeDtypeStruct((9 * QPART, IDXD), bf16),) * 8,
        grid=(n // PB,),
        in_specs=[whole(a) for a in fixed] + [pl.BlockSpec((PB, ROWS, BLOCK), lambda i: (i, 0, 0))],
        out_specs=(
            pl.BlockSpec((PB * BLOCK, IDXD), lambda i: (i, 0)),
        )
        + (pl.BlockSpec((9 * QPART, IDXD), lambda i: (0, 0)),) * 8,
        scratch_shapes=[
            pltpu.VMEM((QPART, n * BLOCK), f32),
            pltpu.VMEM((IDXH * QPART, PB * BLOCK), bf16),
            pltpu.VMEM((IDXH, QPART, 128), f32),
            pltpu.VMEM((IDXH * QPART, IDXD), f32),
        ],
        cost_estimate=pl.CostEstimate(flops=6 * IDXH * QPART * n * BLOCK * IDXD, bytes_accessed=8 << 20, transcendentals=0),
        name="backward",
    )(*fixed, kj)


def step(queries, lse, latent, index_keys, index_queries, index_weights, block_lists, block_place):
    head = lax.axis_index("head")
    core = head & 1
    quarter = head >> 1
    partner = [(h, h ^ 1) for h in range(8)]

    wanted = lookup(block_lists, block_place).reshape(SEL, 1, 2)
    wanted = lax.all_to_all(wanted, "seq", split_axis=0, concat_axis=0, tiled=True).reshape(SEL, 2)

    packed = pack_pages(core.reshape(1), wanted, latent.transpose(0, 2, 1), index_keys)
    kj = lax.all_to_all(packed, "seq", split_axis=0, concat_axis=0, tiled=True)

    dealt = [*deal(head.reshape(1), index_queries, index_weights.T)]
    dealt = dealt[:1] + [lax.ppermute(dealt[k], "head", [(h, (h + k) & 7) for h in range(8)]) for k in range(1, 8)]
    iq = jnp.stack(dealt)
    iqt = iq[:, : 8 * QPART].reshape(IDXH * QPART, IDXD).T

    qa, qs, la, ls = flip_queries(jnp.stack([core, quarter]), queries.transpose(1, 2, 0), lse.T)
    qb = lax.ppermute(qs, "head", partner)
    lb = lax.ppermute(ls, "head", partner)

    *parts, own = teacher_terms(qa, qb, la, lb, kj)
    moved = []
    for d in (2, 1, 3):
        ring = [(2 * x + c, 2 * ((x + d) % 4) + c) for x in range(4) for c in range(2)]
        moved.append(lax.ppermute(parts[d - 1], "head", ring))
    score, wb = scores(iq, kj)

    gk, *gq = backward(own, moved, score, iq, iqt, wb, kj)

    gk = lax.all_to_all(gk.reshape(128, 16, IDXD), ("seq", "head"), split_axis=0, concat_axis=0, tiled=True)
    gq = gq[:1] + [lax.ppermute(gq[k], "head", [(h, (h - k) & 7) for h in range(8)]) for k in range(1, 8)]
    gq, gw = place(head.reshape(1), gq)
    return gq, gw.T, add_pages(wanted, gk)


def solution(mesh):
    return jax.shard_map(
        step,
        mesh=mesh,
        in_specs=(
            P("seq", "head", None),
            P("seq", "head"),
            P("seq", None, None),
            P("seq", None, None),
            P("seq", "head", None),
            P("seq", "head"),
            P("seq", None),
            P(),
        ),
        out_specs=(P("seq", "head", None), P("seq", "head"), P("seq", "head", None)),
        check_vma=False,
    )
```

time: 172 us -> 137 us (0.80)
  blocking collectives: 34.3 us -> 0 us
  starting transfers between devices: 23.6 us -> 49.1 us
  waiting for transfers between devices: 43.8 us -> 24 us
  local copies, waits for them, and re-layouts: 12.9 us -> 6.32 us
    all_to_all x2 -> x0, blocking collectives: 34.3 us -> none  [the longest x1 17.8 us: shards(): gq = lax.all_to_all(gq, 'head', split_axis=0, concat_axis=0, tiled=True)]
    all_to_all x3, waiting for transfers between devices: 41.9 us -> 15.9 us  [the longest x1 9.55 us: step(): kj = lax.all_to_all(packed, 'seq', split_axis=0, concat_axis=0, tiled=True)]
    ppermute x5 -> x19, starting transfers between devices: 2.98 us -> 26.1 us  [the longest x7 9.57 us: step(): lax.ppermute(gq[k], 'head', [(h, h - k & 7) for h in range(8)])]
    ppermute x5 -> x19, waiting for transfers between devices: 1.94 us -> 8.1 us  [the longest x7 5.04 us: step(): lax.ppermute(gq[k], 'head', [(h, h - k & 7) for h in range(8)])]
    reshape x9 -> x1, local copies, waits for them, and re-layouts: 6.51 us -> 1.01 us  [step(): iqt = iq[:, :8 * QPART].reshape(IDXH * QPART, IDXD).T]
    all_to_all x3, starting transfers between devices: 20.6 us -> 23 us  [the longest x1 10.7 us: step(): lax.all_to_all(gk.reshape(128, 16, IDXD), ('seq', 'head'), split_axis=0,...]
    unnamed x17 -> x35, local copies, waits for them, and re-layouts: 3.46 us -> 5.26 us
    pallas_call x4 -> x5, Pallas kernels: 25.6 us -> 25.6 us  [the longest x1 17.6 us: teacher_terms(): pl.pallas_call(teacher_body, out_shape=[jax.ShapeDtypeStruct((QPART, n *...]
  transfers between devices with their start and end apart: 8 -> 22, of which waited for: 4 -> 10; matrix products, arithmetic and copies ran while one was open for 4% -> 2% of each run, Pallas kernels for 18% -> 26%
where the time goes in v3:
time: 137 us; the launch traced here: 135 us
  Pallas kernels  54.6 us (40%)
  starting transfers between devices  49.1 us (36%)
  waiting for transfers between devices  24 us (18%)
  local copies, waits for them, and re-layouts  6.32 us (5%)
    pallas_call x1, Pallas kernels, teacher_terms(): pl.pallas_call(teacher_body, out_shape=[jax.ShapeDtypeStruct((QPART, n *...  17.6 us
    pallas_call x1, Pallas kernels, backward(): pl.pallas_call(backward_body, out_shape=(jax.ShapeDtypeStruct((n * BLOCK,...  11.6 us
    all_to_all x1, starting transfers between devices, step(): lax.all_to_all(gk.reshape(128, 16, IDXD), ('seq', 'head'), split_axis=0,...  10.7 us
    ppermute x7, starting transfers between devices, step(): lax.ppermute(gq[k], 'head', [(h, h - k & 7) for h in range(8)])  9.57 us
    all_to_all x1, waiting for transfers between devices, step(): kj = lax.all_to_all(packed, 'seq', split_axis=0, concat_axis=0, tiled=True)  9.55 us
    ppermute x7, starting transfers between devices, step(): lax.ppermute(dealt[k], 'head', [(h, h + k & 7) for h in range(8)])  8.81 us
    all_to_all x1, starting transfers between devices, step(): lax.all_to_all(wanted, 'seq', split_axis=0, concat_axis=0, tiled=True)  8.6 us
    pallas_call x1, Pallas kernels, flip_queries(): pl.pallas_call(flip_body, out_shape=(oq, oq, ol, ol), grid_spec=pltpu.Pre...  6.56 us
  transfers between devices with their start and end apart: 22, of which 10 were waited for; matrix products, arithmetic and copies ran while one was open for 2% of the time, Pallas kernels for 26%

profile of v3, /device:TPU:1, one launch (start us, length us, event | category | flops | bytes accessed | tf_op | source)
XLA Modules:
  0.0 135.4 jit_solution(3875786994326178957)
XLA Ops:
  0.6 1.4 %lookup.1 = s32[16,2]{1,0:T(8,128)} custom-call(s32[2,16]{1,0:T(2,128)} %lists_ref.1, s32[1024]{0:T(1024)} %place_ref.1), custom_call_target="tpu_custom_call" | custom-call | tf_op jit(solution)/shard_map/lookup/pallas_call | solution.py:50
  2.1 8.6 %all-to-all-start = ((s32[16,1,2]{2,1,0:T(1,128)}), s32[16,1,2]{2,1,0:T(1,128)S(1)}, u32[]{:S(2)}, u32[]{:S(2)}) async-start(s32[16,1,2]{2,1,0:T(1,128)} %bitcast.41), calls=%async_computation | async-start | bytes 16384 | tf_op jit(solution)/shard_map/all_to_all | solution.py:365
  10.7 6.4 %all-to-all-done = s32[16,1,2]{2,1,0:T(1,128)S(1)} async-done(((s32[16,1,2]{2,1,0:T(1,128)}), s32[16,1,2]{2,1,0:T(1,128)S(1)}, u32[]{:S(2)}, u32[]{:S(2)}) %all-to-all-start) | async-done | bytes 160 | tf_op jit(solution)/shard_map/all_to_all | solution.py:365
  17.0 0.6 copy-done.3
  17.6 4.5 %pack_pages.1 = bf16[16,704,128]{2,1,0:T(8,128)(2,1)} custom-call(s32[1]{0:T(128)} %bitcast.1.core_ref, s32[16,2]{1,0:T(8,128)} %bitcast.37, bf16[64,576,128]{2,1,0:T(8,128)(2,1)} %bitcast.33, bf16[64,128,128]{2,1,0:T(8,128)(2,1)} %key_ref.1), custom_call_target="tpu_custom_call" | custom-call | bytes 6291456 | tf_op jit(solution)/shard_map/pack_pages/pallas_call | solution.py:72
  22.1 3.7 %all-to-all-start.1 = ((bf16[16,704,128]{2,1,0:T(8,128)(2,1)}), bf16[16,704,128]{2,1,0:T(8,128)(2,1)S(1)}, u32[]{:S(2)}, u32[]{:S(2)}) async-start(bf16[16,704,128]{2,1,0:T(8,128)(2,1)} %pack_pages.1), calls=%async_computation.1 | async-start | bytes 5767168 | tf_op jit(solution)/shard_map/all_to_all | solution.py:368
  25.9 0.6 pad_add_fusion.place_ref
  26.4 6.6 %flip_queries.1 = (bf16[16,128,640]{2,1,0:T(8,128)(2,1)}, bf16[16,128,640]{2,1,0:T(8,128)(2,1)}, f32[128,128]{1,0:T(8,128)}, f32[128,128]{1,0:T(8,128)}) custom-call(s32[2]{0:T(128)} %pad_add_fusion.place_ref, bf16[16,576,256]{2,1,0:T(8,128)(2,1)} %bitcast.31, bf16[16,576,256]{2,1,0:T(8,128)(2,1)} %bitcast.32, f32[16,256]{1,0:T(8,128)} %bitcast.39, ...), custom_call_target="tpu_custom_call" | custom-call | bytes 25165824 | tf_op jit(solution)/shard_map/flip_queries/pallas_call | solution.py:115
  33.0 2.2 %collective-permute-start = (bf16[16,128,640]{2,1,0:T(8,128)(2,1)}, bf16[16,128,640]{2,1,0:T(8,128)(2,1)}, u32[]{:S(2)}, u32[]{:S(2)}) collective-permute-start(bf16[16,128,640]{2,1,0:T(8,128)(2,1)} %get-tuple-element.33), channel_id=1, source_target_pairs={{0,1},{1,0},{2,3},{3,2},{4,5},{5,4},{6,7},{7,6},{8,9},{9,8},{10,11... | collective-permute-start | bytes 7864328 | tf_op jit(solution)/shard_map/ppermute | solution.py:376
  35.3 2.1 %deal.1 = (bf16[288,128]{1,0:T(8,128)(2,1)}, bf16[288,128]{1,0:T(8,128)(2,1)}, bf16[288,128]{1,0:T(8,128)(2,1)}, bf16[288,128]{1,0:T(8,128)(2,1)}, bf16[288,128]...) custom-call(s32[1]{0:T(128)} %bitcast.head_ref, ...), custom_call_target="tpu_custom_call" | custom-call | bytes 2097152 | tf_op jit(solution)/shard_map/deal/pallas_call | solution.py:152
  37.4 1.5 %collective-permute-start.5 = (bf16[288,128]{1,0:T(8,128)(2,1)}, bf16[288,128]{1,0:T(8,128)(2,1)S(1)}, u32[]{:S(2)}, u32[]{:S(2)}) collective-permute-start(bf16[288,128]{1,0:T(8,128)(2,1)} %get-tuple-element.41), channel_id=1, source_target_pairs={{0,1},{1,2},{2,3},{3,4},{4,5},{5,6},{6,7},{7,0},{8,9},{9,10},{10,1... | collective-permute-start | bytes 221192 | tf_op jit(solution)/shard_map/ppermute | solution.py:371
  38.9 1.2 collective-permute-start.6
  40.2 1.6 %collective-permute-start.7 = (bf16[288,128]{1,0:T(8,128)(2,1)}, bf16[288,128]{1,0:T(8,128)(2,1)S(1)}, u32[]{:S(2)}, u32[]{:S(2)}) collective-permute-start(bf16[288,128]{1,0:T(8,128)(2,1)} %get-tuple-element.43), channel_id=1, source_target_pairs={{0,3},{1,4},{2,5},{3,6},{4,7},{5,0},{6,1},{7,2},{8,11},{9,12},{10,... | collective-permute-start | bytes 221192 | tf_op jit(solution)/shard_map/ppermute | solution.py:371
  41.8 0.9 bitcast_dynamic-update-slice_fusion.7
  42.7 0.6 collective-permute-start.8
  43.3 1.0 collective-permute-done.6
  44.2 1.6 %collective-permute-start.9 = (bf16[288,128]{1,0:T(8,128)(2,1)}, bf16[288,128]{1,0:T(8,128)(2,1)S(1)}, u32[]{:S(2)}, u32[]{:S(2)}) collective-permute-start(bf16[288,128]{1,0:T(8,128)(2,1)} %get-tuple-element.45), channel_id=1, source_target_pairs={{0,5},{1,6},{2,7},{3,0},{4,1},{5,2},{6,3},{7,4},{8,13},{9,14},{10,... | collective-permute-start | bytes 221192 | tf_op jit(solution)/shard_map/ppermute | solution.py:371
  45.8 0.1 collective-permute-done.7
  46.0 1.0 collective-permute-start.10
  47.0 1.0 collective-permute-done.8
  47.9 1.3 collective-permute-start.11
  49.2 0.8 collective-permute-done.9
  50.0 0.2 collective-permute-done.10
  50.3 9.5 %all-to-all-done.1.kj_ref = bf16[16,704,128]{2,1,0:T(8,128)(2,1)S(1)} async-done(((bf16[16,704,128]{2,1,0:T(8,128)(2,1)}), bf16[16,704,128]{2,1,0:T(8,128)(2,1)S(1)}, u32[]{:S(2)}, u32[]{:S(2)}) %all-to-all-start.1) | async-done | bytes 2883616 | tf_op jit(solution)/shard_map/all_to_all | solution.py:368
  59.8 1.5 %copy-done = bf16[16,704,128]{2,1,0:T(8,128)(2,1)} copy-done((bf16[16,704,128]{2,1,0:T(8,128)(2,1)}, bf16[16,704,128]{2,1,0:T(8,128)(2,1)S(1)}, u32[]{:S(2)}) %copy-start) | copy-done | bytes 2883608
  61.4 17.6 %teacher_terms.1 = (bf16[32,2048]{1,0:T(8,128)(2,1)}, bf16[32,2048]{1,0:T(8,128)(2,1)}, bf16[32,2048]{1,0:T(8,128)(2,1)}, f32[32,2048]{1,0:T(8,128)}) custom-call(bf16[16,128,640]{2,1,0:T(8,128)(2,1)} %get-tuple-element.32.qa_ref, bf16[16,128,640]{2,1,0:T(8,128)(2,1)} %collective-permute-done.qb_ref, f32[128,128]{1,0:T(8,128)} %get-tuple-element.34.la_ref, ...), custom_call_target="tpu_custom_call" | custom-call | flops 9663676416 | bytes 12582912 | tf_op jit(solution)/shard_map/teacher_terms/pallas_call | solution.py:228
  79.0 2.8 %collective-permute-start.2 = (bf16[32,2048]{1,0:T(8,128)(2,1)}, bf16[32,2048]{1,0:T(8,128)(2,1)S(1)}, u32[]{:S(2)}, u32[]{:S(2)}) collective-permute-start(bf16[32,2048]{1,0:T(8,128)(2,1)} %get-tuple-element.37), channel_id=1, source_target_pairs={{0,4},{1,5},{2,6},{3,7},{4,0},{5,1},{6,2},{7,3},{8,12},{9,13},{10,... | collective-permute-start | bytes 393224 | tf_op jit(solution)/shard_map/ppermute | solution.py:383
  81.8 0.3 collective-permute-start.3
  82.1 2.4 %collective-permute-start.4 = (bf16[32,2048]{1,0:T(8,128)(2,1)}, bf16[32,2048]{1,0:T(8,128)(2,1)S(1)}, u32[]{:S(2)}, u32[]{:S(2)}) collective-permute-start(bf16[32,2048]{1,0:T(8,128)(2,1)} %get-tuple-element.39), channel_id=1, source_target_pairs={{0,6},{1,7},{2,0},{3,1},{4,2},{5,3},{6,4},{7,5},{8,14},{9,15},{10,... | collective-permute-start | bytes 393224 | tf_op jit(solution)/shard_map/ppermute | solution.py:383
  84.5 1.0 copy.24
  85.5 6.3 %scores.1 = (f32[32,2048]{1,0:T(8,128)}, f32[64,32,128]{2,1,0:T(8,128)}) custom-call(bf16[8,288,128]{2,1,0:T(8,128)(2,1)} %copy-done.2, bf16[16,704,128]{2,1,0:T(8,128)(2,1)} %copy-done), custom_call_target="tpu_custom_call" | custom-call | flops 1073741824 | bytes 6291456 | tf_op jit(solution)/shard_map/scores/pallas_call | solution.py:266
  91.9 0.6 copy-done.11
  92.6 11.6 %backward.1 = (bf16[2048,128]{1,0:T(8,128)(2,1)}, bf16[288,128]{1,0:T(8,128)(2,1)}, bf16[288,128]{1,0:T(8,128)(2,1)}, bf16[288,128]{1,0:T(8,128)(2,1)}, bf16[288...) custom-call(f32[32,2048]{1,0:T(8,128)} %get-tuple-element.36.own_ref, ...), custom_call_target="tpu_custom_call" | custom-call | flops 3221225472 | bytes 8388608 | tf_op jit(solution)/shard_map/backward/pallas_call | solution.py:335
  104.2 10.7 %all-to-all-start.2 = ((bf16[128,16,128]{2,1,0:T(8,128)(2,1)}), bf16[128,16,128]{2,1,0:T(8,128)(2,1)S(1)}, u32[]{:S(2)}, u32[]{:S(2)}) async-start(bf16[128,16,128]{2,1,0:T(8,128)(2,1)} %bitcast.35), calls=%async_computation.2 | async-start | bytes 1048576 | tf_op jit(solution)/shard_map/all_to_all | solution.py:388
  114.9 1.2 collective-permute-start.12
  116.1 1.8 %collective-permute-start.13 = (bf16[288,128]{1,0:T(8,128)(2,1)}, bf16[288,128]{1,0:T(8,128)(2,1)S(1)}, u32[]{:S(2)}, u32[]{:S(2)}) collective-permute-start(bf16[288,128]{1,0:T(8,128)(2,1)} %get-tuple-element.52), channel_id=1, source_target_pairs={{0,6},{1,7},{2,0},{3,1},{4,2},{5,3},{6,4},{7,5},{8,14},{9,15},{10,... | collective-permute-start | bytes 221192 | tf_op jit(solution)/shard_map/ppermute | solution.py:389
  117.9 1.0 collective-permute-start.14
  118.9 2.4 %collective-permute-start.15 = (bf16[288,128]{1,0:T(8,128)(2,1)}, bf16[288,128]{1,0:T(8,128)(2,1)S(1)}, u32[]{:S(2)}, u32[]{:S(2)}) collective-permute-start(bf16[288,128]{1,0:T(8,128)(2,1)} %get-tuple-element.54), channel_id=1, source_target_pairs={{0,4},{1,5},{2,6},{3,7},{4,0},{5,1},{6,2},{7,3},{8,12},{9,13},{10,... | collective-permute-start | bytes 221192 | tf_op jit(solution)/shard_map/ppermute | solution.py:389
  121.4 0.6 collective-permute-start.16
  122.0 2.6 %collective-permute-done.12.refs_1_ = bf16[288,128]{1,0:T(8,128)(2,1)S(1)} collective-permute-done((bf16[288,128]{1,0:T(8,128)(2,1)}, bf16[288,128]{1,0:T(8,128)(2,1)S(1)}, u32[]{:S(2)}, u32[]{:S(2)}) %collective-permute-start.12) | collective-permute-done | bytes 73760 | tf_op jit(solution)/shard_map/ppermute | solution.py:389
  124.6 1.2 collective-permute-start.17
  125.8 1.3 collective-permute-start.18
  127.2 0.8 collective-permute-done.16.refs_5_
  128.0 1.6 %collective-permute-done.17.refs_6_ = bf16[288,128]{1,0:T(8,128)(2,1)S(1)} collective-permute-done((bf16[288,128]{1,0:T(8,128)(2,1)}, bf16[288,128]{1,0:T(8,128)(2,1)S(1)}, u32[]{:S(2)}, u32[]{:S(2)}) %collective-permute-start.17) | collective-permute-done | bytes 73760 | tf_op jit(solution)/shard_map/ppermute | solution.py:389
  129.6 0.6 copy-done.9
  130.2 2.4 %place.1 = (f32[256,8,128]{2,1,0:T(8,128)}, f32[8,256]{1,0:T(8,128)}) custom-call(s32[1]{0:T(128)} %bitcast.head_ref, bf16[288,128]{1,0:T(8,128)(2,1)} %get-tuple-element.50.refs_0_, bf16[288,128]{1,0:T(8,128)(2,1)} %copy-done.4, bf16[288,128]{1,0:T(8,128)(2,1)} %copy-done.5, bf16[288,128]{1,0:T(8,128)(2,1)} %copy-done.6, bf16[288,128]{1,0:T(8,128)(2,1)} %copy-done.7, ...), custom_call_target="tpu_custom_call" | custom-call | bytes 2097152 | tf_op jit(solution)/shard_map/place/pallas_call | solution.py:176
  132.7 0.8 copy-done.1
  133.5 2.0 %add_pages.1 = f32[64,16,128]{2,1,0:T(8,128)} custom-call(s32[16,2]{1,0:T(8,128)} %bitcast.38, bf16[128,16,128]{2,1,0:T(8,128)(2,1)} %copy-done.1), custom_call_target="tpu_custom_call" | custom-call | bytes 1048576 | tf_op jit(solution)/shard_map/add_pages/pallas_call | solution.py:197
  (44 shorter events, 0.4 us)
Async XLA Ops:
  2.1 15.0 %all-to-all-start = ((s32[16,1,2]{2,1,0:T(1,128)}), s32[16,1,2]{2,1,0:T(1,128)S(1)}, u32[]{:S(2)}, u32[]{:S(2)}) async-start(s32[16,1,2]{2,1,0:T(1,128)} %bitcast.41), calls=%async_computation | async-start | bytes 16384 | tf_op jit(solution)/shard_map/all_to_all | solution.py:365
  17.0 0.6 copy-start.3
  22.1 37.7 %all-to-all-start.1 = ((bf16[16,704,128]{2,1,0:T(8,128)(2,1)}), bf16[16,704,128]{2,1,0:T(8,128)(2,1)S(1)}, u32[]{:S(2)}, u32[]{:S(2)}) async-start(bf16[16,704,128]{2,1,0:T(8,128)(2,1)} %pack_pages.1), calls=%async_computation.1 | async-start | bytes 5767168 | tf_op jit(solution)/shard_map/all_to_all | solution.py:368
  33.0 17.3 %collective-permute-start = (bf16[16,128,640]{2,1,0:T(8,128)(2,1)}, bf16[16,128,640]{2,1,0:T(8,128)(2,1)}, u32[]{:S(2)}, u32[]{:S(2)}) collective-permute-start(bf16[16,128,640]{2,1,0:T(8,128)(2,1)} %get-tuple-element.33), channel_id=1, source_target_pairs={{0,1},{1,0},{2,3},{3,2},{4,5},{5,4},{6,7},{7,6},{8,9},{9,8},{10,11... | collective-permute-start | bytes 7864328 | tf_op jit(solution)/shard_map/ppermute | solution.py:376
  35.2 15.1 %collective-permute-start.1 = (f32[128,128]{1,0:T(8,128)}, f32[128,128]{1,0:T(8,128)}, u32[]{:S(2)}, u32[]{:S(2)}) collective-permute-start(f32[128,128]{1,0:T(8,128)} %get-tuple-element.35), channel_id=1, source_target_pairs={{0,1},{1,0},{2,3},{3,2},{4,5},{5,4},{6,7},{7,6},{8,9},{9,8},{10,11... | collective-permute-start | bytes 196616 | tf_op jit(solution)/shard_map/ppermute | solution.py:377
  37.4 5.2 %collective-permute-start.5 = (bf16[288,128]{1,0:T(8,128)(2,1)}, bf16[288,128]{1,0:T(8,128)(2,1)S(1)}, u32[]{:S(2)}, u32[]{:S(2)}) collective-permute-start(bf16[288,128]{1,0:T(8,128)(2,1)} %get-tuple-element.41), channel_id=1, source_target_pairs={{0,1},{1,2},{2,3},{3,4},{4,5},{5,6},{6,7},{7,0},{8,9},{9,10},{10,1... | collective-permute-start | bytes 221192 | tf_op jit(solution)/shard_map/ppermute | solution.py:371
  38.9 5.3 %collective-permute-start.6 = (bf16[288,128]{1,0:T(8,128)(2,1)}, bf16[288,128]{1,0:T(8,128)(2,1)S(1)}, u32[]{:S(2)}, u32[]{:S(2)}) collective-permute-start(bf16[288,128]{1,0:T(8,128)(2,1)} %get-tuple-element.42), channel_id=1, source_target_pairs={{0,2},{1,3},{2,4},{3,5},{4,6},{5,7},{6,0},{7,1},{8,10},{9,11},{10,... | collective-permute-start | bytes 221192 | tf_op jit(solution)/shard_map/ppermute | solution.py:371
  40.2 5.8 %collective-permute-start.7 = (bf16[288,128]{1,0:T(8,128)(2,1)}, bf16[288,128]{1,0:T(8,128)(2,1)S(1)}, u32[]{:S(2)}, u32[]{:S(2)}) collective-permute-start(bf16[288,128]{1,0:T(8,128)(2,1)} %get-tuple-element.43), channel_id=1, source_target_pairs={{0,3},{1,4},{2,5},{3,6},{4,7},{5,0},{6,1},{7,2},{8,11},{9,12},{10,... | collective-permute-start | bytes 221192 | tf_op jit(solution)/shard_map/ppermute | solution.py:371
  42.7 5.3 %collective-permute-start.8 = (bf16[288,128]{1,0:T(8,128)(2,1)}, bf16[288,128]{1,0:T(8,128)(2,1)S(1)}, u32[]{:S(2)}, u32[]{:S(2)}) collective-permute-start(bf16[288,128]{1,0:T(8,128)(2,1)} %get-tuple-element.44), channel_id=1, source_target_pairs={{0,4},{1,5},{2,6},{3,7},{4,0},{5,1},{6,2},{7,3},{8,12},{9,13},{10,... | collective-permute-start | bytes 221192 | tf_op jit(solution)/shard_map/ppermute | solution.py:371
  44.2 5.8 %collective-permute-start.9 = (bf16[288,128]{1,0:T(8,128)(2,1)}, bf16[288,128]{1,0:T(8,128)(2,1)S(1)}, u32[]{:S(2)}, u32[]{:S(2)}) collective-permute-start(bf16[288,128]{1,0:T(8,128)(2,1)} %get-tuple-element.45), channel_id=1, source_target_pairs={{0,5},{1,6},{2,7},{3,0},{4,1},{5,2},{6,3},{7,4},{8,13},{9,14},{10,... | collective-permute-start | bytes 221192 | tf_op jit(solution)/shard_map/ppermute | solution.py:371
  46.0 4.3 %collective-permute-start.10 = (bf16[288,128]{1,0:T(8,128)(2,1)}, bf16[288,128]{1,0:T(8,128)(2,1)S(1)}, u32[]{:S(2)}, u32[]{:S(2)}) collective-permute-start(bf16[288,128]{1,0:T(8,128)(2,1)} %get-tuple-element.46), channel_id=1, source_target_pairs={{0,6},{1,7},{2,0},{3,1},{4,2},{5,3},{6,4},{7,5},{8,14},{9,15},{10,... | collective-permute-start | bytes 221192 | tf_op jit(solution)/shard_map/ppermute | solution.py:371
  47.9 36.5 %collective-permute-start.11 = (bf16[288,128]{1,0:T(8,128)(2,1)}, bf16[288,128]{1,0:T(8,128)(2,1)S(1)}, u32[]{:S(2)}, u32[]{:S(2)}) collective-permute-start(bf16[288,128]{1,0:T(8,128)(2,1)} %get-tuple-element.47), channel_id=1, source_target_pairs={{0,7},{1,0},{2,1},{3,2},{4,3},{5,4},{6,5},{7,6},{8,15},{9,8},{10,9... | collective-permute-start | bytes 221192 | tf_op jit(solution)/shard_map/ppermute | solution.py:371
  59.8 1.6 %copy-start = (bf16[16,704,128]{2,1,0:T(8,128)(2,1)}, bf16[16,704,128]{2,1,0:T(8,128)(2,1)S(1)}, u32[]{:S(2)}) copy-start(bf16[16,704,128]{2,1,0:T(8,128)(2,1)S(1)} %all-to-all-done.1.kj_ref) | copy-start | bytes 8650756
  79.0 12.9 %collective-permute-start.2 = (bf16[32,2048]{1,0:T(8,128)(2,1)}, bf16[32,2048]{1,0:T(8,128)(2,1)S(1)}, u32[]{:S(2)}, u32[]{:S(2)}) collective-permute-start(bf16[32,2048]{1,0:T(8,128)(2,1)} %get-tuple-element.37), channel_id=1, source_target_pairs={{0,4},{1,5},{2,6},{3,7},{4,0},{5,1},{6,2},{7,3},{8,12},{9,13},{10,... | collective-permute-start | bytes 393224 | tf_op jit(solution)/shard_map/ppermute | solution.py:383
  81.8 10.1 %collective-permute-start.3 = (bf16[32,2048]{1,0:T(8,128)(2,1)}, bf16[32,2048]{1,0:T(8,128)(2,1)S(1)}, u32[]{:S(2)}, u32[]{:S(2)}) collective-permute-start(bf16[32,2048]{1,0:T(8,128)(2,1)} %get-tuple-element.38), channel_id=1, source_target_pairs={{0,2},{1,3},{2,4},{3,5},{4,6},{5,7},{6,0},{7,1},{8,10},{9,11},{10,... | collective-permute-start | bytes 393224 | tf_op jit(solution)/shard_map/ppermute | solution.py:383
  82.1 9.8 %collective-permute-start.4 = (bf16[32,2048]{1,0:T(8,128)(2,1)}, bf16[32,2048]{1,0:T(8,128)(2,1)S(1)}, u32[]{:S(2)}, u32[]{:S(2)}) collective-permute-start(bf16[32,2048]{1,0:T(8,128)(2,1)} %get-tuple-element.39), channel_id=1, source_target_pairs={{0,6},{1,7},{2,0},{3,1},{4,2},{5,3},{6,4},{7,5},{8,14},{9,15},{10,... | collective-permute-start | bytes 393224 | tf_op jit(solution)/shard_map/ppermute | solution.py:383
  84.5 1.1 copy-start.2
  91.9 0.6 copy-start.11
  91.9 0.7 copy-start.12
  91.9 0.7 copy-start.13
  104.2 28.4 %all-to-all-start.2 = ((bf16[128,16,128]{2,1,0:T(8,128)(2,1)}), bf16[128,16,128]{2,1,0:T(8,128)(2,1)S(1)}, u32[]{:S(2)}, u32[]{:S(2)}) async-start(bf16[128,16,128]{2,1,0:T(8,128)(2,1)} %bitcast.35), calls=%async_computation.2 | async-start | bytes 1048576 | tf_op jit(solution)/shard_map/all_to_all | solution.py:388
  114.9 9.7 %collective-permute-start.12 = (bf16[288,128]{1,0:T(8,128)(2,1)}, bf16[288,128]{1,0:T(8,128)(2,1)S(1)}, u32[]{:S(2)}, u32[]{:S(2)}) collective-permute-start(bf16[288,128]{1,0:T(8,128)(2,1)} %get-tuple-element.51), channel_id=1, source_target_pairs={{0,7},{1,0},{2,1},{3,2},{4,3},{5,4},{6,5},{7,6},{8,15},{9,8},{10,9... | collective-permute-start | bytes 221192 | tf_op jit(solution)/shard_map/ppermute | solution.py:389
  116.1 9.7 %collective-permute-start.13 = (bf16[288,128]{1,0:T(8,128)(2,1)}, bf16[288,128]{1,0:T(8,128)(2,1)S(1)}, u32[]{:S(2)}, u32[]{:S(2)}) collective-permute-start(bf16[288,128]{1,0:T(8,128)(2,1)} %get-tuple-element.52), channel_id=1, source_target_pairs={{0,6},{1,7},{2,0},{3,1},{4,2},{5,3},{6,4},{7,5},{8,14},{9,15},{10,... | collective-permute-start | bytes 221192 | tf_op jit(solution)/shard_map/ppermute | solution.py:389
  117.9 9.2 %collective-permute-start.14 = (bf16[288,128]{1,0:T(8,128)(2,1)}, bf16[288,128]{1,0:T(8,128)(2,1)S(1)}, u32[]{:S(2)}, u32[]{:S(2)}) collective-permute-start(bf16[288,128]{1,0:T(8,128)(2,1)} %get-tuple-element.53), channel_id=1, source_target_pairs={{0,5},{1,6},{2,7},{3,0},{4,1},{5,2},{6,3},{7,4},{8,13},{9,14},{10,... | collective-permute-start | bytes 221192 | tf_op jit(solution)/shard_map/ppermute | solution.py:389
  118.9 8.2 %collective-permute-start.15 = (bf16[288,128]{1,0:T(8,128)(2,1)}, bf16[288,128]{1,0:T(8,128)(2,1)S(1)}, u32[]{:S(2)}, u32[]{:S(2)}) collective-permute-start(bf16[288,128]{1,0:T(8,128)(2,1)} %get-tuple-element.54), channel_id=1, source_target_pairs={{0,4},{1,5},{2,6},{3,7},{4,0},{5,1},{6,2},{7,3},{8,12},{9,13},{10,... | collective-permute-start | bytes 221192 | tf_op jit(solution)/shard_map/ppermute | solution.py:389
  121.4 6.6 %collective-permute-start.16 = (bf16[288,128]{1,0:T(8,128)(2,1)}, bf16[288,128]{1,0:T(8,128)(2,1)S(1)}, u32[]{:S(2)}, u32[]{:S(2)}) collective-permute-start(bf16[288,128]{1,0:T(8,128)(2,1)} %get-tuple-element.55), channel_id=1, source_target_pairs={{0,3},{1,4},{2,5},{3,6},{4,7},{5,0},{6,1},{7,2},{8,11},{9,12},{10,... | collective-permute-start | bytes 221192 | tf_op jit(solution)/shard_map/ppermute | solution.py:389
  124.6 4.9 %copy-start.4 = (bf16[288,128]{1,0:T(8,128)(2,1)}, bf16[288,128]{1,0:T(8,128)(2,1)S(1)}, u32[]{:S(2)}) copy-start(bf16[288,128]{1,0:T(8,128)(2,1)S(1)} %collective-permute-done.12.refs_1_) | copy-start | bytes 221188
  124.6 4.9 %collective-permute-start.17 = (bf16[288,128]{1,0:T(8,128)(2,1)}, bf16[288,128]{1,0:T(8,128)(2,1)S(1)}, u32[]{:S(2)}, u32[]{:S(2)}) collective-permute-start(bf16[288,128]{1,0:T(8,128)(2,1)} %get-tuple-element.56), channel_id=1, source_target_pairs={{0,2},{1,3},{2,4},{3,5},{4,6},{5,7},{6,0},{7,1},{8,10},{9,11},{10,... | collective-permute-start | bytes 221192 | tf_op jit(solution)/shard_map/ppermute | solution.py:389
  125.8 3.7 %copy-start.5 = (bf16[288,128]{1,0:T(8,128)(2,1)}, bf16[288,128]{1,0:T(8,128)(2,1)S(1)}, u32[]{:S(2)}) copy-start(bf16[288,128]{1,0:T(8,128)(2,1)S(1)} %collective-permute-done.13.refs_2_) | copy-start | bytes 221188
  125.8 3.7 %collective-permute-start.18 = (bf16[288,128]{1,0:T(8,128)(2,1)}, bf16[288,128]{1,0:T(8,128)(2,1)S(1)}, u32[]{:S(2)}, u32[]{:S(2)}) collective-permute-start(bf16[288,128]{1,0:T(8,128)(2,1)} %get-tuple-element.57), channel_id=1, source_target_pairs={{0,1},{1,2},{2,3},{3,4},{4,5},{5,6},{6,7},{7,0},{8,9},{9,10},{10,1... | collective-permute-start | bytes 221192 | tf_op jit(solution)/shard_map/ppermute | solution.py:389
  127.1 2.4 %copy-start.6 = (bf16[288,128]{1,0:T(8,128)(2,1)}, bf16[288,128]{1,0:T(8,128)(2,1)S(1)}, u32[]{:S(2)}) copy-start(bf16[288,128]{1,0:T(8,128)(2,1)S(1)} %collective-permute-done.14.refs_3_) | copy-start | bytes 221188
  127.1 2.4 %copy-start.7 = (bf16[288,128]{1,0:T(8,128)(2,1)}, bf16[288,128]{1,0:T(8,128)(2,1)S(1)}, u32[]{:S(2)}) copy-start(bf16[288,128]{1,0:T(8,128)(2,1)S(1)} %collective-permute-done.15.refs_4_) | copy-start | bytes 221188
  128.0 1.6 %copy-start.8 = (bf16[288,128]{1,0:T(8,128)(2,1)}, bf16[288,128]{1,0:T(8,128)(2,1)S(1)}, u32[]{:S(2)}) copy-start(bf16[288,128]{1,0:T(8,128)(2,1)S(1)} %collective-permute-done.16.refs_5_) | copy-start | bytes 221188
  129.6 0.6 copy-start.9
  129.6 0.7 copy-start.10
  132.7 0.8 copy-start.1

commit v4 on v3

--- a/solution.py
+++ b/solution.py
@@ -56,16 +56,26 @@
     )(lists, place)
 
 
-def pack_body(core_ref, wanted_ref, lat_ref, key_ref, out_ref, sems):
-    copies = []
-    slots_ref = [wanted_ref[i, core_ref[0]] for i in range(SEL)]
+def pack_body(core_ref, wanted_ref, lat_ref, key_ref, out_ref, pages, sems, done):
+    reads, writes = [], []
     for i in range(SEL):
-        copies.append(pltpu.make_async_copy(lat_ref.at[slots_ref[i]], out_ref.at[i, :LAT, :], sems.at[2 * i]))
-        copies.append(pltpu.make_async_copy(key_ref.at[slots_ref[i]], out_ref.at[i, LAT:, :], sems.at[2 * i + 1]))
-    for c in copies:
-        c.start()
-    for c in copies:
-        c.wait()
+        slot = wanted_ref[i, core_ref[0]]
+        reads.append(
+            (
+                pltpu.make_async_copy(lat_ref.at[slot], pages.at[i, pl.ds(BLOCK, LAT), :], sems.at[2 * i]),
+                pltpu.make_async_copy(key_ref.at[slot], pages.at[i, pl.ds(0, BLOCK), :], sems.at[2 * i + 1]),
+            )
+        )
+        writes.append(pltpu.make_async_copy(pages.at[i], out_ref.at[i], done.at[i]))
+    for pair in reads:
+        for c in pair:
+            c.start()
+    for pair, w in zip(reads, writes):
+        for c in pair:
+            c.wait()
+        w.start()
+    for w in writes:
+        w.wait()
 
 
 def pack_pages(core, wanted, lat, keys):
@@ -78,8 +88,12 @@
             pl.BlockSpec(memory_space=pl.ANY),
             pl.BlockSpec(memory_space=pl.ANY),
         ],
-        out_specs=pl.BlockSpec(memory_space=pltpu.VMEM),
-        scratch_shapes=[pltpu.SemaphoreType.DMA((2 * SEL,))],
+        out_specs=pl.BlockSpec(memory_space=pl.ANY),
+        scratch_shapes=[
+            pltpu.VMEM((SEL, ROWS, BLOCK), bf16),
+            pltpu.SemaphoreType.DMA((2 * SEL,)),
+            pltpu.SemaphoreType.DMA((SEL,)),
+        ],
         cost_estimate=pl.CostEstimate(flops=0, bytes_accessed=6 << 20, transcendentals=0),
         name="pack_pages",
     )(core, wanted, lat, keys)
@@ -181,6 +195,7 @@
         scratch_shapes=[pltpu.VMEM((2 * QBLK, 8), f32)],
         cost_estimate=pl.CostEstimate(flops=0, bytes_accessed=2 << 20, transcendentals=0),
         name="place",
+        compiler_params=pltpu.CompilerParams(vmem_limit_bytes=8 << 20),
     )(head, *blocks)
 
 
@@ -201,6 +216,7 @@
         out_specs=vmem,
         cost_estimate=pl.CostEstimate(flops=0, bytes_accessed=1 << 20, transcendentals=0),
         name="add_pages",
+        compiler_params=pltpu.CompilerParams(vmem_limit_bytes=4 << 20),
     )(wanted, gk)
 
 
@@ -209,11 +225,11 @@
 
 
 def teacher_body(qa_ref, qb_ref, la_ref, lb_ref, kj_ref, t1_ref, t2_ref, t3_ref, own_ref):
-    keys = jnp.concatenate([kj_ref[p, :LATP, :] for p in range(PT)], axis=1)
+    keys = jnp.concatenate([kj_ref[p, BLOCK:, :] for p in range(PT)], axis=1)
     acc = None
     for q_ref, l_ref in ((qa_ref, la_ref), (qb_ref, lb_ref)):
         for g in range(q_ref.shape[0] // HG):
-            s = dot(q_ref[g * HG : (g + 1) * HG].reshape(HG * QBLK, LATP), keys)
+            s = dot(q_ref[g * HG : (g + 1) * HG, :, :LAT].reshape(HG * QBLK, LAT), keys)
             for k in range(HG):
                 h = g * HG + k
                 part = jnp.exp2(s[k * QBLK : (k + 1) * QBLK] * (softmax_scale * LOG2E) - l_ref[:, h : h + 1])
@@ -235,23 +251,44 @@
             flops=2 * 32 * QBLK * n * BLOCK * LAT, bytes_accessed=12 << 20, transcendentals=32 * QBLK * n * BLOCK
         ),
         name="teacher_terms",
+        compiler_params=pltpu.CompilerParams(vmem_limit_bytes=24 << 20),
     )(qa, qb, la, lb, kj)
 
 
+def spread_body(*refs):
+    *in_refs, iq_ref, iqt_ref, wb_ref = refs
+    for src in range(8):
+        rows = in_refs[src][: 8 * QPART, :]
+        iq_ref[src * 8 * QPART : (src + 1) * 8 * QPART, :] = rows
+        iqt_ref[:, src * 8 * QPART : (src + 1) * 8 * QPART] = rows.T
+        w = in_refs[src][8 * QPART :, :].astype(f32)
+        for i in range(8):
+            col = w[:, i : i + 1] + w[:, 8 + i : 9 + i] + w[:, 16 + i : 17 + i]
+            wb_ref[src * 8 + i] = jnp.broadcast_to(col, (QPART, 128))
+
+
+def spread(blocks):
+    vmem = pl.BlockSpec(memory_space=pltpu.VMEM)
+    return pl.pallas_call(
+        spread_body,
+        out_shape=(
+            jax.ShapeDtypeStruct((IDXH * QPART, IDXD), bf16),
+            jax.ShapeDtypeStruct((IDXD, IDXH * QPART), bf16),
+            jax.ShapeDtypeStruct((IDXH, QPART, 128), f32),
+        ),
+        in_specs=[vmem] * 8,
+        out_specs=(vmem,) * 3,
+        cost_estimate=pl.CostEstimate(flops=0, bytes_accessed=3 << 20, transcendentals=0),
+        name="spread",
+    )(*blocks)
+
+
 PS = 4
 
 
-def score_body(iq_ref, kj_ref, out_ref, wb_ref):
-    @pl.when(pl.program_id(0) == 0)
-    def _():
-        for src in range(8):
-            rows = iq_ref[src, 8 * QPART :, :].astype(f32)
-            for i in range(8):
-                col = rows[:, i : i + 1] + rows[:, 8 + i : 9 + i] + rows[:, 16 + i : 17 + i]
-                wb_ref[src * 8 + i] = jnp.broadcast_to(col, (QPART, 128))
-
-    keys = kj_ref[:, LAT:, :].reshape(-1, IDXD)
-    raw = dot_nt(iq_ref[:, : 8 * QPART, :].reshape(IDXH * QPART, IDXD), keys)
+def score_body(iq_ref, wb_ref, kj_ref, out_ref, raw_ref):
+    raw = dot_nt(iq_ref[...], kj_ref[...].reshape(-1, IDXD))
+    raw_ref[...] = raw.astype(bf16)
     for t in range(PS):
         acc = None
         for e in range(IDXH):
@@ -261,30 +298,30 @@
         out_ref[:, t * 128 : (t + 1) * 128] = acc
 
 
-def scores(iq, kj):
+def scores(iq, wb, kj):
     n = kj.shape[0]
     return pl.pallas_call(
         score_body,
         out_shape=(
             jax.ShapeDtypeStruct((QPART, n * BLOCK), f32),
-            jax.ShapeDtypeStruct((IDXH, QPART, 128), f32),
+            jax.ShapeDtypeStruct((IDXH * QPART, n * BLOCK), bf16),
         ),
         grid=(n // PS,),
-        in_specs=[whole(iq), pl.BlockSpec((PS, ROWS, BLOCK), lambda i: (i, 0, 0))],
+        in_specs=[whole(iq), whole(wb), pl.BlockSpec((PS, BLOCK, IDXD), lambda i: (i, 0, 0))],
         out_specs=(
             pl.BlockSpec((QPART, PS * BLOCK), lambda i: (0, i)),
-            pl.BlockSpec((IDXH, QPART, 128), lambda i: (0, 0, 0)),
-        ),
-        cost_estimate=pl.CostEstimate(flops=2 * IDXH * QPART * n * BLOCK * IDXD, bytes_accessed=6 << 20, transcendentals=0),
+            pl.BlockSpec((IDXH * QPART, PS * BLOCK), lambda i: (0, i)),
+        ),
+        cost_estimate=pl.CostEstimate(flops=2 * IDXH * QPART * n * BLOCK * IDXD, bytes_accessed=12 << 20, transcendentals=0),
         name="scores",
-    )(iq, kj)
+    )(iq, wb, kj)
 
 
 PB = 4
 
 
-def backward_body(own_ref, t1_ref, t2_ref, t3_ref, score_ref, iq_ref, iqt_ref, wb_ref, kj_ref, gk_ref, *refs):
-    *gq_refs, grad_ref, gr_ref, gw_ref, acc_ref = refs
+def backward_body(own_ref, t1_ref, t2_ref, t3_ref, score_ref, iq_ref, iqt_ref, wb_ref, raw_ref, kj_ref, gk_ref, *refs):
+    *gq_refs, grad_ref, gr_ref, acc_ref = refs
     step = pl.program_id(0)
     span = PB * BLOCK
 
@@ -297,19 +334,14 @@
         probs = e / jnp.sum(e, axis=1, keepdims=True)
         grad_ref[...] = loss_scale * (probs - target)
         acc_ref[...] = jnp.zeros_like(acc_ref)
-        gw_ref[...] = jnp.zeros_like(gw_ref)
-
-    keys = kj_ref[:, LAT:, :].reshape(-1, IDXD)
-    raw = dot_nt(iq_ref[:, : 8 * QPART, :].reshape(IDXH * QPART, IDXD), keys)
-    for e in range(IDXH):
-        gsum = gw_ref[e]
-        w = wb_ref[e]
-        for t in range(PB):
-            g = grad_ref[:, pl.ds(pl.multiple_of(step * span + t * 128, 128), 128)]
-            r = raw[e * QPART : (e + 1) * QPART, t * 128 : (t + 1) * 128]
-            gsum = gsum + g * jnp.maximum(r, 0.0)
-            gr_ref[e * QPART : (e + 1) * QPART, t * 128 : (t + 1) * 128] = jnp.where(r > 0.0, g * w, 0.0).astype(bf16)
-        gw_ref[e] = gsum
+
+    keys = kj_ref[...].reshape(-1, IDXD)
+    for t in range(PB):
+        g = grad_ref[:, pl.ds(pl.multiple_of(step * span + t * 128, 128), 128)]
+        at = slice(t * 128, (t + 1) * 128)
+        for e in range(IDXH):
+            rows = slice(e * QPART, (e + 1) * QPART)
+            gr_ref[rows, at] = jnp.where(raw_ref[rows, at] > 0, (g * wb_ref[e]).astype(bf16), 0)
     gr = gr_ref[...]
     gk_ref[...] = dot(iqt_ref[...], gr).T.astype(gk_ref.dtype)
     acc_ref[...] += dot(gr, keys)
@@ -321,7 +353,10 @@
             gq_refs[src][: 8 * QPART, :] = acc_ref[src * 8 * QPART : (src + 1) * 8 * QPART, :].astype(bf16)
             out = jnp.zeros((QPART, 128), f32)
             for i in range(8):
-                rest = jnp.sum(gw_ref[src * 8 + i], axis=1, keepdims=True)
+                e = src * 8 + i
+                rows = slice(e * QPART, (e + 1) * QPART)
+                gw = jnp.sum(iq_ref[rows, :].astype(f32) * acc_ref[rows, :], axis=1, keepdims=True)
+                rest = gw / wb_ref[e]
                 for k in range(3):
                     piece = rest.astype(bf16).astype(f32)
                     out = jnp.where(lane == 8 * k + i, piece, out)
@@ -329,30 +364,29 @@
             gq_refs[src][8 * QPART :, :] = out.astype(bf16)
 
 
-def backward(own, moved, score, iq, iqt, wb, kj):
+def backward(own, moved, score, iq, iqt, wb, raw, kj):
     n = kj.shape[0]
     fixed = (own, *moved, score, iq, iqt, wb)
     return pl.pallas_call(
         backward_body,
-        out_shape=(
-            jax.ShapeDtypeStruct((n * BLOCK, IDXD), bf16),
-        )
+        out_shape=(jax.ShapeDtypeStruct((n * BLOCK, IDXD), bf16),)
         + (jax.ShapeDtypeStruct((9 * QPART, IDXD), bf16),) * 8,
         grid=(n // PB,),
-        in_specs=[whole(a) for a in fixed] + [pl.BlockSpec((PB, ROWS, BLOCK), lambda i: (i, 0, 0))],
-        out_specs=(
-            pl.BlockSpec((PB * BLOCK, IDXD), lambda i: (i, 0)),
-        )
+        in_specs=[whole(a) for a in fixed]
+        + [
+            pl.BlockSpec((IDXH * QPART, PB * BLOCK), lambda i: (0, i)),
+            pl.BlockSpec((PB, BLOCK, IDXD), lambda i: (i, 0, 0)),
+        ],
+        out_specs=(pl.BlockSpec((PB * BLOCK, IDXD), lambda i: (i, 0)),)
         + (pl.BlockSpec((9 * QPART, IDXD), lambda i: (0, 0)),) * 8,
         scratch_shapes=[
             pltpu.VMEM((QPART, n * BLOCK), f32),
             pltpu.VMEM((IDXH * QPART, PB * BLOCK), bf16),
-            pltpu.VMEM((IDXH, QPART, 128), f32),
             pltpu.VMEM((IDXH * QPART, IDXD), f32),
         ],
-        cost_estimate=pl.CostEstimate(flops=6 * IDXH * QPART * n * BLOCK * IDXD, bytes_accessed=8 << 20, transcendentals=0),
+        cost_estimate=pl.CostEstimate(flops=4 * IDXH * QPART * n * BLOCK * IDXD, bytes_accessed=16 << 20, transcendentals=0),
         name="backward",
-    )(*fixed, kj)
+    )(*fixed, raw, kj)
 
 
 def step(queries, lse, latent, index_keys, index_queries, index_weights, block_lists, block_place):
@@ -369,8 +403,7 @@
 
     dealt = [*deal(head.reshape(1), index_queries, index_weights.T)]
     dealt = dealt[:1] + [lax.ppermute(dealt[k], "head", [(h, (h + k) & 7) for h in range(8)]) for k in range(1, 8)]
-    iq = jnp.stack(dealt)
-    iqt = iq[:, : 8 * QPART].reshape(IDXH * QPART, IDXD).T
+    iq, iqt, wb = spread(dealt)
 
     qa, qs, la, ls = flip_queries(jnp.stack([core, quarter]), queries.transpose(1, 2, 0), lse.T)
     qb = lax.ppermute(qs, "head", partner)
@@ -381,9 +414,9 @@
     for d in (2, 1, 3):
         ring = [(2 * x + c, 2 * ((x + d) % 4) + c) for x in range(4) for c in range(2)]
         moved.append(lax.ppermute(parts[d - 1], "head", ring))
-    score, wb = scores(iq, kj)
-
-    gk, *gq = backward(own, moved, score, iq, iqt, wb, kj)
+    score, raw = scores(iq, wb, kj)
+
+    gk, *gq = backward(own, moved, score, iq, iqt, wb, raw, kj)
 
     gk = lax.all_to_all(gk.reshape(128, 16, IDXD), ("seq", "head"), split_axis=0, concat_axis=0, tiled=True)
     gq = gq[:1] + [lax.ppermute(gq[k], "head", [(h, (h - k) & 7) for h in range(8)]) for k in range(1, 8)]

time: 137 us -> 138 us (level)
  starting transfers between devices: 49.1 us -> 51.2 us
    pallas_call x0 -> x1, Pallas kernels: none -> 3.35 us  [spread(): pl.pallas_call(spread_body, out_shape=(jax.ShapeDtypeStruct((IDXH * QPART...]
    ppermute x7, waiting for transfers between devices: 3.05 us -> 0.02 us  [step(): lax.ppermute(dealt[k], 'head', [(h, h + k & 7) for h in range(8)])]
    all_to_all x1, waiting for transfers between devices: 9.55 us -> 11.6 us  [step(): kj = lax.all_to_all(packed, 'seq', split_axis=0, concat_axis=0, tiled=True)]
    pallas_call x1, Pallas kernels: 17.6 us -> 15.9 us  [teacher_terms(): pl.pallas_call(teacher_body, out_shape=[jax.ShapeDtypeStruct((QPART, n *...]
    unnamed x35 -> x24, local copies, waits for them, and re-layouts: 5.26 us -> 6.52 us
  transfers between devices with their start and end apart: 22 -> 22, of which waited for: 10 -> 5; matrix products, arithmetic and copies ran while one was open for 2% -> 0% of each run, Pallas kernels for 26% -> 27%
where the time goes in v4:
time: 138 us; the launch traced here: 136 us
  Pallas kernels  53.7 us (39%)
  starting transfers between devices  51.2 us (37%)
  waiting for transfers between devices  23 us (17%)
  local copies, waits for them, and re-layouts  6.52 us (5%)
    pallas_call x1, Pallas kernels, teacher_terms(): pl.pallas_call(teacher_body, out_shape=[jax.ShapeDtypeStruct((QPART, n *...  15.9 us
    all_to_all x1, waiting for transfers between devices, step(): kj = lax.all_to_all(packed, 'seq', split_axis=0, concat_axis=0, tiled=True)  11.6 us
    all_to_all x1, starting transfers between devices, step(): lax.all_to_all(gk.reshape(128, 16, IDXD), ('seq', 'head'), split_axis=0,...  11.5 us
    pallas_call x1, Pallas kernels, backward(): pl.pallas_call(backward_body, out_shape=(jax.ShapeDtypeStruct((n * BLOCK,...  10.9 us
    ppermute x7, starting transfers between devices, step(): lax.ppermute(dealt[k], 'head', [(h, h + k & 7) for h in range(8)])  9.67 us
    ppermute x7, starting transfers between devices, step(): lax.ppermute(gq[k], 'head', [(h, h - k & 7) for h in range(8)])  9.54 us
    all_to_all x1, starting transfers between devices, step(): lax.all_to_all(wanted, 'seq', split_axis=0, concat_axis=0, tiled=True)  8.6 us
    pallas_call x1, Pallas kernels, scores(): pl.pallas_call(score_body, out_shape=(jax.ShapeDtypeStruct((QPART, n * BL...  6.72 us
  transfers between devices with their start and end apart: 22, of which 5 were waited for; matrix products, arithmetic and copies ran while one was open for 0% of the time, Pallas kernels for 27%

profile of v4, /device:TPU:1, one launch (start us, length us, event | category | flops | bytes accessed | tf_op | source)
XLA Modules:
  0.0 135.8 jit_solution(14833754205296648556)
XLA Ops:
  0.6 1.4 %lookup.1 = s32[16,2]{1,0:T(8,128)} custom-call(s32[2,16]{1,0:T(2,128)} %lists_ref.1, s32[1024]{0:T(1024)} %place_ref.1), custom_call_target="tpu_custom_call" | custom-call | tf_op jit(solution)/shard_map/lookup/pallas_call | solution.py:50
  2.1 8.6 %all-to-all-start = ((s32[16,1,2]{2,1,0:T(1,128)}), s32[16,1,2]{2,1,0:T(1,128)S(1)}, u32[]{:S(2)}, u32[]{:S(2)}) async-start(s32[16,1,2]{2,1,0:T(1,128)} %bitcast.21), calls=%async_computation | async-start | bytes 16384 | tf_op jit(solution)/shard_map/all_to_all | solution.py:399
  10.7 6.4 %all-to-all-done = s32[16,1,2]{2,1,0:T(1,128)S(1)} async-done(((s32[16,1,2]{2,1,0:T(1,128)}), s32[16,1,2]{2,1,0:T(1,128)S(1)}, u32[]{:S(2)}, u32[]{:S(2)}) %all-to-all-start) | async-done | bytes 160 | tf_op jit(solution)/shard_map/all_to_all | solution.py:399
  17.0 0.6 copy-done.2
  17.6 3.8 %pack_pages.1 = bf16[16,704,128]{2,1,0:T(8,128)(2,1)} custom-call(s32[1]{0:T(128)} %bitcast.1.core_ref, s32[16,2]{1,0:T(8,128)} %bitcast.13, bf16[64,576,128]{2,1,0:T(8,128)(2,1)} %bitcast.17, bf16[64,128,128]{2,1,0:T(8,128)(2,1)} %key_ref.1), custom_call_target="tpu_custom_call" | custom-call | bytes 6291456 | tf_op jit(solution)/shard_map/pack_pages/pallas_call | solution.py:82
  21.4 3.7 %all-to-all-start.1 = ((bf16[16,704,128]{2,1,0:T(8,128)(2,1)}), bf16[16,704,128]{2,1,0:T(8,128)(2,1)S(1)}, u32[]{:S(2)}, u32[]{:S(2)}) async-start(bf16[16,704,128]{2,1,0:T(8,128)(2,1)} %pack_pages.1), calls=%async_computation.1 | async-start | bytes 5767168 | tf_op jit(solution)/shard_map/all_to_all | solution.py:402
  25.2 0.6 pad_add_fusion.place_ref
  25.8 6.6 %flip_queries.1 = (bf16[16,128,640]{2,1,0:T(8,128)(2,1)}, bf16[16,128,640]{2,1,0:T(8,128)(2,1)}, f32[128,128]{1,0:T(8,128)}, f32[128,128]{1,0:T(8,128)}) custom-call(s32[2]{0:T(128)} %pad_add_fusion.place_ref, bf16[16,576,256]{2,1,0:T(8,128)(2,1)} %bitcast.15, bf16[16,576,256]{2,1,0:T(8,128)(2,1)} %bitcast.16, f32[16,256]{1,0:T(8,128)} %bitcast.19, ...), custom_call_target="tpu_custom_call" | custom-call | bytes 25165824 | tf_op jit(solution)/shard_map/flip_queries/pallas_call | solution.py:129
  32.4 2.7 %collective-permute-start = (bf16[16,128,640]{2,1,0:T(8,128)(2,1)}, bf16[16,128,640]{2,1,0:T(8,128)(2,1)}, u32[]{:S(2)}, u32[]{:S(2)}) collective-permute-start(bf16[16,128,640]{2,1,0:T(8,128)(2,1)} %get-tuple-element.36), channel_id=1, source_target_pairs={{0,1},{1,0},{2,3},{3,2},{4,5},{5,4},{6,7},{7,6},{8,9},{9,8},{10,11... | collective-permute-start | bytes 7864328 | tf_op jit(solution)/shard_map/ppermute | solution.py:409
  35.1 2.1 %deal.1 = (bf16[288,128]{1,0:T(8,128)(2,1)}, bf16[288,128]{1,0:T(8,128)(2,1)}, bf16[288,128]{1,0:T(8,128)(2,1)}, bf16[288,128]{1,0:T(8,128)(2,1)}, bf16[288,128]...) custom-call(s32[1]{0:T(128)} %bitcast.head_ref, ...), custom_call_target="tpu_custom_call" | custom-call | bytes 2097152 | tf_op jit(solution)/shard_map/deal/pallas_call | solution.py:166
  37.2 1.1 collective-permute-start.5
  38.4 1.2 collective-permute-start.6
  39.6 2.0 %collective-permute-start.7 = (bf16[288,128]{1,0:T(8,128)(2,1)}, bf16[288,128]{1,0:T(8,128)(2,1)}, u32[]{:S(2)}, u32[]{:S(2)}) collective-permute-start(bf16[288,128]{1,0:T(8,128)(2,1)} %get-tuple-element.46), channel_id=1, source_target_pairs={{0,3},{1,4},{2,5},{3,6},{4,7},{5,0},{6,1},{7,2},{8,11},{9,12},{10,... | collective-permute-start | bytes 221192 | tf_op jit(solution)/shard_map/ppermute | solution.py:405
  41.6 1.4 collective-permute-start.8
  42.9 0.0 collective-permute-done.5.refs_1_
  42.9 1.7 %collective-permute-start.9 = (bf16[288,128]{1,0:T(8,128)(2,1)}, bf16[288,128]{1,0:T(8,128)(2,1)}, u32[]{:S(2)}, u32[]{:S(2)}) collective-permute-start(bf16[288,128]{1,0:T(8,128)(2,1)} %get-tuple-element.48), channel_id=1, source_target_pairs={{0,5},{1,6},{2,7},{3,0},{4,1},{5,2},{6,3},{7,4},{8,13},{9,14},{10,... | collective-permute-start | bytes 221192 | tf_op jit(solution)/shard_map/ppermute | solution.py:405
  44.7 0.0 collective-permute-done.6.refs_2_
  44.7 0.0 collective-permute-done.qb_ref
  44.7 2.2 %collective-permute-start.11 = (bf16[288,128]{1,0:T(8,128)(2,1)}, bf16[288,128]{1,0:T(8,128)(2,1)}, u32[]{:S(2)}, u32[]{:S(2)}) collective-permute-start(bf16[288,128]{1,0:T(8,128)(2,1)} %get-tuple-element.50), channel_id=1, source_target_pairs={{0,7},{1,0},{2,1},{3,2},{4,3},{5,4},{6,5},{7,6},{8,15},{9,8},{10,9... | collective-permute-start | bytes 221192 | tf_op jit(solution)/shard_map/ppermute | solution.py:405
  46.9 11.6 %all-to-all-done.1.kj_ref = bf16[16,704,128]{2,1,0:T(8,128)(2,1)S(1)} async-done(((bf16[16,704,128]{2,1,0:T(8,128)(2,1)}), bf16[16,704,128]{2,1,0:T(8,128)(2,1)S(1)}, u32[]{:S(2)}, u32[]{:S(2)}) %all-to-all-start.1) | async-done | bytes 2883616 | tf_op jit(solution)/shard_map/all_to_all | solution.py:402
  58.5 2.8 %copy-done.5 = bf16[16,128,640]{2,1,0:T(8,128)(2,1)S(1)} copy-done((bf16[16,128,640]{2,1,0:T(8,128)(2,1)S(1)}, bf16[16,128,640]{2,1,0:T(8,128)(2,1)}, u32[]{:S(2)}) %copy-start.5) | copy-done | bytes 2621464
  61.3 0.8 copy-done.6
  62.1 15.9 %teacher_terms.1 = (bf16[32,2048]{1,0:T(8,128)(2,1)S(1)}, bf16[32,2048]{1,0:T(8,128)(2,1)S(1)}, bf16[32,2048]{1,0:T(8,128)(2,1)S(1)}, f32[32,2048]{1,0:T(8,128)S(1)}) custom-call(bf16[16,128,640]{2,1,0:T(8,128)(2,1)S(1)} %copy-done.5, bf16[16,128,640]{2,1,0:T(8,128)(2,1)} %collective-permute-done.qb_ref, f32[128,128]{1,0:T(8,128)S(1)} %copy-done.6, ...), custom_call_target="tpu_custom_call" | custom-call | flops 9663676416 | bytes 12582912 | tf_op jit(solution)/shard_map/teacher_terms/pallas_call | solution.py:244
  78.1 0.7 copy-done.1
  78.8 0.0 collective-permute-done.7.refs_3_
  78.8 2.7 %collective-permute-start.2 = (bf16[32,2048]{1,0:T(8,128)(2,1)S(1)}, bf16[32,2048]{1,0:T(8,128)(2,1)S(1)}, u32[]{:S(2)}, u32[]{:S(2)}) collective-permute-start(bf16[32,2048]{1,0:T(8,128)(2,1)S(1)} %get-tuple-element.40), channel_id=1, source_target_pairs={{0,4},{1,5},{2,6},{3,7},{4,0},{5,1},{6,2},{7,3},{8,12},{9,13},{10,... | collective-permute-start | bytes 393224 | tf_op jit(solution)/shard_map/ppermute | solution.py:416
  81.6 0.3 collective-permute-start.3
  81.9 2.4 %collective-permute-start.4 = (bf16[32,2048]{1,0:T(8,128)(2,1)S(1)}, bf16[32,2048]{1,0:T(8,128)(2,1)S(1)}, u32[]{:S(2)}, u32[]{:S(2)}) collective-permute-start(bf16[32,2048]{1,0:T(8,128)(2,1)S(1)} %get-tuple-element.42), channel_id=1, source_target_pairs={{0,6},{1,7},{2,0},{3,1},{4,2},{5,3},{6,4},{7,5},{8,14},{9,15},{10,... | collective-permute-start | bytes 393224 | tf_op jit(solution)/shard_map/ppermute | solution.py:416
  84.2 3.3 %spread.1 = (bf16[2048,128]{1,0:T(8,128)(2,1)}, bf16[128,2048]{1,0:T(8,128)(2,1)}, f32[64,32,128]{2,1,0:T(8,128)}) custom-call(bf16[288,128]{1,0:T(8,128)(2,1)} %get-tuple-element.43.refs_0_, bf16[288,128]{1,0:T(8,128)(2,1)} %copy-done.10, bf16[288,128]{1,0:T(8,128)(2,1)} %copy-done.11, bf16[288,128]{1,0:T(8,128)(2,1)} %collective-permute-done.7.refs_3_, ...), custom_call_target="tpu_custom_call" | custom-call | bytes 3145728 | tf_op jit(solution)/shard_map/spread/pallas_call | solution.py:272
  87.6 6.7 %scores.1 = (f32[32,2048]{1,0:T(8,128)}, bf16[2048,2048]{1,0:T(8,128)(2,1)}) custom-call(bf16[2048,128]{1,0:T(8,128)(2,1)} %get-tuple-element.51.iq_ref, f32[64,32,128]{2,1,0:T(8,128)} %get-tuple-element.52.wb_ref, bf16[16,704,128]{2,1,0:T(8,128)(2,1)} %copy-done), custom_call_target="tpu_custom_call" | custom-call | flops 1073741824 | bytes 12582912 | tf_op jit(solution)/shard_map/scores/pallas_call | solution.py:303
  94.4 0.6 copy-done.7
  95.0 0.1 copy-done.8
  95.0 0.1 copy-done.9
  95.1 10.9 %backward.1 = (bf16[2048,128]{1,0:T(8,128)(2,1)}, bf16[288,128]{1,0:T(8,128)(2,1)}, bf16[288,128]{1,0:T(8,128)(2,1)}, bf16[288,128]{1,0:T(8,128)(2,1)}, bf16[288...) custom-call(f32[32,2048]{1,0:T(8,128)} %copy-done.1, ...), custom_call_target="tpu_custom_call" | custom-call | flops 2147483648 | bytes 16777216 | tf_op jit(solution)/shard_map/backward/pallas_call | solution.py:370
  105.9 11.5 %all-to-all-start.2 = ((bf16[128,16,128]{2,1,0:T(8,128)(2,1)}), bf16[128,16,128]{2,1,0:T(8,128)(2,1)S(1)}, u32[]{:S(2)}, u32[]{:S(2)}) async-start(bf16[128,16,128]{2,1,0:T(8,128)(2,1)} %bitcast.18), calls=%async_computation.2 | async-start | bytes 1048576 | tf_op jit(solution)/shard_map/all_to_all | solution.py:421
  117.4 1.1 collective-permute-start.12
  118.5 1.9 %collective-permute-start.13 = (bf16[288,128]{1,0:T(8,128)(2,1)}, bf16[288,128]{1,0:T(8,128)(2,1)S(1)}, u32[]{:S(2)}, u32[]{:S(2)}) collective-permute-start(bf16[288,128]{1,0:T(8,128)(2,1)} %get-tuple-element.58), channel_id=1, source_target_pairs={{0,6},{1,7},{2,0},{3,1},{4,2},{5,3},{6,4},{7,5},{8,14},{9,15},{10,... | collective-permute-start | bytes 221192 | tf_op jit(solution)/shard_map/ppermute | solution.py:422
  120.4 1.0 collective-permute-start.14
  121.4 2.4 %collective-permute-start.15 = (bf16[288,128]{1,0:T(8,128)(2,1)}, bf16[288,128]{1,0:T(8,128)(2,1)S(1)}, u32[]{:S(2)}, u32[]{:S(2)}) collective-permute-start(bf16[288,128]{1,0:T(8,128)(2,1)} %get-tuple-element.60), channel_id=1, source_target_pairs={{0,4},{1,5},{2,6},{3,7},{4,0},{5,1},{6,2},{7,3},{8,12},{9,13},{10,... | collective-permute-start | bytes 221192 | tf_op jit(solution)/shard_map/ppermute | solution.py:422
  123.8 0.7 collective-permute-start.16
  124.5 2.6 %collective-permute-done.12.refs_1_ = bf16[288,128]{1,0:T(8,128)(2,1)S(1)} collective-permute-done((bf16[288,128]{1,0:T(8,128)(2,1)}, bf16[288,128]{1,0:T(8,128)(2,1)S(1)}, u32[]{:S(2)}, u32[]{:S(2)}) %collective-permute-start.12) | collective-permute-done | bytes 73760 | tf_op jit(solution)/shard_map/ppermute | solution.py:422
  127.1 1.2 collective-permute-start.17
  128.3 1.3 collective-permute-start.18
  129.6 0.8 collective-permute-done.16.refs_5_
  130.4 1.6 %collective-permute-done.17.refs_6_ = bf16[288,128]{1,0:T(8,128)(2,1)S(1)} collective-permute-done((bf16[288,128]{1,0:T(8,128)(2,1)}, bf16[288,128]{1,0:T(8,128)(2,1)S(1)}, u32[]{:S(2)}, u32[]{:S(2)}) %collective-permute-start.17) | collective-permute-done | bytes 73760 | tf_op jit(solution)/shard_map/ppermute | solution.py:422
  132.0 0.9 copy-done.4
  132.9 1.3 place.1
  134.2 1.6 %add_pages.1 = f32[64,16,128]{2,1,0:T(8,128)} custom-call(s32[16,2]{1,0:T(8,128)S(1)} %bitcast.14, bf16[128,16,128]{2,1,0:T(8,128)(2,1)S(1)} %all-to-all-done.2.gk_ref), custom_call_target="tpu_custom_call" | custom-call | bytes 1048576 | tf_op jit(solution)/shard_map/add_pages/pallas_call | solution.py:212
  (31 shorter events, 0.1 us)
Async XLA Ops:
  2.1 15.0 %all-to-all-start = ((s32[16,1,2]{2,1,0:T(1,128)}), s32[16,1,2]{2,1,0:T(1,128)S(1)}, u32[]{:S(2)}, u32[]{:S(2)}) async-start(s32[16,1,2]{2,1,0:T(1,128)} %bitcast.21), calls=%async_computation | async-start | bytes 16384 | tf_op jit(solution)/shard_map/all_to_all | solution.py:399
  17.0 0.6 copy-start.2
  21.4 37.1 %all-to-all-start.1 = ((bf16[16,704,128]{2,1,0:T(8,128)(2,1)}), bf16[16,704,128]{2,1,0:T(8,128)(2,1)S(1)}, u32[]{:S(2)}, u32[]{:S(2)}) async-start(bf16[16,704,128]{2,1,0:T(8,128)(2,1)} %pack_pages.1), calls=%async_computation.1 | async-start | bytes 5767168 | tf_op jit(solution)/shard_map/all_to_all | solution.py:402
  32.4 12.3 %collective-permute-start = (bf16[16,128,640]{2,1,0:T(8,128)(2,1)}, bf16[16,128,640]{2,1,0:T(8,128)(2,1)}, u32[]{:S(2)}, u32[]{:S(2)}) collective-permute-start(bf16[16,128,640]{2,1,0:T(8,128)(2,1)} %get-tuple-element.36), channel_id=1, source_target_pairs={{0,1},{1,0},{2,3},{3,2},{4,5},{5,4},{6,7},{7,6},{8,9},{9,8},{10,11... | collective-permute-start | bytes 7864328 | tf_op jit(solution)/shard_map/ppermute | solution.py:409
  37.2 5.7 %collective-permute-start.5 = (bf16[288,128]{1,0:T(8,128)(2,1)}, bf16[288,128]{1,0:T(8,128)(2,1)S(1)}, u32[]{:S(2)}, u32[]{:S(2)}) collective-permute-start(bf16[288,128]{1,0:T(8,128)(2,1)} %get-tuple-element.44), channel_id=1, source_target_pairs={{0,1},{1,2},{2,3},{3,4},{4,5},{5,6},{6,7},{7,0},{8,9},{9,10},{10,1... | collective-permute-start | bytes 221192 | tf_op jit(solution)/shard_map/ppermute | solution.py:405
  38.4 6.3 %collective-permute-start.6 = (bf16[288,128]{1,0:T(8,128)(2,1)}, bf16[288,128]{1,0:T(8,128)(2,1)S(1)}, u32[]{:S(2)}, u32[]{:S(2)}) collective-permute-start(bf16[288,128]{1,0:T(8,128)(2,1)} %get-tuple-element.45), channel_id=1, source_target_pairs={{0,2},{1,3},{2,4},{3,5},{4,6},{5,7},{6,0},{7,1},{8,10},{9,11},{10,... | collective-permute-start | bytes 221192 | tf_op jit(solution)/shard_map/ppermute | solution.py:405
  39.6 2.0 %collective-permute-start.1 = (f32[128,128]{1,0:T(8,128)}, f32[128,128]{1,0:T(8,128)S(1)}, u32[]{:S(2)}, u32[]{:S(2)}) collective-permute-start(f32[128,128]{1,0:T(8,128)} %get-tuple-element.38), channel_id=1, source_target_pairs={{0,1},{1,0},{2,3},{3,2},{4,5},{5,4},{6,7},{7,6},{8,9},{9,8},{10,11... | collective-permute-start | bytes 196616 | tf_op jit(solution)/shard_map/ppermute | solution.py:410
  39.6 39.2 %collective-permute-start.7 = (bf16[288,128]{1,0:T(8,128)(2,1)}, bf16[288,128]{1,0:T(8,128)(2,1)}, u32[]{:S(2)}, u32[]{:S(2)}) collective-permute-start(bf16[288,128]{1,0:T(8,128)(2,1)} %get-tuple-element.46), channel_id=1, source_target_pairs={{0,3},{1,4},{2,5},{3,6},{4,7},{5,0},{6,1},{7,2},{8,11},{9,12},{10,... | collective-permute-start | bytes 221192 | tf_op jit(solution)/shard_map/ppermute | solution.py:405
  41.6 40.0 %collective-permute-start.8 = (bf16[288,128]{1,0:T(8,128)(2,1)}, bf16[288,128]{1,0:T(8,128)(2,1)}, u32[]{:S(2)}, u32[]{:S(2)}) collective-permute-start(bf16[288,128]{1,0:T(8,128)(2,1)} %get-tuple-element.47), channel_id=1, source_target_pairs={{0,4},{1,5},{2,6},{3,7},{4,0},{5,1},{6,2},{7,3},{8,12},{9,13},{10,... | collective-permute-start | bytes 221192 | tf_op jit(solution)/shard_map/ppermute | solution.py:405
  42.9 35.1 %copy-start.10 = (bf16[288,128]{1,0:T(8,128)(2,1)}, bf16[288,128]{1,0:T(8,128)(2,1)S(1)}, u32[]{:S(2)}) copy-start(bf16[288,128]{1,0:T(8,128)(2,1)S(1)} %collective-permute-done.5.refs_1_) | copy-start | bytes 221188
  42.9 38.9 %collective-permute-start.9 = (bf16[288,128]{1,0:T(8,128)(2,1)}, bf16[288,128]{1,0:T(8,128)(2,1)}, u32[]{:S(2)}, u32[]{:S(2)}) collective-permute-start(bf16[288,128]{1,0:T(8,128)(2,1)} %get-tuple-element.48), channel_id=1, source_target_pairs={{0,5},{1,6},{2,7},{3,0},{4,1},{5,2},{6,3},{7,4},{8,13},{9,14},{10,... | collective-permute-start | bytes 221192 | tf_op jit(solution)/shard_map/ppermute | solution.py:405
  44.7 33.4 %copy-start.11 = (bf16[288,128]{1,0:T(8,128)(2,1)}, bf16[288,128]{1,0:T(8,128)(2,1)S(1)}, u32[]{:S(2)}) copy-start(bf16[288,128]{1,0:T(8,128)(2,1)S(1)} %collective-permute-done.6.refs_2_) | copy-start | bytes 221188
  44.7 39.6 %collective-permute-start.10 = (bf16[288,128]{1,0:T(8,128)(2,1)}, bf16[288,128]{1,0:T(8,128)(2,1)}, u32[]{:S(2)}, u32[]{:S(2)}) collective-permute-start(bf16[288,128]{1,0:T(8,128)(2,1)} %get-tuple-element.49), channel_id=1, source_target_pairs={{0,6},{1,7},{2,0},{3,1},{4,2},{5,3},{6,4},{7,5},{8,14},{9,15},{10,... | collective-permute-start | bytes 221192 | tf_op jit(solution)/shard_map/ppermute | solution.py:405
  44.7 39.5 %collective-permute-start.11 = (bf16[288,128]{1,0:T(8,128)(2,1)}, bf16[288,128]{1,0:T(8,128)(2,1)}, u32[]{:S(2)}, u32[]{:S(2)}) collective-permute-start(bf16[288,128]{1,0:T(8,128)(2,1)} %get-tuple-element.50), channel_id=1, source_target_pairs={{0,7},{1,0},{2,1},{3,2},{4,3},{5,4},{6,5},{7,6},{8,15},{9,8},{10,9... | collective-permute-start | bytes 221192 | tf_op jit(solution)/shard_map/ppermute | solution.py:405
  58.5 19.6 %copy-start = (bf16[16,704,128]{2,1,0:T(8,128)(2,1)}, bf16[16,704,128]{2,1,0:T(8,128)(2,1)S(1)}, u32[]{:S(2)}) copy-start(bf16[16,704,128]{2,1,0:T(8,128)(2,1)S(1)} %all-to-all-done.1.kj_ref) | copy-start | bytes 8650756
  58.5 2.8 %copy-start.5 = (bf16[16,128,640]{2,1,0:T(8,128)(2,1)S(1)}, bf16[16,128,640]{2,1,0:T(8,128)(2,1)}, u32[]{:S(2)}) copy-start(bf16[16,128,640]{2,1,0:T(8,128)(2,1)} %get-tuple-element.35.qa_ref) | copy-start | bytes 7864324
  61.3 0.8 copy-start.6
  78.1 0.7 copy-start.1
  78.8 15.5 %collective-permute-start.2 = (bf16[32,2048]{1,0:T(8,128)(2,1)S(1)}, bf16[32,2048]{1,0:T(8,128)(2,1)S(1)}, u32[]{:S(2)}, u32[]{:S(2)}) collective-permute-start(bf16[32,2048]{1,0:T(8,128)(2,1)S(1)} %get-tuple-element.40), channel_id=1, source_target_pairs={{0,4},{1,5},{2,6},{3,7},{4,0},{5,1},{6,2},{7,3},{8,12},{9,13},{10,... | collective-permute-start | bytes 393224 | tf_op jit(solution)/shard_map/ppermute | solution.py:416
  81.6 12.8 %collective-permute-start.3 = (bf16[32,2048]{1,0:T(8,128)(2,1)S(1)}, bf16[32,2048]{1,0:T(8,128)(2,1)S(1)}, u32[]{:S(2)}, u32[]{:S(2)}) collective-permute-start(bf16[32,2048]{1,0:T(8,128)(2,1)S(1)} %get-tuple-element.41), channel_id=1, source_target_pairs={{0,2},{1,3},{2,4},{3,5},{4,6},{5,7},{6,0},{7,1},{8,10},{9,11},{10,... | collective-permute-start | bytes 393224 | tf_op jit(solution)/shard_map/ppermute | solution.py:416
  81.9 12.5 %collective-permute-start.4 = (bf16[32,2048]{1,0:T(8,128)(2,1)S(1)}, bf16[32,2048]{1,0:T(8,128)(2,1)S(1)}, u32[]{:S(2)}, u32[]{:S(2)}) collective-permute-start(bf16[32,2048]{1,0:T(8,128)(2,1)S(1)} %get-tuple-element.42), channel_id=1, source_target_pairs={{0,6},{1,7},{2,0},{3,1},{4,2},{5,3},{6,4},{7,5},{8,14},{9,15},{10,... | collective-permute-start | bytes 393224 | tf_op jit(solution)/shard_map/ppermute | solution.py:416
  94.3 0.6 copy-start.7
  94.3 0.7 copy-start.8
  94.4 0.7 copy-start.9
  95.1 39.1 %copy-start.3 = (s32[16,1,2]{2,1,0:T(1,128)S(1)}, s32[16,1,2]{2,1,0:T(1,128)}, u32[]{:S(2)}) copy-start(s32[16,1,2]{2,1,0:T(1,128)} %copy-done.2) | copy-start | bytes 388
  105.9 28.3 %all-to-all-start.2 = ((bf16[128,16,128]{2,1,0:T(8,128)(2,1)}), bf16[128,16,128]{2,1,0:T(8,128)(2,1)S(1)}, u32[]{:S(2)}, u32[]{:S(2)}) async-start(bf16[128,16,128]{2,1,0:T(8,128)(2,1)} %bitcast.18), calls=%async_computation.2 | async-start | bytes 1048576 | tf_op jit(solution)/shard_map/all_to_all | solution.py:421
  117.4 9.7 %collective-permute-start.12 = (bf16[288,128]{1,0:T(8,128)(2,1)}, bf16[288,128]{1,0:T(8,128)(2,1)S(1)}, u32[]{:S(2)}, u32[]{:S(2)}) collective-permute-start(bf16[288,128]{1,0:T(8,128)(2,1)} %get-tuple-element.57), channel_id=1, source_target_pairs={{0,7},{1,0},{2,1},{3,2},{4,3},{5,4},{6,5},{7,6},{8,15},{9,8},{10,9... | collective-permute-start | bytes 221192 | tf_op jit(solution)/shard_map/ppermute | solution.py:422
  118.5 9.8 %collective-permute-start.13 = (bf16[288,128]{1,0:T(8,128)(2,1)}, bf16[288,128]{1,0:T(8,128)(2,1)S(1)}, u32[]{:S(2)}, u32[]{:S(2)}) collective-permute-start(bf16[288,128]{1,0:T(8,128)(2,1)} %get-tuple-element.58), channel_id=1, source_target_pairs={{0,6},{1,7},{2,0},{3,1},{4,2},{5,3},{6,4},{7,5},{8,14},{9,15},{10,... | collective-permute-start | bytes 221192 | tf_op jit(solution)/shard_map/ppermute | solution.py:422
  120.4 9.2 %collective-permute-start.14 = (bf16[288,128]{1,0:T(8,128)(2,1)}, bf16[288,128]{1,0:T(8,128)(2,1)S(1)}, u32[]{:S(2)}, u32[]{:S(2)}) collective-permute-start(bf16[288,128]{1,0:T(8,128)(2,1)} %get-tuple-element.59), channel_id=1, source_target_pairs={{0,5},{1,6},{2,7},{3,0},{4,1},{5,2},{6,3},{7,4},{8,13},{9,14},{10,... | collective-permute-start | bytes 221192 | tf_op jit(solution)/shard_map/ppermute | solution.py:422
  121.4 8.2 %collective-permute-start.15 = (bf16[288,128]{1,0:T(8,128)(2,1)}, bf16[288,128]{1,0:T(8,128)(2,1)S(1)}, u32[]{:S(2)}, u32[]{:S(2)}) collective-permute-start(bf16[288,128]{1,0:T(8,128)(2,1)} %get-tuple-element.60), channel_id=1, source_target_pairs={{0,4},{1,5},{2,6},{3,7},{4,0},{5,1},{6,2},{7,3},{8,12},{9,13},{10,... | collective-permute-start | bytes 221192 | tf_op jit(solution)/shard_map/ppermute | solution.py:422
  123.8 6.6 %collective-permute-start.16 = (bf16[288,128]{1,0:T(8,128)(2,1)}, bf16[288,128]{1,0:T(8,128)(2,1)S(1)}, u32[]{:S(2)}, u32[]{:S(2)}) collective-permute-start(bf16[288,128]{1,0:T(8,128)(2,1)} %get-tuple-element.61), channel_id=1, source_target_pairs={{0,3},{1,4},{2,5},{3,6},{4,7},{5,0},{6,1},{7,2},{8,11},{9,12},{10,... | collective-permute-start | bytes 221192 | tf_op jit(solution)/shard_map/ppermute | solution.py:422
  127.1 4.9 %collective-permute-start.17 = (bf16[288,128]{1,0:T(8,128)(2,1)}, bf16[288,128]{1,0:T(8,128)(2,1)S(1)}, u32[]{:S(2)}, u32[]{:S(2)}) collective-permute-start(bf16[288,128]{1,0:T(8,128)(2,1)} %get-tuple-element.62), channel_id=1, source_target_pairs={{0,2},{1,3},{2,4},{3,5},{4,6},{5,7},{6,0},{7,1},{8,10},{9,11},{10,... | collective-permute-start | bytes 221192 | tf_op jit(solution)/shard_map/ppermute | solution.py:422
  128.3 3.7 %collective-permute-start.18 = (bf16[288,128]{1,0:T(8,128)(2,1)}, bf16[288,128]{1,0:T(8,128)(2,1)S(1)}, u32[]{:S(2)}, u32[]{:S(2)}) collective-permute-start(bf16[288,128]{1,0:T(8,128)(2,1)} %get-tuple-element.63), channel_id=1, source_target_pairs={{0,1},{1,2},{2,3},{3,4},{4,5},{5,6},{6,7},{7,0},{8,9},{9,10},{10,1... | collective-permute-start | bytes 221192 | tf_op jit(solution)/shard_map/ppermute | solution.py:422
  132.0 0.9 copy-start.4

commit v5 on v4

--- a/solution.py
+++ b/solution.py
@@ -165,38 +165,38 @@
     vmem = pl.BlockSpec(memory_space=pltpu.VMEM)
     return pl.pallas_call(
         deal_body,
-        out_shape=[jax.ShapeDtypeStruct((9 * QPART, IDXD), bf16)] * 8,
+        out_shape=[jax.ShapeDtypeStruct((9 * QPART, IDXD), bf16)] + [pltpu.HBM((9 * QPART, IDXD), bf16)] * 7,
         in_specs=[pl.BlockSpec(memory_space=pltpu.SMEM), vmem, vmem],
         out_specs=[vmem] * 8,
         scratch_shapes=[pltpu.VMEM((2 * QBLK, 8), f32)],
         cost_estimate=pl.CostEstimate(flops=0, bytes_accessed=2 << 20, transcendentals=0),
         name="deal",
+        compiler_params=pltpu.CompilerParams(vmem_limit_bytes=4 << 20),
     )(head, iq, wt)
 
 
-def place_body(head_ref, *refs):
+def place_body(head_ref, iq_ref, w_ref, *refs):
     *in_refs, gq_ref, gw_ref, wt_ref = refs
     for k in range(8):
         q0 = first_query((head_ref[0] + k) & 7)
-        rows = in_refs[k][: 8 * QPART, :].astype(f32).reshape(8, QPART, IDXD)
-        gq_ref[pl.ds(q0, QPART)] = pltpu.einshape("eqd->qed", rows)
-        w = in_refs[k][8 * QPART :, :].astype(f32)
-        wt_ref[pl.ds(q0, QPART), :] = w[:, :8] + w[:, 8:16] + w[:, 16:24]
-    gw_ref[...] = wt_ref[...].T
-
-
-def place(head, blocks):
+        rows = pltpu.einshape("eqd->qed", in_refs[k][...].astype(f32).reshape(8, QPART, IDXD))
+        gq_ref[pl.ds(q0, QPART)] = rows
+        wt_ref[pl.ds(q0, QPART), :] = jnp.sum(rows * iq_ref[pl.ds(q0, QPART)].astype(f32), axis=2)
+    gw_ref[...] = wt_ref[...].T / w_ref[...]
+
+
+def place(head, iq, wt, blocks):
     vmem = pl.BlockSpec(memory_space=pltpu.VMEM)
     return pl.pallas_call(
         place_body,
         out_shape=(jax.ShapeDtypeStruct((2 * QBLK, 8, IDXD), f32), jax.ShapeDtypeStruct((8, 2 * QBLK), f32)),
-        in_specs=[pl.BlockSpec(memory_space=pltpu.SMEM)] + [vmem] * 8,
+        in_specs=[pl.BlockSpec(memory_space=pltpu.SMEM)] + [vmem] * 10,
         out_specs=(vmem, vmem),
         scratch_shapes=[pltpu.VMEM((2 * QBLK, 8), f32)],
         cost_estimate=pl.CostEstimate(flops=0, bytes_accessed=2 << 20, transcendentals=0),
         name="place",
         compiler_params=pltpu.CompilerParams(vmem_limit_bytes=8 << 20),
-    )(head, *blocks)
+    )(head, iq, wt, *blocks)
 
 
 def add_pages_body(wanted_ref, gk_ref, out_ref):
@@ -221,38 +221,59 @@
 
 
 HG = 8
-PT = 4
-
-
-def teacher_body(qa_ref, qb_ref, la_ref, lb_ref, kj_ref, t1_ref, t2_ref, t3_ref, own_ref):
-    keys = jnp.concatenate([kj_ref[p, BLOCK:, :] for p in range(PT)], axis=1)
-    acc = None
-    for q_ref, l_ref in ((qa_ref, la_ref), (qb_ref, lb_ref)):
-        for g in range(q_ref.shape[0] // HG):
+PT = 8
+
+
+def teacher_body(qa_ref, qb_ref, la_ref, lb_ref, kj_ref, t1_ref, t2_ref, t3_ref, own_ref, q_ref, l_ref, sems):
+    half = qa_ref.shape[0]
+    copies = []
+    lses = [pltpu.make_async_copy(src, l_ref.at[k], sems.at[4 + k]) for k, src in enumerate((la_ref, lb_ref))]
+    for c in lses:
+        c.start()
+    for g in range(2 * half // HG):
+        src = (qa_ref, qb_ref)[g * HG // half].at[pl.ds(g * HG % half, HG)]
+        copies.append(pltpu.make_async_copy(src, q_ref.at[pl.ds(g * HG, HG)], sems.at[g]))
+    for c in copies:
+        c.start()
+    for c in lses:
+        c.wait()
+    for i in range(SEL // PT):
+        keys = jnp.concatenate([kj_ref[i * PT + p, BLOCK:, :] for p in range(PT)], axis=1)
+        acc = None
+        for g, c in enumerate(copies):
+            if i == 0:
+                c.wait()
             s = dot(q_ref[g * HG : (g + 1) * HG, :, :LAT].reshape(HG * QBLK, LAT), keys)
             for k in range(HG):
-                h = g * HG + k
-                part = jnp.exp2(s[k * QBLK : (k + 1) * QBLK] * (softmax_scale * LOG2E) - l_ref[:, h : h + 1])
+                side, h = g * HG // half, g * HG % half + k
+                part = jnp.exp2(s[k * QBLK : (k + 1) * QBLK] * (softmax_scale * LOG2E) - l_ref[side, :, h : h + 1])
                 acc = part if acc is None else acc + part
-    for k, ref in enumerate((t1_ref, t2_ref, t3_ref, own_ref)):
-        ref[...] = acc[k * QPART : (k + 1) * QPART].astype(ref.dtype)
+        at = slice(i * PT * BLOCK, (i + 1) * PT * BLOCK)
+        for k, ref in enumerate((t1_ref, t2_ref, t3_ref, own_ref)):
+            ref[:, at] = acc[k * QPART : (k + 1) * QPART].astype(ref.dtype)
 
 
 def teacher_terms(qa, qb, la, lb, kj):
     n = kj.shape[0]
-    spec = pl.BlockSpec((QPART, PT * BLOCK), lambda i: (0, i))
+    vmem = pl.BlockSpec(memory_space=pltpu.VMEM)
+    hbm = pl.BlockSpec(memory_space=pltpu.HBM)
+    heads = 2 * qa.shape[0]
     return pl.pallas_call(
         teacher_body,
         out_shape=[jax.ShapeDtypeStruct((QPART, n * BLOCK), t) for t in (bf16, bf16, bf16, f32)],
-        grid=(n // PT,),
-        in_specs=[whole(qa), whole(qb), whole(la), whole(lb), pl.BlockSpec((PT, ROWS, BLOCK), lambda i: (i, 0, 0))],
-        out_specs=[spec] * 4,
+        in_specs=[hbm, hbm, hbm, hbm, vmem],
+        out_specs=[vmem] * 4,
+        scratch_shapes=[
+            pltpu.VMEM((heads, QBLK, LATP), bf16),
+            pltpu.VMEM((2, QBLK, 128), f32),
+            pltpu.SemaphoreType.DMA((heads // HG + 2,)),
+        ],
         cost_estimate=pl.CostEstimate(
-            flops=2 * 32 * QBLK * n * BLOCK * LAT, bytes_accessed=12 << 20, transcendentals=32 * QBLK * n * BLOCK
+            flops=2 * heads * QBLK * n * BLOCK * LAT, bytes_accessed=12 << 20, transcendentals=heads * QBLK * n * BLOCK
         ),
         name="teacher_terms",
-        compiler_params=pltpu.CompilerParams(vmem_limit_bytes=24 << 20),
-    )(qa, qb, la, lb, kj)
+        compiler_params=pltpu.CompilerParams(vmem_limit_bytes=36 << 20),
+    )(*[pltpu.with_memory_space_constraint(a, pltpu.HBM) for a in (qa, qb, la, lb)], kj)
 
 
 def spread_body(*refs):
@@ -280,6 +301,7 @@
         out_specs=(vmem,) * 3,
         cost_estimate=pl.CostEstimate(flops=0, bytes_accessed=3 << 20, transcendentals=0),
         name="spread",
+        compiler_params=pltpu.CompilerParams(vmem_limit_bytes=8 << 20),
     )(*blocks)
 
 
@@ -314,13 +336,14 @@
         ),
         cost_estimate=pl.CostEstimate(flops=2 * IDXH * QPART * n * BLOCK * IDXD, bytes_accessed=12 << 20, transcendentals=0),
         name="scores",
+        compiler_params=pltpu.CompilerParams(vmem_limit_bytes=24 << 20),
     )(iq, wb, kj)
 
 
 PB = 4
 
 
-def backward_body(own_ref, t1_ref, t2_ref, t3_ref, score_ref, iq_ref, iqt_ref, wb_ref, raw_ref, kj_ref, gk_ref, *refs):
+def backward_body(own_ref, t1_ref, t2_ref, t3_ref, score_ref, iqt_ref, wb_ref, raw_ref, kj_ref, gk_ref, *refs):
     *gq_refs, grad_ref, gr_ref, acc_ref = refs
     step = pl.program_id(0)
     span = PB * BLOCK
@@ -348,29 +371,20 @@
 
     @pl.when(step == pl.num_programs(0) - 1)
     def _():
-        lane = lax.broadcasted_iota(jnp.int32, (QPART, 128), 1)
         for src in range(8):
-            gq_refs[src][: 8 * QPART, :] = acc_ref[src * 8 * QPART : (src + 1) * 8 * QPART, :].astype(bf16)
-            out = jnp.zeros((QPART, 128), f32)
-            for i in range(8):
-                e = src * 8 + i
-                rows = slice(e * QPART, (e + 1) * QPART)
-                gw = jnp.sum(iq_ref[rows, :].astype(f32) * acc_ref[rows, :], axis=1, keepdims=True)
-                rest = gw / wb_ref[e]
-                for k in range(3):
-                    piece = rest.astype(bf16).astype(f32)
-                    out = jnp.where(lane == 8 * k + i, piece, out)
-                    rest = rest - piece
-            gq_refs[src][8 * QPART :, :] = out.astype(bf16)
-
-
-def backward(own, moved, score, iq, iqt, wb, raw, kj):
+            gq_refs[src][...] = acc_ref[src * 8 * QPART : (src + 1) * 8 * QPART, :].astype(bf16)
+
+
+def backward(own, moved, score, iqt, wb, raw, kj):
     n = kj.shape[0]
-    fixed = (own, *moved, score, iq, iqt, wb)
+    fixed = (own, *moved, score, iqt, wb)
     return pl.pallas_call(
         backward_body,
-        out_shape=(jax.ShapeDtypeStruct((n * BLOCK, IDXD), bf16),)
-        + (jax.ShapeDtypeStruct((9 * QPART, IDXD), bf16),) * 8,
+        out_shape=(
+            pltpu.HBM((n * BLOCK, IDXD), bf16),
+            jax.ShapeDtypeStruct((8 * QPART, IDXD), bf16),
+        )
+        + (pltpu.HBM((8 * QPART, IDXD), bf16),) * 7,
         grid=(n // PB,),
         in_specs=[whole(a) for a in fixed]
         + [
@@ -378,7 +392,7 @@
             pl.BlockSpec((PB, BLOCK, IDXD), lambda i: (i, 0, 0)),
         ],
         out_specs=(pl.BlockSpec((PB * BLOCK, IDXD), lambda i: (i, 0)),)
-        + (pl.BlockSpec((9 * QPART, IDXD), lambda i: (0, 0)),) * 8,
+        + (pl.BlockSpec((8 * QPART, IDXD), lambda i: (0, 0)),) * 8,
         scratch_shapes=[
             pltpu.VMEM((QPART, n * BLOCK), f32),
             pltpu.VMEM((IDXH * QPART, PB * BLOCK), bf16),
@@ -386,6 +400,7 @@
         ],
         cost_estimate=pl.CostEstimate(flops=4 * IDXH * QPART * n * BLOCK * IDXD, bytes_accessed=16 << 20, transcendentals=0),
         name="backward",
+        compiler_params=pltpu.CompilerParams(vmem_limit_bytes=30 << 20),
     )(*fixed, raw, kj)
 
 
@@ -416,11 +431,11 @@
         moved.append(lax.ppermute(parts[d - 1], "head", ring))
     score, raw = scores(iq, wb, kj)
 
-    gk, *gq = backward(own, moved, score, iq, iqt, wb, raw, kj)
+    gk, *gq = backward(own, moved, score, iqt, wb, raw, kj)
 
     gk = lax.all_to_all(gk.reshape(128, 16, IDXD), ("seq", "head"), split_axis=0, concat_axis=0, tiled=True)
     gq = gq[:1] + [lax.ppermute(gq[k], "head", [(h, (h - k) & 7) for h in range(8)]) for k in range(1, 8)]
-    gq, gw = place(head.reshape(1), gq)
+    gq, gw = place(head.reshape(1), index_queries, index_weights.T, gq)
     return gq, gw.T, add_pages(wanted, gk)
 
 

time: 138 us -> 124 us (0.90)
  Pallas kernels: 53.7 us -> 45.9 us
  local copies, waits for them, and re-layouts: 6.52 us -> 2.76 us
  waiting for transfers between devices: 23 us -> 21.5 us
    unnamed x24 -> x18, local copies, waits for them, and re-layouts: 6.52 us -> 2.76 us
    pallas_call x1, Pallas kernels: 6.72 us -> 3.64 us  [scores(): pl.pallas_call(score_body, out_shape=(jax.ShapeDtypeStruct((QPART, n * BL...]
    pallas_call x1, Pallas kernels: 10.9 us -> 8.41 us  [backward(): pl.pallas_call(backward_body, out_shape=(pltpu.HBM((n * BLOCK, IDXD), bf1...]
    all_to_all x1, waiting for transfers between devices: 11.6 us -> 10.1 us  [step(): kj = lax.all_to_all(packed, 'seq', split_axis=0, concat_axis=0, tiled=True)]
  transfers between devices with their start and end apart: 22 -> 22, of which waited for: 5 -> 5; matrix products, arithmetic and copies ran while one was open for 0% -> 0% of each run, Pallas kernels for 27% -> 25%
where the time goes in v5:
time: 124 us; the launch traced here: 123 us
  starting transfers between devices  51.2 us (41%)
  Pallas kernels  45.9 us (37%)
  waiting for transfers between devices  21.5 us (17%)
  local copies, waits for them, and re-layouts  2.76 us (2%)
    pallas_call x1, Pallas kernels, teacher_terms(): pl.pallas_call(teacher_body, out_shape=[jax.ShapeDtypeStruct((QPART, n *...  15.4 us
    all_to_all x1, starting transfers between devices, step(): lax.all_to_all(gk.reshape(128, 16, IDXD), ('seq', 'head'), split_axis=0,...  11.5 us
    all_to_all x1, waiting for transfers between devices, step(): kj = lax.all_to_all(packed, 'seq', split_axis=0, concat_axis=0, tiled=True)  10.1 us
    ppermute x7, starting transfers between devices, step(): lax.ppermute(dealt[k], 'head', [(h, h + k & 7) for h in range(8)])  9.78 us
    ppermute x7, starting transfers between devices, step(): lax.ppermute(gq[k], 'head', [(h, h - k & 7) for h in range(8)])  9.37 us
    all_to_all x1, starting transfers between devices, step(): lax.all_to_all(wanted, 'seq', split_axis=0, concat_axis=0, tiled=True)  8.6 us
    pallas_call x1, Pallas kernels, backward(): pl.pallas_call(backward_body, out_shape=(pltpu.HBM((n * BLOCK, IDXD), bf1...  8.41 us
    pallas_call x1, Pallas kernels, flip_queries(): pl.pallas_call(flip_body, out_shape=(oq, oq, ol, ol), grid_spec=pltpu.Pre...  6.77 us
  transfers between devices with their start and end apart: 22, of which 5 were waited for; matrix products, arithmetic and copies ran while one was open for 0% of the time, Pallas kernels for 25%

profile of v5, /device:TPU:1, one launch (start us, length us, event | category | flops | bytes accessed | tf_op | source)
XLA Modules:
  0.0 122.6 jit_solution(879186855710083030)
XLA Ops:
  0.6 1.4 %lookup.1 = s32[16,2]{1,0:T(8,128)} custom-call(s32[2,16]{1,0:T(2,128)} %lists_ref.1, s32[1024]{0:T(1024)} %place_ref.1), custom_call_target="tpu_custom_call" | custom-call | tf_op jit(solution)/shard_map/lookup/pallas_call | solution.py:50
  2.1 8.6 %all-to-all-start = ((s32[16,1,2]{2,1,0:T(1,128)}), s32[16,1,2]{2,1,0:T(1,128)S(1)}, u32[]{:S(2)}, u32[]{:S(2)}) async-start(s32[16,1,2]{2,1,0:T(1,128)} %bitcast.23), calls=%async_computation | async-start | bytes 16384 | tf_op jit(solution)/shard_map/all_to_all | solution.py:414
  10.7 6.4 %all-to-all-done = s32[16,1,2]{2,1,0:T(1,128)S(1)} async-done(((s32[16,1,2]{2,1,0:T(1,128)}), s32[16,1,2]{2,1,0:T(1,128)S(1)}, u32[]{:S(2)}, u32[]{:S(2)}) %all-to-all-start) | async-done | bytes 160 | tf_op jit(solution)/shard_map/all_to_all | solution.py:414
  17.0 0.6 copy-done.1
  17.6 3.8 %pack_pages.1 = bf16[16,704,128]{2,1,0:T(8,128)(2,1)} custom-call(s32[1]{0:T(128)} %bitcast.2.core_ref, s32[16,2]{1,0:T(8,128)} %bitcast.13, bf16[64,576,128]{2,1,0:T(8,128)(2,1)} %bitcast.19, bf16[64,128,128]{2,1,0:T(8,128)(2,1)} %key_ref.1), custom_call_target="tpu_custom_call" | custom-call | bytes 6291456 | tf_op jit(solution)/shard_map/pack_pages/pallas_call | solution.py:82
  21.4 3.7 %all-to-all-start.1 = ((bf16[16,704,128]{2,1,0:T(8,128)(2,1)}), bf16[16,704,128]{2,1,0:T(8,128)(2,1)S(1)}, u32[]{:S(2)}, u32[]{:S(2)}) async-start(bf16[16,704,128]{2,1,0:T(8,128)(2,1)} %pack_pages.1), calls=%async_computation.1 | async-start | bytes 5767168 | tf_op jit(solution)/shard_map/all_to_all | solution.py:417
  25.2 0.6 pad_add_fusion.place_ref
  25.8 6.8 %flip_queries.1 = (bf16[16,128,640]{2,1,0:T(8,128)(2,1)}, bf16[16,128,640]{2,1,0:T(8,128)(2,1)}, f32[128,128]{1,0:T(8,128)}, f32[128,128]{1,0:T(8,128)}) custom-call(s32[2]{0:T(128)} %pad_add_fusion.place_ref, bf16[16,576,256]{2,1,0:T(8,128)(2,1)} %bitcast.17, bf16[16,576,256]{2,1,0:T(8,128)(2,1)} %bitcast.18, f32[16,256]{1,0:T(8,128)} %bitcast.21, ...), custom_call_target="tpu_custom_call" | custom-call | bytes 25165824 | tf_op jit(solution)/shard_map/flip_queries/pallas_call | solution.py:129
  32.6 2.7 %collective-permute-start = (bf16[16,128,640]{2,1,0:T(8,128)(2,1)}, bf16[16,128,640]{2,1,0:T(8,128)(2,1)S(1)}, u32[]{:S(2)}, u32[]{:S(2)}) collective-permute-start(bf16[16,128,640]{2,1,0:T(8,128)(2,1)} %get-tuple-element.36), channel_id=1, source_target_pairs={{0,1},{1,0},{2,3},{3,2},{4,5},{5,4},{6,7},{7,6},{8,9},{9,8},{10,11... | collective-permute-start | bytes 7864328 | tf_op jit(solution)/shard_map/ppermute | solution.py:424
  35.3 1.2 deal.1
  36.5 1.1 collective-permute-start.5
  37.6 1.2 collective-permute-start.6
  38.8 0.0 collective-permute-start.1
  38.8 2.0 %collective-permute-start.7 = (bf16[288,128]{1,0:T(8,128)(2,1)}, bf16[288,128]{1,0:T(8,128)(2,1)}, u32[]{:S(2)}, u32[]{:S(2)}) collective-permute-start(bf16[288,128]{1,0:T(8,128)(2,1)} %get-tuple-element.46), channel_id=1, source_target_pairs={{0,3},{1,4},{2,5},{3,6},{4,7},{5,0},{6,1},{7,2},{8,11},{9,12},{10,... | collective-permute-start | bytes 221192 | tf_op jit(solution)/shard_map/ppermute | solution.py:420
  40.8 0.0 collective-permute-done.1.lb_ref
  40.8 2.1 %collective-permute-start.8 = (bf16[288,128]{1,0:T(8,128)(2,1)}, bf16[288,128]{1,0:T(8,128)(2,1)}, u32[]{:S(2)}, u32[]{:S(2)}) collective-permute-start(bf16[288,128]{1,0:T(8,128)(2,1)} %get-tuple-element.47), channel_id=1, source_target_pairs={{0,4},{1,5},{2,6},{3,7},{4,0},{5,1},{6,2},{7,3},{8,12},{9,13},{10,... | collective-permute-start | bytes 221192 | tf_op jit(solution)/shard_map/ppermute | solution.py:420
  42.9 1.4 %collective-permute-start.9 = (bf16[288,128]{1,0:T(8,128)(2,1)}, bf16[288,128]{1,0:T(8,128)(2,1)}, u32[]{:S(2)}, u32[]{:S(2)}) collective-permute-start(bf16[288,128]{1,0:T(8,128)(2,1)} %get-tuple-element.48), channel_id=1, source_target_pairs={{0,5},{1,6},{2,7},{3,0},{4,1},{5,2},{6,3},{7,4},{8,13},{9,14},{10,... | collective-permute-start | bytes 221192 | tf_op jit(solution)/shard_map/ppermute | solution.py:420
  44.3 0.0 collective-permute-done.6.refs_2_
  44.3 0.6 copy-done.3
  44.9 0.0 collective-permute-start.10
  44.9 0.0 collective-permute-done.qb_ref
  44.9 1.5 %copy-done.7 = bf16[16,128,640]{2,1,0:T(8,128)(2,1)} copy-done((bf16[16,128,640]{2,1,0:T(8,128)(2,1)}, bf16[16,128,640]{2,1,0:T(8,128)(2,1)S(1)}, u32[]{:S(2)}) %copy-start.7) | copy-done | bytes 2621464
  46.5 2.0 %collective-permute-start.11 = (bf16[288,128]{1,0:T(8,128)(2,1)}, bf16[288,128]{1,0:T(8,128)(2,1)}, u32[]{:S(2)}, u32[]{:S(2)}) collective-permute-start(bf16[288,128]{1,0:T(8,128)(2,1)} %get-tuple-element.50), channel_id=1, source_target_pairs={{0,7},{1,0},{2,1},{3,2},{4,3},{5,4},{6,5},{7,6},{8,15},{9,8},{10,9... | collective-permute-start | bytes 221192 | tf_op jit(solution)/shard_map/ppermute | solution.py:420
  48.4 10.1 %all-to-all-done.1.kj_ref = bf16[16,704,128]{2,1,0:T(8,128)(2,1)S(1)} async-done(((bf16[16,704,128]{2,1,0:T(8,128)(2,1)}), bf16[16,704,128]{2,1,0:T(8,128)(2,1)S(1)}, u32[]{:S(2)}, u32[]{:S(2)}) %all-to-all-start.1) | async-done | bytes 2883616 | tf_op jit(solution)/shard_map/all_to_all | solution.py:417
  58.5 15.4 %teacher_terms.1 = (bf16[32,2048]{1,0:T(8,128)(2,1)S(1)}, bf16[32,2048]{1,0:T(8,128)(2,1)S(1)}, bf16[32,2048]{1,0:T(8,128)(2,1)S(1)}, f32[32,2048]{1,0:T(8,128)S(1)}) custom-call(bf16[16,128,640]{2,1,0:T(8,128)(2,1)} %get-tuple-element.35.qa_ref, bf16[16,128,640]{2,1,0:T(8,128)(2,1)} %copy-done.7, f32[128,128]{1,0:T(8,128)} %get-tuple-element.37.la_ref, ...), custom_call_target="tpu_custom_call" | custom-call | flops 9663676416 | bytes 12582912 | tf_op jit(solution)/shard_map/teacher_terms/pallas_call | solution.py:261
  73.9 0.0 collective-permute-done.7.refs_3_
  74.0 2.8 %collective-permute-start.2 = (bf16[32,2048]{1,0:T(8,128)(2,1)S(1)}, bf16[32,2048]{1,0:T(8,128)(2,1)S(1)}, u32[]{:S(2)}, u32[]{:S(2)}) collective-permute-start(bf16[32,2048]{1,0:T(8,128)(2,1)S(1)} %get-tuple-element.40), channel_id=1, source_target_pairs={{0,4},{1,5},{2,6},{3,7},{4,0},{5,1},{6,2},{7,3},{8,12},{9,13},{10,... | collective-permute-start | bytes 393224 | tf_op jit(solution)/shard_map/ppermute | solution.py:431
  76.8 0.3 collective-permute-start.3
  77.1 2.4 %collective-permute-start.4 = (bf16[32,2048]{1,0:T(8,128)(2,1)S(1)}, bf16[32,2048]{1,0:T(8,128)(2,1)S(1)}, u32[]{:S(2)}, u32[]{:S(2)}) collective-permute-start(bf16[32,2048]{1,0:T(8,128)(2,1)S(1)} %get-tuple-element.42), channel_id=1, source_target_pairs={{0,6},{1,7},{2,0},{3,1},{4,2},{5,3},{6,4},{7,5},{8,14},{9,15},{10,... | collective-permute-start | bytes 393224 | tf_op jit(solution)/shard_map/ppermute | solution.py:431
  79.5 2.3 %spread.1 = (bf16[2048,128]{1,0:T(8,128)(2,1)S(1)}, bf16[128,2048]{1,0:T(8,128)(2,1)S(1)}, f32[64,32,128]{2,1,0:T(8,128)S(1)}) custom-call(bf16[288,128]{1,0:T(8,128)(2,1)S(1)} %get-tuple-element.43.refs_0_, bf16[288,128]{1,0:T(8,128)(2,1)S(1)} %collective-permute-done.5.refs_1_, bf16[288,128]{1,0:T(8,128)(2,1)S(1)} %copy-done.4, ...), custom_call_target="tpu_custom_call" | custom-call | bytes 3145728 | tf_op jit(solution)/shard_map/spread/pallas_call | solution.py:293
  81.7 3.6 %scores.1 = (f32[32,2048]{1,0:T(8,128)S(1)}, bf16[2048,2048]{1,0:T(8,128)(2,1)S(1)}) custom-call(bf16[2048,128]{1,0:T(8,128)(2,1)S(1)} %get-tuple-element.51.iq_ref, f32[64,32,128]{2,1,0:T(8,128)S(1)} %get-tuple-element.52.wb_ref, bf16[16,704,128]{2,1,0:T(8,128)(2,1)S(1)} %all-to-all-done.1.kj_ref), custom_call_target="tpu_custom_call" | custom-call | flops 1073741824 | bytes 12582912 | tf_op jit(solution)/shard_map/scores/pallas_call | solution.py:325
  85.4 0.0 collective-permute-done.2.t1_ref
  85.4 0.0 collective-permute-done.3.t2_ref
  85.4 0.0 copy-start.6
  85.5 8.4 %backward.1 = (bf16[2048,128]{1,0:T(8,128)(2,1)}, bf16[256,128]{1,0:T(8,128)(2,1)S(1)}, bf16[256,128]{1,0:T(8,128)(2,1)}, bf16[256,128]{1,0:T(8,128)(2,1)}, bf16...) custom-call(f32[32,2048]{1,0:T(8,128)S(1)} %get-tuple-element.39.own, ...), custom_call_target="tpu_custom_call" | custom-call | flops 2147483648 | bytes 16777216 | tf_op jit(solution)/shard_map/backward/pallas_call | solution.py:381
  93.9 11.5 %all-to-all-start.2 = ((bf16[128,16,128]{2,1,0:T(8,128)(2,1)}), bf16[128,16,128]{2,1,0:T(8,128)(2,1)S(1)}, u32[]{:S(2)}, u32[]{:S(2)}) async-start(bf16[128,16,128]{2,1,0:T(8,128)(2,1)} %bitcast.20), calls=%async_computation.2 | async-start | bytes 1048576 | tf_op jit(solution)/shard_map/all_to_all | solution.py:436
  105.3 1.1 collective-permute-start.12
  106.4 1.9 %collective-permute-start.13 = (bf16[256,128]{1,0:T(8,128)(2,1)}, bf16[256,128]{1,0:T(8,128)(2,1)S(1)}, u32[]{:S(2)}, u32[]{:S(2)}) collective-permute-start(bf16[256,128]{1,0:T(8,128)(2,1)} %get-tuple-element.58), channel_id=1, source_target_pairs={{0,6},{1,7},{2,0},{3,1},{4,2},{5,3},{6,4},{7,5},{8,14},{9,15},{10,... | collective-permute-start | bytes 196616 | tf_op jit(solution)/shard_map/ppermute | solution.py:437
  108.3 1.0 collective-permute-start.14
  109.3 2.4 %collective-permute-start.15 = (bf16[256,128]{1,0:T(8,128)(2,1)}, bf16[256,128]{1,0:T(8,128)(2,1)S(1)}, u32[]{:S(2)}, u32[]{:S(2)}) collective-permute-start(bf16[256,128]{1,0:T(8,128)(2,1)} %get-tuple-element.60), channel_id=1, source_target_pairs={{0,4},{1,5},{2,6},{3,7},{4,0},{5,1},{6,2},{7,3},{8,12},{9,13},{10,... | collective-permute-start | bytes 196616 | tf_op jit(solution)/shard_map/ppermute | solution.py:437
  111.7 0.7 collective-permute-start.16
  112.4 2.4 %collective-permute-done.12.refs_1_ = bf16[256,128]{1,0:T(8,128)(2,1)S(1)} collective-permute-done((bf16[256,128]{1,0:T(8,128)(2,1)}, bf16[256,128]{1,0:T(8,128)(2,1)S(1)}, u32[]{:S(2)}, u32[]{:S(2)}) %collective-permute-start.12) | collective-permute-done | bytes 65568 | tf_op jit(solution)/shard_map/ppermute | solution.py:437
  114.8 1.2 collective-permute-start.17
  116.0 1.1 collective-permute-start.18
  117.2 0.7 collective-permute-done.16.refs_5_
  117.9 1.8 %collective-permute-done.17.refs_6_ = bf16[256,128]{1,0:T(8,128)(2,1)S(1)} collective-permute-done((bf16[256,128]{1,0:T(8,128)(2,1)}, bf16[256,128]{1,0:T(8,128)(2,1)S(1)}, u32[]{:S(2)}, u32[]{:S(2)}) %collective-permute-start.17) | collective-permute-done | bytes 65568 | tf_op jit(solution)/shard_map/ppermute | solution.py:437
  119.7 1.3 %place.1 = (f32[256,8,128]{2,1,0:T(8,128)}, f32[8,256]{1,0:T(8,128)}) custom-call(s32[1]{0:T(128)} %bitcast.head_ref, bf16[256,8,128]{2,1,0:T(8,128)(2,1)S(1)} %copy-done, f32[8,256]{1,0:T(8,128)S(1)} %bitcast.16, bf16[256,128]{1,0:T(8,128)(2,1)S(1)} %get-tuple-element.56.refs_0_, bf16[256,128]{1,0:T(8,128)(2,1)S(1)} %collective-permute-done.12.refs_1_, ...), custom_call_target="tpu_custom_call" | custom-call | bytes 2097152 | tf_op jit(solution)/shard_map/place/pallas_call | solution.py:190
  121.0 1.6 %add_pages.1 = f32[64,16,128]{2,1,0:T(8,128)} custom-call(s32[16,2]{1,0:T(8,128)S(1)} %bitcast.14, bf16[128,16,128]{2,1,0:T(8,128)(2,1)S(1)} %all-to-all-done.2.gk_ref), custom_call_target="tpu_custom_call" | custom-call | bytes 1048576 | tf_op jit(solution)/shard_map/add_pages/pallas_call | solution.py:212
  (25 shorter events, 0.1 us)
Async XLA Ops:
  2.1 15.0 %all-to-all-start = ((s32[16,1,2]{2,1,0:T(1,128)}), s32[16,1,2]{2,1,0:T(1,128)S(1)}, u32[]{:S(2)}, u32[]{:S(2)}) async-start(s32[16,1,2]{2,1,0:T(1,128)} %bitcast.23), calls=%async_computation | async-start | bytes 16384 | tf_op jit(solution)/shard_map/all_to_all | solution.py:414
  17.0 0.6 copy-start.1
  21.4 37.1 %all-to-all-start.1 = ((bf16[16,704,128]{2,1,0:T(8,128)(2,1)}), bf16[16,704,128]{2,1,0:T(8,128)(2,1)S(1)}, u32[]{:S(2)}, u32[]{:S(2)}) async-start(bf16[16,704,128]{2,1,0:T(8,128)(2,1)} %pack_pages.1), calls=%async_computation.1 | async-start | bytes 5767168 | tf_op jit(solution)/shard_map/all_to_all | solution.py:417
  25.8 9.5 %copy-start = (bf16[256,8,128]{2,1,0:T(8,128)(2,1)S(1)}, bf16[256,8,128]{2,1,0:T(8,128)(2,1)}, u32[]{:S(2)}) copy-start(bf16[256,8,128]{2,1,0:T(8,128)(2,1)} %iq_ref.3) | copy-start | bytes 1572868
  25.8 9.5 %copy-start.5 = (f32[256,8]{0,1:T(8,128)S(1)}, f32[256,8]{0,1:T(8,128)}, u32[]{:S(2)}) copy-start(f32[256,8]{0,1:T(8,128)} %param.13) | copy-start | bytes 24580
  32.6 12.4 %collective-permute-start = (bf16[16,128,640]{2,1,0:T(8,128)(2,1)}, bf16[16,128,640]{2,1,0:T(8,128)(2,1)S(1)}, u32[]{:S(2)}, u32[]{:S(2)}) collective-permute-start(bf16[16,128,640]{2,1,0:T(8,128)(2,1)} %get-tuple-element.36), channel_id=1, source_target_pairs={{0,1},{1,0},{2,3},{3,2},{4,5},{5,4},{6,7},{7,6},{8,9},{9,8},{10,11... | collective-permute-start | bytes 7864328 | tf_op jit(solution)/shard_map/ppermute | solution.py:424
  36.5 6.4 %collective-permute-start.5 = (bf16[288,128]{1,0:T(8,128)(2,1)}, bf16[288,128]{1,0:T(8,128)(2,1)S(1)}, u32[]{:S(2)}, u32[]{:S(2)}) collective-permute-start(bf16[288,128]{1,0:T(8,128)(2,1)} %get-tuple-element.44), channel_id=1, source_target_pairs={{0,1},{1,2},{2,3},{3,4},{4,5},{5,6},{6,7},{7,0},{8,9},{9,10},{10,1... | collective-permute-start | bytes 221192 | tf_op jit(solution)/shard_map/ppermute | solution.py:420
  37.6 6.7 %collective-permute-start.6 = (bf16[288,128]{1,0:T(8,128)(2,1)}, bf16[288,128]{1,0:T(8,128)(2,1)S(1)}, u32[]{:S(2)}, u32[]{:S(2)}) collective-permute-start(bf16[288,128]{1,0:T(8,128)(2,1)} %get-tuple-element.45), channel_id=1, source_target_pairs={{0,2},{1,3},{2,4},{3,5},{4,6},{5,7},{6,0},{7,1},{8,10},{9,11},{10,... | collective-permute-start | bytes 221192 | tf_op jit(solution)/shard_map/ppermute | solution.py:420
  38.8 2.0 %collective-permute-start.1 = (f32[128,128]{1,0:T(8,128)}, f32[128,128]{1,0:T(8,128)S(1)}, u32[]{:S(2)}, u32[]{:S(2)}) collective-permute-start(f32[128,128]{1,0:T(8,128)} %get-tuple-element.38), channel_id=1, source_target_pairs={{0,1},{1,0},{2,3},{3,2},{4,5},{5,4},{6,7},{7,6},{8,9},{9,8},{10,11... | collective-permute-start | bytes 196616 | tf_op jit(solution)/shard_map/ppermute | solution.py:425
  38.8 35.1 %collective-permute-start.7 = (bf16[288,128]{1,0:T(8,128)(2,1)}, bf16[288,128]{1,0:T(8,128)(2,1)}, u32[]{:S(2)}, u32[]{:S(2)}) collective-permute-start(bf16[288,128]{1,0:T(8,128)(2,1)} %get-tuple-element.46), channel_id=1, source_target_pairs={{0,3},{1,4},{2,5},{3,6},{4,7},{5,0},{6,1},{7,2},{8,11},{9,12},{10,... | collective-permute-start | bytes 221192 | tf_op jit(solution)/shard_map/ppermute | solution.py:420
  40.8 4.1 %copy-start.8 = (f32[128,128]{1,0:T(8,128)}, f32[128,128]{1,0:T(8,128)S(1)}, u32[]{:S(2)}) copy-start(f32[128,128]{1,0:T(8,128)S(1)} %collective-permute-done.1.lb_ref) | copy-start | bytes 196612
  40.8 36.0 %collective-permute-start.8 = (bf16[288,128]{1,0:T(8,128)(2,1)}, bf16[288,128]{1,0:T(8,128)(2,1)}, u32[]{:S(2)}, u32[]{:S(2)}) collective-permute-start(bf16[288,128]{1,0:T(8,128)(2,1)} %get-tuple-element.47), channel_id=1, source_target_pairs={{0,4},{1,5},{2,6},{3,7},{4,0},{5,1},{6,2},{7,3},{8,12},{9,13},{10,... | collective-permute-start | bytes 221192 | tf_op jit(solution)/shard_map/ppermute | solution.py:420
  42.9 34.2 %collective-permute-start.9 = (bf16[288,128]{1,0:T(8,128)(2,1)}, bf16[288,128]{1,0:T(8,128)(2,1)}, u32[]{:S(2)}, u32[]{:S(2)}) collective-permute-start(bf16[288,128]{1,0:T(8,128)(2,1)} %get-tuple-element.48), channel_id=1, source_target_pairs={{0,5},{1,6},{2,7},{3,0},{4,1},{5,2},{6,3},{7,4},{8,13},{9,14},{10,... | collective-permute-start | bytes 221192 | tf_op jit(solution)/shard_map/ppermute | solution.py:420
  44.3 0.6 copy-start.3
  44.9 34.5 %collective-permute-start.10 = (bf16[288,128]{1,0:T(8,128)(2,1)}, bf16[288,128]{1,0:T(8,128)(2,1)}, u32[]{:S(2)}, u32[]{:S(2)}) collective-permute-start(bf16[288,128]{1,0:T(8,128)(2,1)} %get-tuple-element.49), channel_id=1, source_target_pairs={{0,6},{1,7},{2,0},{3,1},{4,2},{5,3},{6,4},{7,5},{8,14},{9,15},{10,... | collective-permute-start | bytes 221192 | tf_op jit(solution)/shard_map/ppermute | solution.py:420
  44.9 1.5 %copy-start.7 = (bf16[16,128,640]{2,1,0:T(8,128)(2,1)}, bf16[16,128,640]{2,1,0:T(8,128)(2,1)S(1)}, u32[]{:S(2)}) copy-start(bf16[16,128,640]{2,1,0:T(8,128)(2,1)S(1)} %collective-permute-done.qb_ref) | copy-start | bytes 7864324
  46.5 33.0 %collective-permute-start.11 = (bf16[288,128]{1,0:T(8,128)(2,1)}, bf16[288,128]{1,0:T(8,128)(2,1)}, u32[]{:S(2)}, u32[]{:S(2)}) collective-permute-start(bf16[288,128]{1,0:T(8,128)(2,1)} %get-tuple-element.50), channel_id=1, source_target_pairs={{0,7},{1,0},{2,1},{3,2},{4,3},{5,4},{6,5},{7,6},{8,15},{9,8},{10,9... | collective-permute-start | bytes 221192 | tf_op jit(solution)/shard_map/ppermute | solution.py:420
  58.5 21.0 %copy-start.4 = (bf16[288,128]{1,0:T(8,128)(2,1)S(1)}, bf16[288,128]{1,0:T(8,128)(2,1)}, u32[]{:S(2)}) copy-start(bf16[288,128]{1,0:T(8,128)(2,1)} %copy-done.3) | copy-start | bytes 221188
  74.0 11.4 %collective-permute-start.2 = (bf16[32,2048]{1,0:T(8,128)(2,1)S(1)}, bf16[32,2048]{1,0:T(8,128)(2,1)S(1)}, u32[]{:S(2)}, u32[]{:S(2)}) collective-permute-start(bf16[32,2048]{1,0:T(8,128)(2,1)S(1)} %get-tuple-element.40), channel_id=1, source_target_pairs={{0,4},{1,5},{2,6},{3,7},{4,0},{5,1},{6,2},{7,3},{8,12},{9,13},{10,... | collective-permute-start | bytes 393224 | tf_op jit(solution)/shard_map/ppermute | solution.py:431
  76.8 8.6 %collective-permute-start.3 = (bf16[32,2048]{1,0:T(8,128)(2,1)S(1)}, bf16[32,2048]{1,0:T(8,128)(2,1)S(1)}, u32[]{:S(2)}, u32[]{:S(2)}) collective-permute-start(bf16[32,2048]{1,0:T(8,128)(2,1)S(1)} %get-tuple-element.41), channel_id=1, source_target_pairs={{0,2},{1,3},{2,4},{3,5},{4,6},{5,7},{6,0},{7,1},{8,10},{9,11},{10,... | collective-permute-start | bytes 393224 | tf_op jit(solution)/shard_map/ppermute | solution.py:431
  77.1 8.3 %collective-permute-start.4 = (bf16[32,2048]{1,0:T(8,128)(2,1)S(1)}, bf16[32,2048]{1,0:T(8,128)(2,1)S(1)}, u32[]{:S(2)}, u32[]{:S(2)}) collective-permute-start(bf16[32,2048]{1,0:T(8,128)(2,1)S(1)} %get-tuple-element.42), channel_id=1, source_target_pairs={{0,6},{1,7},{2,0},{3,1},{4,2},{5,3},{6,4},{7,5},{8,14},{9,15},{10,... | collective-permute-start | bytes 393224 | tf_op jit(solution)/shard_map/ppermute | solution.py:431
  85.4 34.3 %copy-start.6 = (f32[256,8]{0,1:T(8,128)S(1)}, f32[256,8]{0,1:T(8,128)}, u32[]{:S(2)}) copy-start(f32[256,8]{0,1:T(8,128)} %param.13) | copy-start | bytes 24580
  85.4 35.6 %copy-start.2 = (s32[16,1,2]{2,1,0:T(1,128)S(1)}, s32[16,1,2]{2,1,0:T(1,128)}, u32[]{:S(2)}) copy-start(s32[16,1,2]{2,1,0:T(1,128)} %copy-done.1) | copy-start | bytes 388
  93.9 27.1 %all-to-all-start.2 = ((bf16[128,16,128]{2,1,0:T(8,128)(2,1)}), bf16[128,16,128]{2,1,0:T(8,128)(2,1)S(1)}, u32[]{:S(2)}, u32[]{:S(2)}) async-start(bf16[128,16,128]{2,1,0:T(8,128)(2,1)} %bitcast.20), calls=%async_computation.2 | async-start | bytes 1048576 | tf_op jit(solution)/shard_map/all_to_all | solution.py:436
  105.3 9.5 %collective-permute-start.12 = (bf16[256,128]{1,0:T(8,128)(2,1)}, bf16[256,128]{1,0:T(8,128)(2,1)S(1)}, u32[]{:S(2)}, u32[]{:S(2)}) collective-permute-start(bf16[256,128]{1,0:T(8,128)(2,1)} %get-tuple-element.57), channel_id=1, source_target_pairs={{0,7},{1,0},{2,1},{3,2},{4,3},{5,4},{6,5},{7,6},{8,15},{9,8},{10,9... | collective-permute-start | bytes 196616 | tf_op jit(solution)/shard_map/ppermute | solution.py:437
  106.4 9.6 %collective-permute-start.13 = (bf16[256,128]{1,0:T(8,128)(2,1)}, bf16[256,128]{1,0:T(8,128)(2,1)S(1)}, u32[]{:S(2)}, u32[]{:S(2)}) collective-permute-start(bf16[256,128]{1,0:T(8,128)(2,1)} %get-tuple-element.58), channel_id=1, source_target_pairs={{0,6},{1,7},{2,0},{3,1},{4,2},{5,3},{6,4},{7,5},{8,14},{9,15},{10,... | collective-permute-start | bytes 196616 | tf_op jit(solution)/shard_map/ppermute | solution.py:437
  108.3 8.9 %collective-permute-start.14 = (bf16[256,128]{1,0:T(8,128)(2,1)}, bf16[256,128]{1,0:T(8,128)(2,1)S(1)}, u32[]{:S(2)}, u32[]{:S(2)}) collective-permute-start(bf16[256,128]{1,0:T(8,128)(2,1)} %get-tuple-element.59), channel_id=1, source_target_pairs={{0,5},{1,6},{2,7},{3,0},{4,1},{5,2},{6,3},{7,4},{8,13},{9,14},{10,... | collective-permute-start | bytes 196616 | tf_op jit(solution)/shard_map/ppermute | solution.py:437
  109.3 7.8 %collective-permute-start.15 = (bf16[256,128]{1,0:T(8,128)(2,1)}, bf16[256,128]{1,0:T(8,128)(2,1)S(1)}, u32[]{:S(2)}, u32[]{:S(2)}) collective-permute-start(bf16[256,128]{1,0:T(8,128)(2,1)} %get-tuple-element.60), channel_id=1, source_target_pairs={{0,4},{1,5},{2,6},{3,7},{4,0},{5,1},{6,2},{7,3},{8,12},{9,13},{10,... | collective-permute-start | bytes 196616 | tf_op jit(solution)/shard_map/ppermute | solution.py:437
  111.7 6.2 %collective-permute-start.16 = (bf16[256,128]{1,0:T(8,128)(2,1)}, bf16[256,128]{1,0:T(8,128)(2,1)S(1)}, u32[]{:S(2)}, u32[]{:S(2)}) collective-permute-start(bf16[256,128]{1,0:T(8,128)(2,1)} %get-tuple-element.61), channel_id=1, source_target_pairs={{0,3},{1,4},{2,5},{3,6},{4,7},{5,0},{6,1},{7,2},{8,11},{9,12},{10,... | collective-permute-start | bytes 196616 | tf_op jit(solution)/shard_map/ppermute | solution.py:437
  114.8 4.8 %collective-permute-start.17 = (bf16[256,128]{1,0:T(8,128)(2,1)}, bf16[256,128]{1,0:T(8,128)(2,1)S(1)}, u32[]{:S(2)}, u32[]{:S(2)}) collective-permute-start(bf16[256,128]{1,0:T(8,128)(2,1)} %get-tuple-element.62), channel_id=1, source_target_pairs={{0,2},{1,3},{2,4},{3,5},{4,6},{5,7},{6,0},{7,1},{8,10},{9,11},{10,... | collective-permute-start | bytes 196616 | tf_op jit(solution)/shard_map/ppermute | solution.py:437
  116.0 3.6 %collective-permute-start.18 = (bf16[256,128]{1,0:T(8,128)(2,1)}, bf16[256,128]{1,0:T(8,128)(2,1)S(1)}, u32[]{:S(2)}, u32[]{:S(2)}) collective-permute-start(bf16[256,128]{1,0:T(8,128)(2,1)} %get-tuple-element.63), channel_id=1, source_target_pairs={{0,1},{1,2},{2,3},{3,4},{4,5},{5,6},{6,7},{7,0},{8,9},{9,10},{10,1... | collective-permute-start | bytes 196616 | tf_op jit(solution)/shard_map/ppermute | solution.py:437

commit v6 on v5

--- a/solution.py
+++ b/solution.py
@@ -310,8 +310,8 @@
 
 def score_body(iq_ref, wb_ref, kj_ref, out_ref, raw_ref):
     raw = dot_nt(iq_ref[...], kj_ref[...].reshape(-1, IDXD))
-    raw_ref[...] = raw.astype(bf16)
     for t in range(PS):
+        raw_ref[t] = raw[:, t * 128 : (t + 1) * 128].astype(bf16)
         acc = None
         for e in range(IDXH):
             r = raw[e * QPART : (e + 1) * QPART, t * 128 : (t + 1) * 128]
@@ -326,13 +326,13 @@
         score_body,
         out_shape=(
             jax.ShapeDtypeStruct((QPART, n * BLOCK), f32),
-            jax.ShapeDtypeStruct((IDXH * QPART, n * BLOCK), bf16),
+            jax.ShapeDtypeStruct((n, IDXH * QPART, BLOCK), bf16),
         ),
         grid=(n // PS,),
         in_specs=[whole(iq), whole(wb), pl.BlockSpec((PS, BLOCK, IDXD), lambda i: (i, 0, 0))],
         out_specs=(
             pl.BlockSpec((QPART, PS * BLOCK), lambda i: (0, i)),
-            pl.BlockSpec((IDXH * QPART, PS * BLOCK), lambda i: (0, i)),
+            pl.BlockSpec((PS, IDXH * QPART, BLOCK), lambda i: (i, 0, 0)),
         ),
         cost_estimate=pl.CostEstimate(flops=2 * IDXH * QPART * n * BLOCK * IDXD, bytes_accessed=12 << 20, transcendentals=0),
         name="scores",
@@ -345,39 +345,41 @@
 
 def backward_body(own_ref, t1_ref, t2_ref, t3_ref, score_ref, iqt_ref, wb_ref, raw_ref, kj_ref, gk_ref, *refs):
     *gq_refs, grad_ref, gr_ref, acc_ref = refs
-    step = pl.program_id(0)
-    span = PB * BLOCK
-
-    @pl.when(step == 0)
-    def _():
-        teacher = own_ref[...] + t1_ref[...].astype(f32) + t2_ref[...].astype(f32) + t3_ref[...].astype(f32)
-        target = teacher / jnp.sum(teacher, axis=1, keepdims=True)
-        score = score_ref[...]
-        e = jnp.exp(score - jnp.max(score, axis=1, keepdims=True))
-        probs = e / jnp.sum(e, axis=1, keepdims=True)
-        grad_ref[...] = loss_scale * (probs - target)
-        acc_ref[...] = jnp.zeros_like(acc_ref)
-
-    keys = kj_ref[...].reshape(-1, IDXD)
-    for t in range(PB):
-        g = grad_ref[:, pl.ds(pl.multiple_of(step * span + t * 128, 128), 128)]
-        at = slice(t * 128, (t + 1) * 128)
+    teacher = own_ref[...] + t1_ref[...].astype(f32) + t2_ref[...].astype(f32) + t3_ref[...].astype(f32)
+    target = teacher / jnp.sum(teacher, axis=1, keepdims=True)
+    score = score_ref[...]
+    e = jnp.exp(score - jnp.max(score, axis=1, keepdims=True))
+    probs = e / jnp.sum(e, axis=1, keepdims=True)
+    grad_ref[...] = loss_scale * (probs - target)
+
+    def grad_raw(t):
+        g = grad_ref[:, t * 128 : (t + 1) * 128]
         for e in range(IDXH):
             rows = slice(e * QPART, (e + 1) * QPART)
-            gr_ref[rows, at] = jnp.where(raw_ref[rows, at] > 0, (g * wb_ref[e]).astype(bf16), 0)
-    gr = gr_ref[...]
-    gk_ref[...] = dot(iqt_ref[...], gr).T.astype(gk_ref.dtype)
-    acc_ref[...] += dot(gr, keys)
-
-    @pl.when(step == pl.num_programs(0) - 1)
-    def _():
-        for src in range(8):
-            gq_refs[src][...] = acc_ref[src * 8 * QPART : (src + 1) * 8 * QPART, :].astype(bf16)
+            gr_ref[t, rows, :] = jnp.where(raw_ref[t, rows, :] > 0, (g * wb_ref[e]).astype(bf16), 0)
+
+    def products(i):
+        tiles = range(i * PB, (i + 1) * PB)
+        gr = jnp.concatenate([gr_ref[t] for t in tiles], axis=1)
+        gk_ref[i * PB * BLOCK : (i + 1) * PB * BLOCK, :] = dot(iqt_ref[...], gr).T.astype(gk_ref.dtype)
+        part = dot(gr, kj_ref[i * PB : (i + 1) * PB, :BLOCK, :].reshape(-1, IDXD))
+        acc_ref[...] = part if i == 0 else acc_ref[...] + part
+
+    steps = raw_ref.shape[0] // PB
+    for i in range(steps + 1):
+        if i < steps:
+            for t in range(i * PB, (i + 1) * PB):
+                grad_raw(t)
+        if i > 0:
+            products(i - 1)
+    for src in range(8):
+        gq_refs[src][...] = acc_ref[src * 8 * QPART : (src + 1) * 8 * QPART, :].astype(bf16)
 
 
 def backward(own, moved, score, iqt, wb, raw, kj):
     n = kj.shape[0]
-    fixed = (own, *moved, score, iqt, wb)
+    vmem = pl.BlockSpec(memory_space=pltpu.VMEM)
+    args = (own, *moved, score, iqt, wb, raw, kj)
     return pl.pallas_call(
         backward_body,
         out_shape=(
@@ -385,23 +387,17 @@
             jax.ShapeDtypeStruct((8 * QPART, IDXD), bf16),
         )
         + (pltpu.HBM((8 * QPART, IDXD), bf16),) * 7,
-        grid=(n // PB,),
-        in_specs=[whole(a) for a in fixed]
-        + [
-            pl.BlockSpec((IDXH * QPART, PB * BLOCK), lambda i: (0, i)),
-            pl.BlockSpec((PB, BLOCK, IDXD), lambda i: (i, 0, 0)),
-        ],
-        out_specs=(pl.BlockSpec((PB * BLOCK, IDXD), lambda i: (i, 0)),)
-        + (pl.BlockSpec((8 * QPART, IDXD), lambda i: (0, 0)),) * 8,
+        in_specs=[vmem] * len(args),
+        out_specs=(vmem,) * 9,
         scratch_shapes=[
             pltpu.VMEM((QPART, n * BLOCK), f32),
-            pltpu.VMEM((IDXH * QPART, PB * BLOCK), bf16),
+            pltpu.VMEM((n, IDXH * QPART, BLOCK), bf16),
             pltpu.VMEM((IDXH * QPART, IDXD), f32),
         ],
         cost_estimate=pl.CostEstimate(flops=4 * IDXH * QPART * n * BLOCK * IDXD, bytes_accessed=16 << 20, transcendentals=0),
         name="backward",
-        compiler_params=pltpu.CompilerParams(vmem_limit_bytes=30 << 20),
-    )(*fixed, raw, kj)
+        compiler_params=pltpu.CompilerParams(vmem_limit_bytes=34 << 20),
+    )(*args)
 
 
 def step(queries, lse, latent, index_keys, index_queries, index_weights, block_lists, block_place):

time: 124 us -> 120 us (0.968)
  Pallas kernels: 45.9 us -> 42.1 us
    pallas_call x1, Pallas kernels: 8.41 us -> 5.31 us  [backward(): pl.pallas_call(backward_body, out_shape=(pltpu.HBM((n * BLOCK, IDXD), bf1...]
where the time goes in v6:
time: 120 us; the launch traced here: 119 us
  starting transfers between devices  51.5 us (43%)
  Pallas kernels  42.1 us (35%)
  waiting for transfers between devices  21.5 us (18%)
  local copies, waits for them, and re-layouts  2.76 us (2%)
    pallas_call x1, Pallas kernels, teacher_terms(): pl.pallas_call(teacher_body, out_shape=[jax.ShapeDtypeStruct((QPART, n *...  15.4 us
    all_to_all x1, starting transfers between devices, step(): lax.all_to_all(gk.reshape(128, 16, IDXD), ('seq', 'head'), split_axis=0,...  11.7 us
    all_to_all x1, waiting for transfers between devices, step(): kj = lax.all_to_all(packed, 'seq', split_axis=0, concat_axis=0, tiled=True)  10.1 us
    ppermute x7, starting transfers between devices, step(): lax.ppermute(dealt[k], 'head', [(h, h + k & 7) for h in range(8)])  9.78 us
    ppermute x7, starting transfers between devices, step(): lax.ppermute(gq[k], 'head', [(h, h - k & 7) for h in range(8)])  9.37 us
    all_to_all x1, starting transfers between devices, step(): lax.all_to_all(wanted, 'seq', split_axis=0, concat_axis=0, tiled=True)  8.6 us
    pallas_call x1, Pallas kernels, flip_queries(): pl.pallas_call(flip_body, out_shape=(oq, oq, ol, ol), grid_spec=pltpu.Pre...  6.77 us
    all_to_all x1, waiting for transfers between devices, step(): lax.all_to_all(wanted, 'seq', split_axis=0, concat_axis=0, tiled=True)  6.36 us
  transfers between devices with their start and end apart: 22, of which 5 were waited for; matrix products, arithmetic and copies ran while one was open for 0% of the time, Pallas kernels for 25%

profile of v6, /device:TPU:1, one launch (start us, length us, event | category | flops | bytes accessed | tf_op | source)
XLA Modules:
  0.0 119.2 jit_solution(9616747724511698811)
XLA Ops:
  0.6 1.4 %lookup.1 = s32[16,2]{1,0:T(8,128)} custom-call(s32[2,16]{1,0:T(2,128)} %lists_ref.1, s32[1024]{0:T(1024)} %place_ref.1), custom_call_target="tpu_custom_call" | custom-call | tf_op jit(solution)/shard_map/lookup/pallas_call | solution.py:50
  2.1 8.6 %all-to-all-start = ((s32[16,1,2]{2,1,0:T(1,128)}), s32[16,1,2]{2,1,0:T(1,128)S(1)}, u32[]{:S(2)}, u32[]{:S(2)}) async-start(s32[16,1,2]{2,1,0:T(1,128)} %bitcast.23), calls=%async_computation | async-start | bytes 16384 | tf_op jit(solution)/shard_map/all_to_all | solution.py:410
  10.7 6.4 %all-to-all-done = s32[16,1,2]{2,1,0:T(1,128)S(1)} async-done(((s32[16,1,2]{2,1,0:T(1,128)}), s32[16,1,2]{2,1,0:T(1,128)S(1)}, u32[]{:S(2)}, u32[]{:S(2)}) %all-to-all-start) | async-done | bytes 160 | tf_op jit(solution)/shard_map/all_to_all | solution.py:410
  17.0 0.6 copy-done.1
  17.6 3.8 %pack_pages.1 = bf16[16,704,128]{2,1,0:T(8,128)(2,1)} custom-call(s32[1]{0:T(128)} %bitcast.2.core_ref, s32[16,2]{1,0:T(8,128)} %bitcast.13, bf16[64,576,128]{2,1,0:T(8,128)(2,1)} %bitcast.19, bf16[64,128,128]{2,1,0:T(8,128)(2,1)} %key_ref.1), custom_call_target="tpu_custom_call" | custom-call | bytes 6291456 | tf_op jit(solution)/shard_map/pack_pages/pallas_call | solution.py:82
  21.4 3.7 %all-to-all-start.1 = ((bf16[16,704,128]{2,1,0:T(8,128)(2,1)}), bf16[16,704,128]{2,1,0:T(8,128)(2,1)S(1)}, u32[]{:S(2)}, u32[]{:S(2)}) async-start(bf16[16,704,128]{2,1,0:T(8,128)(2,1)} %pack_pages.1), calls=%async_computation.1 | async-start | bytes 5767168 | tf_op jit(solution)/shard_map/all_to_all | solution.py:413
  25.2 0.6 pad_add_fusion.place_ref
  25.8 6.8 %flip_queries.1 = (bf16[16,128,640]{2,1,0:T(8,128)(2,1)}, bf16[16,128,640]{2,1,0:T(8,128)(2,1)}, f32[128,128]{1,0:T(8,128)}, f32[128,128]{1,0:T(8,128)}) custom-call(s32[2]{0:T(128)} %pad_add_fusion.place_ref, bf16[16,576,256]{2,1,0:T(8,128)(2,1)} %bitcast.17, bf16[16,576,256]{2,1,0:T(8,128)(2,1)} %bitcast.18, f32[16,256]{1,0:T(8,128)} %bitcast.21, ...), custom_call_target="tpu_custom_call" | custom-call | bytes 25165824 | tf_op jit(solution)/shard_map/flip_queries/pallas_call | solution.py:129
  32.6 2.7 %collective-permute-start = (bf16[16,128,640]{2,1,0:T(8,128)(2,1)}, bf16[16,128,640]{2,1,0:T(8,128)(2,1)S(1)}, u32[]{:S(2)}, u32[]{:S(2)}) collective-permute-start(bf16[16,128,640]{2,1,0:T(8,128)(2,1)} %get-tuple-element.36), channel_id=1, source_target_pairs={{0,1},{1,0},{2,3},{3,2},{4,5},{5,4},{6,7},{7,6},{8,9},{9,8},{10,11... | collective-permute-start | bytes 7864328 | tf_op jit(solution)/shard_map/ppermute | solution.py:420
  35.3 1.2 deal.1
  36.5 1.1 collective-permute-start.5
  37.6 1.2 %collective-permute-start.6 = (bf16[288,128]{1,0:T(8,128)(2,1)}, bf16[288,128]{1,0:T(8,128)(2,1)S(1)}, u32[]{:S(2)}, u32[]{:S(2)}) collective-permute-start(bf16[288,128]{1,0:T(8,128)(2,1)} %get-tuple-element.45), channel_id=1, source_target_pairs={{0,2},{1,3},{2,4},{3,5},{4,6},{5,7},{6,0},{7,1},{8,10},{9,11},{10,... | collective-permute-start | bytes 221192 | tf_op jit(solution)/shard_map/ppermute | solution.py:416
  38.8 0.0 collective-permute-start.1
  38.8 2.0 %collective-permute-start.7 = (bf16[288,128]{1,0:T(8,128)(2,1)}, bf16[288,128]{1,0:T(8,128)(2,1)}, u32[]{:S(2)}, u32[]{:S(2)}) collective-permute-start(bf16[288,128]{1,0:T(8,128)(2,1)} %get-tuple-element.46), channel_id=1, source_target_pairs={{0,3},{1,4},{2,5},{3,6},{4,7},{5,0},{6,1},{7,2},{8,11},{9,12},{10,... | collective-permute-start | bytes 221192 | tf_op jit(solution)/shard_map/ppermute | solution.py:416
  40.8 0.0 collective-permute-done.1.lb_ref
  40.8 2.1 %collective-permute-start.8 = (bf16[288,128]{1,0:T(8,128)(2,1)}, bf16[288,128]{1,0:T(8,128)(2,1)}, u32[]{:S(2)}, u32[]{:S(2)}) collective-permute-start(bf16[288,128]{1,0:T(8,128)(2,1)} %get-tuple-element.47), channel_id=1, source_target_pairs={{0,4},{1,5},{2,6},{3,7},{4,0},{5,1},{6,2},{7,3},{8,12},{9,13},{10,... | collective-permute-start | bytes 221192 | tf_op jit(solution)/shard_map/ppermute | solution.py:416
  42.9 1.4 %collective-permute-start.9 = (bf16[288,128]{1,0:T(8,128)(2,1)}, bf16[288,128]{1,0:T(8,128)(2,1)}, u32[]{:S(2)}, u32[]{:S(2)}) collective-permute-start(bf16[288,128]{1,0:T(8,128)(2,1)} %get-tuple-element.48), channel_id=1, source_target_pairs={{0,5},{1,6},{2,7},{3,0},{4,1},{5,2},{6,3},{7,4},{8,13},{9,14},{10,... | collective-permute-start | bytes 221192 | tf_op jit(solution)/shard_map/ppermute | solution.py:416
  44.3 0.0 collective-permute-done.6.refs_2_
  44.3 0.6 copy-done.3
  44.9 0.0 collective-permute-start.10
  44.9 0.0 collective-permute-done.qb_ref
  44.9 1.5 %copy-done.7 = bf16[16,128,640]{2,1,0:T(8,128)(2,1)} copy-done((bf16[16,128,640]{2,1,0:T(8,128)(2,1)}, bf16[16,128,640]{2,1,0:T(8,128)(2,1)S(1)}, u32[]{:S(2)}) %copy-start.7) | copy-done | bytes 2621464
  46.5 2.0 %collective-permute-start.11 = (bf16[288,128]{1,0:T(8,128)(2,1)}, bf16[288,128]{1,0:T(8,128)(2,1)}, u32[]{:S(2)}, u32[]{:S(2)}) collective-permute-start(bf16[288,128]{1,0:T(8,128)(2,1)} %get-tuple-element.50), channel_id=1, source_target_pairs={{0,7},{1,0},{2,1},{3,2},{4,3},{5,4},{6,5},{7,6},{8,15},{9,8},{10,9... | collective-permute-start | bytes 221192 | tf_op jit(solution)/shard_map/ppermute | solution.py:416
  48.4 10.1 %all-to-all-done.1.kj_ref = bf16[16,704,128]{2,1,0:T(8,128)(2,1)S(1)} async-done(((bf16[16,704,128]{2,1,0:T(8,128)(2,1)}), bf16[16,704,128]{2,1,0:T(8,128)(2,1)S(1)}, u32[]{:S(2)}, u32[]{:S(2)}) %all-to-all-start.1) | async-done | bytes 2883616 | tf_op jit(solution)/shard_map/all_to_all | solution.py:413
  58.5 15.4 %teacher_terms.1 = (bf16[32,2048]{1,0:T(8,128)(2,1)S(1)}, bf16[32,2048]{1,0:T(8,128)(2,1)S(1)}, bf16[32,2048]{1,0:T(8,128)(2,1)S(1)}, f32[32,2048]{1,0:T(8,128)S(1)}) custom-call(bf16[16,128,640]{2,1,0:T(8,128)(2,1)} %get-tuple-element.35.qa_ref, bf16[16,128,640]{2,1,0:T(8,128)(2,1)} %copy-done.7, f32[128,128]{1,0:T(8,128)} %get-tuple-element.37.la_ref, ...), custom_call_target="tpu_custom_call" | custom-call | flops 9663676416 | bytes 12582912 | tf_op jit(solution)/shard_map/teacher_terms/pallas_call | solution.py:261
  73.9 0.0 collective-permute-done.7.refs_3_
  74.0 2.8 %collective-permute-start.2 = (bf16[32,2048]{1,0:T(8,128)(2,1)S(1)}, bf16[32,2048]{1,0:T(8,128)(2,1)S(1)}, u32[]{:S(2)}, u32[]{:S(2)}) collective-permute-start(bf16[32,2048]{1,0:T(8,128)(2,1)S(1)} %get-tuple-element.40), channel_id=1, source_target_pairs={{0,4},{1,5},{2,6},{3,7},{4,0},{5,1},{6,2},{7,3},{8,12},{9,13},{10,... | collective-permute-start | bytes 393224 | tf_op jit(solution)/shard_map/ppermute | solution.py:427
  76.8 0.3 collective-permute-start.3
  77.1 2.4 %collective-permute-start.4 = (bf16[32,2048]{1,0:T(8,128)(2,1)S(1)}, bf16[32,2048]{1,0:T(8,128)(2,1)S(1)}, u32[]{:S(2)}, u32[]{:S(2)}) collective-permute-start(bf16[32,2048]{1,0:T(8,128)(2,1)S(1)} %get-tuple-element.42), channel_id=1, source_target_pairs={{0,6},{1,7},{2,0},{3,1},{4,2},{5,3},{6,4},{7,5},{8,14},{9,15},{10,... | collective-permute-start | bytes 393224 | tf_op jit(solution)/shard_map/ppermute | solution.py:427
  79.5 2.3 %spread.1 = (bf16[2048,128]{1,0:T(8,128)(2,1)S(1)}, bf16[128,2048]{1,0:T(8,128)(2,1)S(1)}, f32[64,32,128]{2,1,0:T(8,128)S(1)}) custom-call(bf16[288,128]{1,0:T(8,128)(2,1)S(1)} %get-tuple-element.43.refs_0_, bf16[288,128]{1,0:T(8,128)(2,1)S(1)} %collective-permute-done.5.refs_1_, bf16[288,128]{1,0:T(8,128)(2,1)S(1)} %copy-done.4, ...), custom_call_target="tpu_custom_call" | custom-call | bytes 3145728 | tf_op jit(solution)/shard_map/spread/pallas_call | solution.py:293
  81.7 3.0 %scores.1 = (f32[32,2048]{1,0:T(8,128)S(1)}, bf16[16,2048,128]{2,1,0:T(8,128)(2,1)S(1)}) custom-call(bf16[2048,128]{1,0:T(8,128)(2,1)S(1)} %get-tuple-element.51.iq_ref, f32[64,32,128]{2,1,0:T(8,128)S(1)} %get-tuple-element.52.wb_ref, bf16[16,704,128]{2,1,0:T(8,128)(2,1)S(1)} %all-to-all-done.1.kj_ref), custom_call_target="tpu_custom_call" | custom-call | flops 1073741824 | bytes 12582912 | tf_op jit(solution)/shard_map/scores/pallas_call | solution.py:325
  84.7 0.0 collective-permute-done.3.t2_ref
  84.7 0.0 collective-permute-done.4.t3_ref
  84.8 0.0 copy-start.6
  84.8 5.3 %backward.1 = (bf16[2048,128]{1,0:T(8,128)(2,1)}, bf16[256,128]{1,0:T(8,128)(2,1)S(1)}, bf16[256,128]{1,0:T(8,128)(2,1)}, bf16[256,128]{1,0:T(8,128)(2,1)}, bf16...) custom-call(f32[32,2048]{1,0:T(8,128)S(1)} %get-tuple-element.39.own, ...), custom_call_target="tpu_custom_call" | custom-call | flops 2147483648 | bytes 16777216 | tf_op jit(solution)/shard_map/backward/pallas_call | solution.py:383
  90.1 11.7 %all-to-all-start.2 = ((bf16[128,16,128]{2,1,0:T(8,128)(2,1)}), bf16[128,16,128]{2,1,0:T(8,128)(2,1)S(1)}, u32[]{:S(2)}, u32[]{:S(2)}) async-start(bf16[128,16,128]{2,1,0:T(8,128)(2,1)} %bitcast.20), calls=%async_computation.2 | async-start | bytes 1048576 | tf_op jit(solution)/shard_map/all_to_all | solution.py:432
  101.8 1.1 collective-permute-start.12
  102.9 1.9 %collective-permute-start.13 = (bf16[256,128]{1,0:T(8,128)(2,1)}, bf16[256,128]{1,0:T(8,128)(2,1)S(1)}, u32[]{:S(2)}, u32[]{:S(2)}) collective-permute-start(bf16[256,128]{1,0:T(8,128)(2,1)} %get-tuple-element.58), channel_id=1, source_target_pairs={{0,6},{1,7},{2,0},{3,1},{4,2},{5,3},{6,4},{7,5},{8,14},{9,15},{10,... | collective-permute-start | bytes 196616 | tf_op jit(solution)/shard_map/ppermute | solution.py:433
  104.8 1.0 collective-permute-start.14
  105.8 2.4 %collective-permute-start.15 = (bf16[256,128]{1,0:T(8,128)(2,1)}, bf16[256,128]{1,0:T(8,128)(2,1)S(1)}, u32[]{:S(2)}, u32[]{:S(2)}) collective-permute-start(bf16[256,128]{1,0:T(8,128)(2,1)} %get-tuple-element.60), channel_id=1, source_target_pairs={{0,4},{1,5},{2,6},{3,7},{4,0},{5,1},{6,2},{7,3},{8,12},{9,13},{10,... | collective-permute-start | bytes 196616 | tf_op jit(solution)/shard_map/ppermute | solution.py:433
  108.2 0.7 collective-permute-start.16
  108.9 2.4 %collective-permute-done.12.refs_1_ = bf16[256,128]{1,0:T(8,128)(2,1)S(1)} collective-permute-done((bf16[256,128]{1,0:T(8,128)(2,1)}, bf16[256,128]{1,0:T(8,128)(2,1)S(1)}, u32[]{:S(2)}, u32[]{:S(2)}) %collective-permute-start.12) | collective-permute-done | bytes 65568 | tf_op jit(solution)/shard_map/ppermute | solution.py:433
  111.4 1.2 collective-permute-start.17
  112.6 1.1 collective-permute-start.18
  113.7 0.7 collective-permute-done.16.refs_5_
  114.4 1.8 %collective-permute-done.17.refs_6_ = bf16[256,128]{1,0:T(8,128)(2,1)S(1)} collective-permute-done((bf16[256,128]{1,0:T(8,128)(2,1)}, bf16[256,128]{1,0:T(8,128)(2,1)S(1)}, u32[]{:S(2)}, u32[]{:S(2)}) %collective-permute-start.17) | collective-permute-done | bytes 65568 | tf_op jit(solution)/shard_map/ppermute | solution.py:433
  116.2 1.3 %place.1 = (f32[256,8,128]{2,1,0:T(8,128)}, f32[8,256]{1,0:T(8,128)}) custom-call(s32[1]{0:T(128)} %bitcast.head_ref, bf16[256,8,128]{2,1,0:T(8,128)(2,1)S(1)} %copy-done, f32[8,256]{1,0:T(8,128)S(1)} %bitcast.16, bf16[256,128]{1,0:T(8,128)(2,1)S(1)} %get-tuple-element.56.refs_0_, bf16[256,128]{1,0:T(8,128)(2,1)S(1)} %collective-permute-done.12.refs_1_, ...), custom_call_target="tpu_custom_call" | custom-call | bytes 2097152 | tf_op jit(solution)/shard_map/place/pallas_call | solution.py:190
  117.5 1.6 %add_pages.1 = f32[64,16,128]{2,1,0:T(8,128)} custom-call(s32[16,2]{1,0:T(8,128)S(1)} %bitcast.14, bf16[128,16,128]{2,1,0:T(8,128)(2,1)S(1)} %all-to-all-done.2.gk_ref), custom_call_target="tpu_custom_call" | custom-call | bytes 1048576 | tf_op jit(solution)/shard_map/add_pages/pallas_call | solution.py:212
  (25 shorter events, 0.1 us)
Async XLA Ops:
  2.1 15.0 %all-to-all-start = ((s32[16,1,2]{2,1,0:T(1,128)}), s32[16,1,2]{2,1,0:T(1,128)S(1)}, u32[]{:S(2)}, u32[]{:S(2)}) async-start(s32[16,1,2]{2,1,0:T(1,128)} %bitcast.23), calls=%async_computation | async-start | bytes 16384 | tf_op jit(solution)/shard_map/all_to_all | solution.py:410
  17.0 0.6 copy-start.1
  21.4 37.1 %all-to-all-start.1 = ((bf16[16,704,128]{2,1,0:T(8,128)(2,1)}), bf16[16,704,128]{2,1,0:T(8,128)(2,1)S(1)}, u32[]{:S(2)}, u32[]{:S(2)}) async-start(bf16[16,704,128]{2,1,0:T(8,128)(2,1)} %pack_pages.1), calls=%async_computation.1 | async-start | bytes 5767168 | tf_op jit(solution)/shard_map/all_to_all | solution.py:413
  25.8 9.5 %copy-start = (bf16[256,8,128]{2,1,0:T(8,128)(2,1)S(1)}, bf16[256,8,128]{2,1,0:T(8,128)(2,1)}, u32[]{:S(2)}) copy-start(bf16[256,8,128]{2,1,0:T(8,128)(2,1)} %iq_ref.3) | copy-start | bytes 1572868
  25.8 9.5 %copy-start.5 = (f32[256,8]{0,1:T(8,128)S(1)}, f32[256,8]{0,1:T(8,128)}, u32[]{:S(2)}) copy-start(f32[256,8]{0,1:T(8,128)} %param.13) | copy-start | bytes 24580
  32.6 12.4 %collective-permute-start = (bf16[16,128,640]{2,1,0:T(8,128)(2,1)}, bf16[16,128,640]{2,1,0:T(8,128)(2,1)S(1)}, u32[]{:S(2)}, u32[]{:S(2)}) collective-permute-start(bf16[16,128,640]{2,1,0:T(8,128)(2,1)} %get-tuple-element.36), channel_id=1, source_target_pairs={{0,1},{1,0},{2,3},{3,2},{4,5},{5,4},{6,7},{7,6},{8,9},{9,8},{10,11... | collective-permute-start | bytes 7864328 | tf_op jit(solution)/shard_map/ppermute | solution.py:420
  36.5 6.4 %collective-permute-start.5 = (bf16[288,128]{1,0:T(8,128)(2,1)}, bf16[288,128]{1,0:T(8,128)(2,1)S(1)}, u32[]{:S(2)}, u32[]{:S(2)}) collective-permute-start(bf16[288,128]{1,0:T(8,128)(2,1)} %get-tuple-element.44), channel_id=1, source_target_pairs={{0,1},{1,2},{2,3},{3,4},{4,5},{5,6},{6,7},{7,0},{8,9},{9,10},{10,1... | collective-permute-start | bytes 221192 | tf_op jit(solution)/shard_map/ppermute | solution.py:416
  37.6 6.7 %collective-permute-start.6 = (bf16[288,128]{1,0:T(8,128)(2,1)}, bf16[288,128]{1,0:T(8,128)(2,1)S(1)}, u32[]{:S(2)}, u32[]{:S(2)}) collective-permute-start(bf16[288,128]{1,0:T(8,128)(2,1)} %get-tuple-element.45), channel_id=1, source_target_pairs={{0,2},{1,3},{2,4},{3,5},{4,6},{5,7},{6,0},{7,1},{8,10},{9,11},{10,... | collective-permute-start | bytes 221192 | tf_op jit(solution)/shard_map/ppermute | solution.py:416
  38.8 2.0 %collective-permute-start.1 = (f32[128,128]{1,0:T(8,128)}, f32[128,128]{1,0:T(8,128)S(1)}, u32[]{:S(2)}, u32[]{:S(2)}) collective-permute-start(f32[128,128]{1,0:T(8,128)} %get-tuple-element.38), channel_id=1, source_target_pairs={{0,1},{1,0},{2,3},{3,2},{4,5},{5,4},{6,7},{7,6},{8,9},{9,8},{10,11... | collective-permute-start | bytes 196616 | tf_op jit(solution)/shard_map/ppermute | solution.py:421
  38.8 35.1 %collective-permute-start.7 = (bf16[288,128]{1,0:T(8,128)(2,1)}, bf16[288,128]{1,0:T(8,128)(2,1)}, u32[]{:S(2)}, u32[]{:S(2)}) collective-permute-start(bf16[288,128]{1,0:T(8,128)(2,1)} %get-tuple-element.46), channel_id=1, source_target_pairs={{0,3},{1,4},{2,5},{3,6},{4,7},{5,0},{6,1},{7,2},{8,11},{9,12},{10,... | collective-permute-start | bytes 221192 | tf_op jit(solution)/shard_map/ppermute | solution.py:416
  40.8 4.1 %copy-start.8 = (f32[128,128]{1,0:T(8,128)}, f32[128,128]{1,0:T(8,128)S(1)}, u32[]{:S(2)}) copy-start(f32[128,128]{1,0:T(8,128)S(1)} %collective-permute-done.1.lb_ref) | copy-start | bytes 196612
  40.8 36.0 %collective-permute-start.8 = (bf16[288,128]{1,0:T(8,128)(2,1)}, bf16[288,128]{1,0:T(8,128)(2,1)}, u32[]{:S(2)}, u32[]{:S(2)}) collective-permute-start(bf16[288,128]{1,0:T(8,128)(2,1)} %get-tuple-element.47), channel_id=1, source_target_pairs={{0,4},{1,5},{2,6},{3,7},{4,0},{5,1},{6,2},{7,3},{8,12},{9,13},{10,... | collective-permute-start | bytes 221192 | tf_op jit(solution)/shard_map/ppermute | solution.py:416
  42.9 34.2 %collective-permute-start.9 = (bf16[288,128]{1,0:T(8,128)(2,1)}, bf16[288,128]{1,0:T(8,128)(2,1)}, u32[]{:S(2)}, u32[]{:S(2)}) collective-permute-start(bf16[288,128]{1,0:T(8,128)(2,1)} %get-tuple-element.48), channel_id=1, source_target_pairs={{0,5},{1,6},{2,7},{3,0},{4,1},{5,2},{6,3},{7,4},{8,13},{9,14},{10,... | collective-permute-start | bytes 221192 | tf_op jit(solution)/shard_map/ppermute | solution.py:416
  44.3 0.6 copy-start.3
  44.9 34.5 %collective-permute-start.10 = (bf16[288,128]{1,0:T(8,128)(2,1)}, bf16[288,128]{1,0:T(8,128)(2,1)}, u32[]{:S(2)}, u32[]{:S(2)}) collective-permute-start(bf16[288,128]{1,0:T(8,128)(2,1)} %get-tuple-element.49), channel_id=1, source_target_pairs={{0,6},{1,7},{2,0},{3,1},{4,2},{5,3},{6,4},{7,5},{8,14},{9,15},{10,... | collective-permute-start | bytes 221192 | tf_op jit(solution)/shard_map/ppermute | solution.py:416
  44.9 1.5 %copy-start.7 = (bf16[16,128,640]{2,1,0:T(8,128)(2,1)}, bf16[16,128,640]{2,1,0:T(8,128)(2,1)S(1)}, u32[]{:S(2)}) copy-start(bf16[16,128,640]{2,1,0:T(8,128)(2,1)S(1)} %collective-permute-done.qb_ref) | copy-start | bytes 7864324
  46.5 33.0 %collective-permute-start.11 = (bf16[288,128]{1,0:T(8,128)(2,1)}, bf16[288,128]{1,0:T(8,128)(2,1)}, u32[]{:S(2)}, u32[]{:S(2)}) collective-permute-start(bf16[288,128]{1,0:T(8,128)(2,1)} %get-tuple-element.50), channel_id=1, source_target_pairs={{0,7},{1,0},{2,1},{3,2},{4,3},{5,4},{6,5},{7,6},{8,15},{9,8},{10,9... | collective-permute-start | bytes 221192 | tf_op jit(solution)/shard_map/ppermute | solution.py:416
  58.5 21.0 %copy-start.4 = (bf16[288,128]{1,0:T(8,128)(2,1)S(1)}, bf16[288,128]{1,0:T(8,128)(2,1)}, u32[]{:S(2)}) copy-start(bf16[288,128]{1,0:T(8,128)(2,1)} %copy-done.3) | copy-start | bytes 221188
  74.0 10.8 %collective-permute-start.2 = (bf16[32,2048]{1,0:T(8,128)(2,1)S(1)}, bf16[32,2048]{1,0:T(8,128)(2,1)S(1)}, u32[]{:S(2)}, u32[]{:S(2)}) collective-permute-start(bf16[32,2048]{1,0:T(8,128)(2,1)S(1)} %get-tuple-element.40), channel_id=1, source_target_pairs={{0,4},{1,5},{2,6},{3,7},{4,0},{5,1},{6,2},{7,3},{8,12},{9,13},{10,... | collective-permute-start | bytes 393224 | tf_op jit(solution)/shard_map/ppermute | solution.py:427
  76.8 8.0 %collective-permute-start.3 = (bf16[32,2048]{1,0:T(8,128)(2,1)S(1)}, bf16[32,2048]{1,0:T(8,128)(2,1)S(1)}, u32[]{:S(2)}, u32[]{:S(2)}) collective-permute-start(bf16[32,2048]{1,0:T(8,128)(2,1)S(1)} %get-tuple-element.41), channel_id=1, source_target_pairs={{0,2},{1,3},{2,4},{3,5},{4,6},{5,7},{6,0},{7,1},{8,10},{9,11},{10,... | collective-permute-start | bytes 393224 | tf_op jit(solution)/shard_map/ppermute | solution.py:427
  77.1 7.7 %collective-permute-start.4 = (bf16[32,2048]{1,0:T(8,128)(2,1)S(1)}, bf16[32,2048]{1,0:T(8,128)(2,1)S(1)}, u32[]{:S(2)}, u32[]{:S(2)}) collective-permute-start(bf16[32,2048]{1,0:T(8,128)(2,1)S(1)} %get-tuple-element.42), channel_id=1, source_target_pairs={{0,6},{1,7},{2,0},{3,1},{4,2},{5,3},{6,4},{7,5},{8,14},{9,15},{10,... | collective-permute-start | bytes 393224 | tf_op jit(solution)/shard_map/ppermute | solution.py:427
  84.8 31.4 %copy-start.6 = (f32[256,8]{0,1:T(8,128)S(1)}, f32[256,8]{0,1:T(8,128)}, u32[]{:S(2)}) copy-start(f32[256,8]{0,1:T(8,128)} %param.13) | copy-start | bytes 24580
  84.8 32.7 %copy-start.2 = (s32[16,1,2]{2,1,0:T(1,128)S(1)}, s32[16,1,2]{2,1,0:T(1,128)}, u32[]{:S(2)}) copy-start(s32[16,1,2]{2,1,0:T(1,128)} %copy-done.1) | copy-start | bytes 388
  90.1 27.4 %all-to-all-start.2 = ((bf16[128,16,128]{2,1,0:T(8,128)(2,1)}), bf16[128,16,128]{2,1,0:T(8,128)(2,1)S(1)}, u32[]{:S(2)}, u32[]{:S(2)}) async-start(bf16[128,16,128]{2,1,0:T(8,128)(2,1)} %bitcast.20), calls=%async_computation.2 | async-start | bytes 1048576 | tf_op jit(solution)/shard_map/all_to_all | solution.py:432
  101.8 9.5 %collective-permute-start.12 = (bf16[256,128]{1,0:T(8,128)(2,1)}, bf16[256,128]{1,0:T(8,128)(2,1)S(1)}, u32[]{:S(2)}, u32[]{:S(2)}) collective-permute-start(bf16[256,128]{1,0:T(8,128)(2,1)} %get-tuple-element.57), channel_id=1, source_target_pairs={{0,7},{1,0},{2,1},{3,2},{4,3},{5,4},{6,5},{7,6},{8,15},{9,8},{10,9... | collective-permute-start | bytes 196616 | tf_op jit(solution)/shard_map/ppermute | solution.py:433
  102.9 9.6 %collective-permute-start.13 = (bf16[256,128]{1,0:T(8,128)(2,1)}, bf16[256,128]{1,0:T(8,128)(2,1)S(1)}, u32[]{:S(2)}, u32[]{:S(2)}) collective-permute-start(bf16[256,128]{1,0:T(8,128)(2,1)} %get-tuple-element.58), channel_id=1, source_target_pairs={{0,6},{1,7},{2,0},{3,1},{4,2},{5,3},{6,4},{7,5},{8,14},{9,15},{10,... | collective-permute-start | bytes 196616 | tf_op jit(solution)/shard_map/ppermute | solution.py:433
  104.8 8.9 %collective-permute-start.14 = (bf16[256,128]{1,0:T(8,128)(2,1)}, bf16[256,128]{1,0:T(8,128)(2,1)S(1)}, u32[]{:S(2)}, u32[]{:S(2)}) collective-permute-start(bf16[256,128]{1,0:T(8,128)(2,1)} %get-tuple-element.59), channel_id=1, source_target_pairs={{0,5},{1,6},{2,7},{3,0},{4,1},{5,2},{6,3},{7,4},{8,13},{9,14},{10,... | collective-permute-start | bytes 196616 | tf_op jit(solution)/shard_map/ppermute | solution.py:433
  105.8 7.8 %collective-permute-start.15 = (bf16[256,128]{1,0:T(8,128)(2,1)}, bf16[256,128]{1,0:T(8,128)(2,1)S(1)}, u32[]{:S(2)}, u32[]{:S(2)}) collective-permute-start(bf16[256,128]{1,0:T(8,128)(2,1)} %get-tuple-element.60), channel_id=1, source_target_pairs={{0,4},{1,5},{2,6},{3,7},{4,0},{5,1},{6,2},{7,3},{8,12},{9,13},{10,... | collective-permute-start | bytes 196616 | tf_op jit(solution)/shard_map/ppermute | solution.py:433
  108.2 6.2 %collective-permute-start.16 = (bf16[256,128]{1,0:T(8,128)(2,1)}, bf16[256,128]{1,0:T(8,128)(2,1)S(1)}, u32[]{:S(2)}, u32[]{:S(2)}) collective-permute-start(bf16[256,128]{1,0:T(8,128)(2,1)} %get-tuple-element.61), channel_id=1, source_target_pairs={{0,3},{1,4},{2,5},{3,6},{4,7},{5,0},{6,1},{7,2},{8,11},{9,12},{10,... | collective-permute-start | bytes 196616 | tf_op jit(solution)/shard_map/ppermute | solution.py:433
  111.4 4.8 %collective-permute-start.17 = (bf16[256,128]{1,0:T(8,128)(2,1)}, bf16[256,128]{1,0:T(8,128)(2,1)S(1)}, u32[]{:S(2)}, u32[]{:S(2)}) collective-permute-start(bf16[256,128]{1,0:T(8,128)(2,1)} %get-tuple-element.62), channel_id=1, source_target_pairs={{0,2},{1,3},{2,4},{3,5},{4,6},{5,7},{6,0},{7,1},{8,10},{9,11},{10,... | collective-permute-start | bytes 196616 | tf_op jit(solution)/shard_map/ppermute | solution.py:433
  112.6 3.6 %collective-permute-start.18 = (bf16[256,128]{1,0:T(8,128)(2,1)}, bf16[256,128]{1,0:T(8,128)(2,1)S(1)}, u32[]{:S(2)}, u32[]{:S(2)}) collective-permute-start(bf16[256,128]{1,0:T(8,128)(2,1)} %get-tuple-element.63), channel_id=1, source_target_pairs={{0,1},{1,2},{2,3},{3,4},{4,5},{5,6},{6,7},{7,0},{8,9},{9,10},{10,1... | collective-permute-start | bytes 196616 | tf_op jit(solution)/shard_map/ppermute | solution.py:433
